TPU v7x, 32 devices: a whole 2x2x4 slice. The times are simulated.
32 devices in a mesh: dp: 8 (over z, x), seq: 4 (over y, core).
Axes of the slice: x: 2, y: 2, z: 4, core: 2. Of those that a mesh axis runs over, the one named last changes fastest.
Arguments:
- tokens: bfloat16 [8, 1024, 1600], P('dp', 'seq'), may hold values from -6 to 6
- cotangent: bfloat16 [8, 1024, 1600], P('dp', 'seq'), may hold values from -6 to 6
- lengths: int32 [8], P('dp'), may hold values from 256 to 1024, as said below
- w_qkv: bfloat16 [7680000], P(('dp', 'seq')), may hold values from -0.15625 to 0.15625
- w_out: bfloat16 [2560000], P(('dp', 'seq')), may hold values from -2.5 to 2.5
- w_fc: bfloat16 [10246400], P(('dp', 'seq')), may hold values from -0.15625 to 0.15625
- w_proj: bfloat16 [10240000], P(('dp', 'seq')), may hold values from -0.078125 to 0.078125
- attention_vectors: bfloat16 [6400], P(('dp', 'seq')), as said below
- block_vectors: bfloat16 [6400], P(('dp', 'seq')), as said below
Outputs:
- output: bfloat16 [8, 1024, 1600], P('dp', 'seq')
- input_grad: float32 [8, 1024, 1600], P('dp', 'seq')
- grad_qkv: float32 [7680000], P(('dp', 'seq'))
- grad_out: float32 [2560000], P(('dp', 'seq'))
- grad_fc: float32 [10246400], P(('dp', 'seq'))
- grad_proj: float32 [10240000], P(('dp', 'seq'))
- grad_attention_vectors: float32 [6400], P(('dp', 'seq'))
- grad_block_vectors: float32 [6400], P(('dp', 'seq'))
Inputs may be any that keep to these rules, and one draw needn't show every extreme that they name: `lengths`: valid positions of each slot; in every draw one slot has all 1024 and one has 256. `attention_vectors`: gains near one, biases of order one half. `block_vectors`: gains near one, biases of order one half.
All inputs are finite; a program needn't handle non-finite values.
Results may differ from a plain program's by a relative error of at most 0.01.
Values may be sent and summed in bfloat16 or wider, within the bound.
No kernel may reach another device: no remote copies, remote signals or barrier semaphores. Data moves between devices by JAX's collectives and lax.ppermute only.
A program may use at most 448 MiB of HBM per device.

v0:
```python
from functools import partial

import jax
import jax.numpy as jnp
from jax import lax
from jax.sharding import PartitionSpec as P

HD = 64


EPS = 1e-05


def layer_norm(value, gain, shift):
    centre = value - jnp.mean(value, axis=-1, keepdims=True)
    spread = jnp.mean(centre * centre, axis=-1, keepdims=True)
    return centre * lax.rsqrt(spread + EPS) * gain + shift


def tanh_gelu(value):
    return jax.nn.gelu(value, approximate=True)


def split_weights(gathered, width):
    flat_qkv, flat_out, flat_fc, flat_proj, first_vectors, second_vectors = gathered
    hidden = flat_fc.shape[0] // (width + 1)
    expand_full = flat_fc.reshape(width + 1, hidden)
    token_rows = (
        jnp.concatenate([first_vectors, second_vectors]).astype(jnp.float32).reshape(8, width)
    )
    expand_bias = expand_full[width].astype(jnp.float32)
    return (
        flat_qkv.reshape(width, 3 * width),
        flat_out.reshape(width, width),
        expand_full[:width],
        flat_proj.reshape(hidden, width),
        token_rows,
        expand_bias,
    )


def to_heads(value, heads):
    slots, count, width = value.shape
    return jnp.moveaxis(value.reshape(slots, count, heads, width // heads), 2, 0)


def from_heads(value):
    heads, slots, count, size = value.shape
    return jnp.moveaxis(value, 0, 2).reshape(slots, count, heads * size)


def head_scores(allowed, query, keys):
    scores = jnp.einsum("sqd,skd->sqk", query, keys, preferred_element_type=jnp.float32) * 0.125
    return jnp.where(allowed, scores, -1e30)


def head_forward(allowed, item):
    query, keys, values = item
    scores = head_scores(allowed, query, keys)
    peak = jnp.max(scores, axis=-1, keepdims=True)
    raised = jnp.exp(scores - peak)
    total = jnp.sum(raised, axis=-1, keepdims=True)
    weights = (raised / total).astype(jnp.bfloat16)
    result = jnp.einsum("sqk,skd->sqd", weights, values, preferred_element_type=jnp.float32)
    return (result, (peak + jnp.log(total))[..., 0])


def head_backward(allowed, item):
    query, keys, values, grad_result, normal = item
    scores = head_scores(allowed, query, keys)
    probs = jnp.where(allowed, jnp.exp(scores - normal[..., None]), 0.0)
    weights = probs.astype(jnp.bfloat16)
    grad_probs = jnp.einsum("sqd,skd->sqk", grad_result, values, preferred_element_type=jnp.float32)
    inner_total = jnp.sum(probs * grad_probs, axis=-1, keepdims=True)
    grad_scores = (probs * (grad_probs - inner_total) * 0.125).astype(jnp.bfloat16)
    grad_query = jnp.einsum("sqk,skd->sqd", grad_scores, keys, preferred_element_type=jnp.float32)
    grad_keys = jnp.einsum("sqk,sqd->skd", grad_scores, query, preferred_element_type=jnp.float32)
    grad_values = jnp.einsum(
        "sqk,sqd->skd", weights, grad_result, preferred_element_type=jnp.float32
    )
    return (grad_query, grad_keys, grad_values)


def local(tokens, cotangent, lengths, w_qkv, w_out, w_fc, w_proj, attention_vectors, block_vectors):
    slots, count, width = tokens.shape
    heads = width // HD
    rank = lax.axis_index("seq")
    span = count * lax.axis_size("seq")
    part_qkv, part_out, part_fc, part_proj, part_first, part_second = (
        lax.all_gather(w_qkv, "seq", axis=0, tiled=True),
        lax.all_gather(w_out, "seq", axis=0, tiled=True),
        lax.all_gather(w_fc, "seq", axis=0, tiled=True),
        lax.all_gather(w_proj, "seq", axis=0, tiled=True),
        lax.all_gather(attention_vectors, "seq", axis=0, tiled=True),
        lax.all_gather(block_vectors, "seq", axis=0, tiled=True),
    )
    gathered = (
        lax.all_gather(part_qkv, "dp", axis=0, tiled=True),
        lax.all_gather(part_out, "dp", axis=0, tiled=True),
        lax.all_gather(part_fc, "dp", axis=0, tiled=True),
        lax.all_gather(part_proj, "dp", axis=0, tiled=True),
        lax.all_gather(part_first, "dp", axis=0, tiled=True),
        lax.all_gather(part_second, "dp", axis=0, tiled=True),
    )
    (
        query_key_value_weight,
        output_weight,
        expand_weight,
        contract_weight,
        token_rows,
        expand_bias,
    ) = split_weights(gathered, width)
    place = rank * count + jnp.arange(count)
    key_place = jnp.arange(span)
    allowed = (key_place[None, None, :] <= place[None, :, None]) & (
        key_place[None, None, :] < lengths[:, None, None]
    )
    valid = place[None, :] < lengths[:, None]
    source = tokens.astype(jnp.float32)
    normed_low = layer_norm(source, token_rows[0], token_rows[1]).astype(jnp.bfloat16)
    mixed_heads = jnp.einsum(
        "scd,de->sce", normed_low, query_key_value_weight, preferred_element_type=jnp.float32
    )
    query = (mixed_heads[..., :width] + token_rows[2]).astype(jnp.bfloat16)
    keys = mixed_heads[..., width : 2 * width].astype(jnp.bfloat16)
    values = (mixed_heads[..., 2 * width :] + token_rows[3]).astype(jnp.bfloat16)
    all_keys, all_values = (
        lax.all_gather(keys, "seq", axis=1, tiled=True),
        lax.all_gather(values, "seq", axis=1, tiled=True),
    )
    query_heads = to_heads(query, heads)
    key_heads = to_heads(all_keys, heads)
    value_heads = to_heads(all_values, heads)
    head_result, normal = lax.map(
        partial(head_forward, allowed), (query_heads, key_heads, value_heads)
    )
    attention_output = from_heads(head_result).astype(jnp.bfloat16)
    middle_state = (
        source
        + jnp.einsum(
            "scd,de->sce", attention_output, output_weight, preferred_element_type=jnp.float32
        )
        + token_rows[4]
    )
    second_normed = layer_norm(middle_state, token_rows[5], token_rows[6]).astype(jnp.bfloat16)
    inner_hidden = (
        jnp.einsum("scd,df->scf", second_normed, expand_weight, preferred_element_type=jnp.float32)
        + expand_bias
    )
    active_low = tanh_gelu(inner_hidden).astype(jnp.bfloat16)
    result = (
        middle_state
        + jnp.einsum("scf,fd->scd", active_low, contract_weight, preferred_element_type=jnp.float32)
        + token_rows[7]
    )
    output = result.astype(jnp.bfloat16)
    again_qkv, again_out, again_fc, again_proj, again_first, again_second = (
        lax.all_gather(w_qkv, "seq", axis=0, tiled=True),
        lax.all_gather(w_out, "seq", axis=0, tiled=True),
        lax.all_gather(w_fc, "seq", axis=0, tiled=True),
        lax.all_gather(w_proj, "seq", axis=0, tiled=True),
        lax.all_gather(attention_vectors, "seq", axis=0, tiled=True),
        lax.all_gather(block_vectors, "seq", axis=0, tiled=True),
    )
    again = (
        lax.all_gather(again_qkv, "dp", axis=0, tiled=True),
        lax.all_gather(again_out, "dp", axis=0, tiled=True),
        lax.all_gather(again_fc, "dp", axis=0, tiled=True),
        lax.all_gather(again_proj, "dp", axis=0, tiled=True),
        lax.all_gather(again_first, "dp", axis=0, tiled=True),
        lax.all_gather(again_second, "dp", axis=0, tiled=True),
    )
    (
        query_key_value_weight,
        output_weight,
        expand_weight,
        contract_weight,
        token_rows,
        expand_bias,
    ) = split_weights(again, width)
    grad_result = cotangent * valid.astype(jnp.bfloat16)[..., None]
    grad_wide = grad_result.astype(jnp.float32)
    grad_proj = jnp.einsum(
        "scf,scd->fd", active_low, grad_result, preferred_element_type=jnp.float32
    )
    bias_proj_grad = jnp.sum(grad_wide, axis=(0, 1))
    grad_active = jnp.einsum(
        "scd,fd->scf", grad_result, contract_weight, preferred_element_type=jnp.float32
    )
    gelu_back = jax.vjp(tanh_gelu, inner_hidden)[1]
    inner_low = gelu_back(grad_active)[0].astype(jnp.bfloat16)
    bias_fc_grad = jnp.sum(inner_low.astype(jnp.float32), axis=(0, 1))
    grad_fc = jnp.einsum(
        "scd,scf->df", second_normed, inner_low, preferred_element_type=jnp.float32
    )
    grad_fc_full = jnp.concatenate([grad_fc, bias_fc_grad[None, :]], axis=0).reshape(-1)
    grad_normed_two = jnp.einsum(
        "scf,df->scd", inner_low, expand_weight, preferred_element_type=jnp.float32
    )
    norm_two_back = jax.vjp(layer_norm, middle_state, token_rows[5], token_rows[6])[1]
    grad_mid, gain_two_grad, shift_two_grad = norm_two_back(grad_normed_two)
    grad_mid = grad_mid + grad_wide
    branch_low = grad_mid.astype(jnp.bfloat16)
    bias_out_grad = jnp.sum(branch_low.astype(jnp.float32), axis=(0, 1))
    grad_out_mat = jnp.einsum(
        "scd,sce->de", attention_output, branch_low, preferred_element_type=jnp.float32
    )
    grad_attended = jnp.einsum(
        "sce,de->scd", branch_low, output_weight, preferred_element_type=jnp.float32
    ).astype(jnp.bfloat16)
    grad_query, grad_keys, grad_values = lax.map(
        partial(head_backward, allowed),
        (query_heads, key_heads, value_heads, to_heads(grad_attended, heads), normal),
    )
    keys_sum, values_sum = (
        lax.psum_scatter(from_heads(grad_keys), "seq", scatter_dimension=1, tiled=True),
        lax.psum_scatter(from_heads(grad_values), "seq", scatter_dimension=1, tiled=True),
    )
    query_low = from_heads(grad_query).astype(jnp.bfloat16)
    keys_low = keys_sum.astype(jnp.bfloat16)
    values_low = values_sum.astype(jnp.bfloat16)
    bias_query_grad = jnp.sum(query_low.astype(jnp.float32), axis=(0, 1))
    bias_value_grad = jnp.sum(values_low.astype(jnp.float32), axis=(0, 1))
    grad_mixed = jnp.concatenate([query_low, keys_low, values_low], axis=-1)
    grad_qkv = jnp.einsum("scd,sce->de", normed_low, grad_mixed, preferred_element_type=jnp.float32)
    grad_normed = jnp.einsum(
        "sce,de->scd", grad_mixed, query_key_value_weight, preferred_element_type=jnp.float32
    )
    norm_one_back = jax.vjp(layer_norm, source, token_rows[0], token_rows[1])[1]
    grad_source, gain_one_grad, shift_one_grad = norm_one_back(grad_normed)
    input_grad = grad_mid + grad_source
    first_grad = jnp.concatenate([gain_one_grad, shift_one_grad, bias_query_grad, bias_value_grad])
    second_grad = jnp.concatenate([bias_out_grad, gain_two_grad, shift_two_grad, bias_proj_grad])
    qkv_part, out_part, fc_part, proj_part, first_part, second_part = (
        lax.psum_scatter(grad_qkv.reshape(-1), "dp", scatter_dimension=0, tiled=True),
        lax.psum_scatter(grad_out_mat.reshape(-1), "dp", scatter_dimension=0, tiled=True),
        lax.psum_scatter(grad_fc_full, "dp", scatter_dimension=0, tiled=True),
        lax.psum_scatter(grad_proj.reshape(-1), "dp", scatter_dimension=0, tiled=True),
        lax.psum_scatter(first_grad, "dp", scatter_dimension=0, tiled=True),
        lax.psum_scatter(second_grad, "dp", scatter_dimension=0, tiled=True),
    )
    qkv_shard, out_shard, fc_shard, proj_shard, first_shard, second_shard = (
        lax.psum_scatter(qkv_part, "seq", scatter_dimension=0, tiled=True),
        lax.psum_scatter(out_part, "seq", scatter_dimension=0, tiled=True),
        lax.psum_scatter(fc_part, "seq", scatter_dimension=0, tiled=True),
        lax.psum_scatter(proj_part, "seq", scatter_dimension=0, tiled=True),
        lax.psum_scatter(first_part, "seq", scatter_dimension=0, tiled=True),
        lax.psum_scatter(second_part, "seq", scatter_dimension=0, tiled=True),
    )
    return (
        output,
        input_grad,
        qkv_shard,
        out_shard,
        fc_shard,
        proj_shard,
        first_shard,
        second_shard,
    )


def solution(mesh):
    in_specs = (
        P("dp", "seq", None),
        P("dp", "seq", None),
        P("dp"),
        P(("dp", "seq")),
        P(("dp", "seq")),
        P(("dp", "seq")),
        P(("dp", "seq")),
        P(("dp", "seq")),
        P(("dp", "seq")),
    )
    out_specs = (
        P("dp", "seq", None),
        P("dp", "seq", None),
        P(("dp", "seq")),
        P(("dp", "seq")),
        P(("dp", "seq")),
        P(("dp", "seq")),
        P(("dp", "seq")),
        P(("dp", "seq")),
    )
    return jax.shard_map(local, mesh=mesh, in_specs=in_specs, out_specs=out_specs, check_vma=False)
```

profile of v0, /device:TPU:0, one launch (start us, length us, event | category | flops | bytes accessed | tf_op | source)
XLA Modules:
  0.0 6387.4 jit_solution(10073918586808207974)
XLA Ops:
  23.4 25.4 all-gather.19.cloned.1.call-done
  57.3 19.0 all-gather.2
  77.1 40.4 all-reduce.29.cloned.1.call-done
  124.8 39.2 dynamic-update-slice.5
  172.5 51.9 all-reduce.22
  226.2 478.7 %all-gather.21.cloned.1.call-done = bf16[8,1,960000]{2,1,0:T(2,128)(2,1)} async-done(((bf16[1,1,960000]{2,1,0:T(2,128)(2,1)}), bf16[8,1,960000]{2,1,0:T(2,128)(2,1)}) %all-gather.21.cloned.1.call-update) | async-done | bytes 15360016 | tf_op jit(solution)/shard_map/all_gather | solution.py:98
  704.9 325.4 %reduce.24 = bf16[8,960000]{1,0:T(8,128)(2,1)} reduce(bf16[8,1,960000]{2,1,0:T(2,128)(2,1)} %all-gather.21.cloned.1.call-done, bf16[]{:T(256)} %constant.172), dimensions={1}, to_apply=%all-gather.1.reduce_sub_computation | reduce | bytes 30720002 | tf_op jit(solution)/shard_map/all_gather | solution.py:98
  1030.3 34.2 reshape.626
  1064.5 25.2 reshape.541
  1089.7 14.8 convolution_bitcast_fusion.4
  1110.4 17.7 reduce.26
  1133.1 32.0 reduce.25
  1187.1 325.9 %all-reduce.31.cloned.1.call-done = bf16[10246400]{0:T(1024)(128)(2,1)} async-done(((bf16[10246400]{0:T(1024)(128)(2,1)}), bf16[10246400]{0:T(1024)(128)(2,1)}) %all-reduce.31.cloned.1.call-update) | async-done | bytes 20492816
  1513.1 16.9 slice.87
  1530.0 35.4 slice.74
  1583.3 79.7 %while.28 = (s32[]{:T(128)}, bf16[25,1,256,64]{2,3,1,0:T(8,128)(2,1)S(1)}, f32[25,1,256]{2,1,0:T(1,128)S(1)}, bf16[25,1,256,64]{3,2,1,0:T(8,128)(2,1)}, bf16[25,...) while((s32[]{:T(128)}, ...), condition=%wide.region_5.6_spmd.clone, body=%wide.region_2.5_spmd.clone.sunk | while | flops 69730048 | bytes 3815529 | solution.py:134
  1681.0 289.2 %all-gather.17.cloned.1.call-done = bf16[10240000]{0:T(1024)(128)(2,1)} async-done(((bf16[1280000]{0:T(1024)(128)(2,1)}), bf16[10240000]{0:T(1024)(128)(2,1)}) %all-gather.17.cloned.1.call-update) | async-done | bytes 20480016 | tf_op jit(solution)/shard_map/all_gather | solution.py:101
  1970.3 34.0 reshape.547
  2004.2 14.1 convert_reduce_fusion
  2039.8 200.8 %while.29 = (s32[]{:T(128)}, bf16[25,1,256,64]{2,3,1,0:T(8,128)(2,1)S(1)}, f32[25,1,1024,64]{2,3,1,0:T(8,128)}, f32[25,1,1024,64]{2,3,1,0:T(8,128)}, bf16[25,1,2...) while((s32[]{:T(128)}, ...), condition=%wide.region_12.13_spmd.clone, body=%wide.region_10.12_spmd.clone.sunk | while | flops 171179776 | bytes 9515137 | solution.py:211
  2241.4 22.7 fusion.84
  2264.1 48.3 reshape.557
  2319.4 13.5 reshape.555
  2332.8 18.4 fusion.101
  2351.2 28.1 pad_maximum_fusion
  2379.3 39.9 reshape.556
  2424.4 13.8 fusion.77
  2438.2 36.5 reshape.554
  2477.1 3609.6 %all-reduce.33.cloned.1.call-done = (f32[7680000]{0:T(1024)}, f32[2560000]{0:T(1024)}, f32[10246400]{0:T(1024)}, f32[10240000]{0:T(1024)}) async-done(((f32[7680000]{0:T(1024)}, f32[2560000]{0:T(1024)}, f32[10246400]{0:T(1024)}, f32[10240000]{0:T(1024)}), (f32[7680000]{0:T(1024)}, f32[2560000]{0:T(1024)}, f32[10246400]{0:T(1024)}, f32[10240000]{0:T(1024)})) %all-reduce.33.cloned.1.call-update) | async-done | bytes 122905616
  6110.5 17.3 fusion.60
  6137.3 35.6 all-reduce.18
  6184.1 186.5 %all-reduce.35.cloned.1.call-done = (f32[960000]{0:T(1024)}, f32[320000]{0:T(1024)}, f32[1280800]{0:T(1024)}, f32[1280000]{0:T(1024)}) async-done(((f32[960000]{0:T(1024)}, f32[320000]{0:T(1024)}, f32[1280800]{0:T(1024)}, f32[1280000]{0:T(1024)}), (f32[960000]{0:T(1024)}, f32[320000]{0:T(1024)}, f32[1280800]{0:T(1024)}, f32[1280000]{0:T(1024)})) %all-reduce.35.cloned.1.call-update) | async-done | bytes 15363216
  (481 shorter events, 471.9 us)
Async XLA Ops:
  7.2 8.7 copy-start.12
  7.2 41.7 all-gather.19.cloned.1.call-start
  13.5 103.9 %all-reduce.29.cloned.1.call-start = ((), (), s32[]{:S(2)}) async-start(), calls=%async_computation.7 | async-start | bytes 5124096
  21.7 27.2 copy-start.13
  23.4 681.5 %all-gather.21.cloned.1.call-start = ((), (), s32[]{:S(2)}) async-start(), calls=%async_computation.10 | async-start | bytes 34560000 | tf_op jit(solution)/shard_map/all_gather | solution.py:98
  48.9 8.2 copy-start.16
  48.9 1061.5 %all-gather.25.cloned.1.call-start = ((), (), s32[]{:S(2)}) async-start(), calls=%async_computation.12 | async-start | bytes 6400000 | tf_op jit(solution)/shard_map/all_gather | solution.py:93
  57.1 1076.1 %all-gather.23.cloned.1.call-start = ((), (), s32[]{:S(2)}) async-start(), calls=%async_computation.11 | async-start | bytes 11520000 | tf_op jit(solution)/shard_map/all_gather | solution.py:99
  76.4 1436.7 %all-reduce.31.cloned.1.call-start = ((), (), s32[]{:S(2)}) async-start(), calls=%async_computation.8 | async-start | bytes 40988672
  117.4 7.4 copy-start.11
  164.0 60.4 copy-start
  164.0 1403.9 %all-gather.13.cloned.1.call-start = ((), (), s32[]{:S(2)}) async-start(), calls=%async_computation.2 | async-start | bytes 4096000 | tf_op jit(solution)/shard_map/all_gather | solution.py:128
  224.6 865.1 %copy-start.19 = (f32[256]{0:T(256)}, f32[256]{0:T(256)S(1)}, u32[]{:S(2)}) copy-start(f32[256]{0:T(256)S(1)} %broadcast_multiply_fusion.1) | copy-start | bytes 3076
  224.9 864.8 %copy-start.21 = (f32[256]{0:T(256)}, f32[256]{0:T(256)S(1)}, u32[]{:S(2)}) copy-start(f32[256]{0:T(256)S(1)} %fusion.95) | copy-start | bytes 3076
  226.2 863.5 %copy-start.14 = (f32[1600]{0:T(1024)}, f32[1600]{0:T(1024)S(1)}, u32[]{:S(2)}) copy-start(f32[1600]{0:T(1024)S(1)} %get-tuple-element.229) | copy-start | bytes 19204
  226.2 863.6 %copy-start.17 = (f32[1600]{0:T(1024)}, f32[1600]{0:T(1024)S(1)}, u32[]{:S(2)}) copy-start(f32[1600]{0:T(1024)S(1)} %get-tuple-element.228) | copy-start | bytes 19204
  1107.0 469.1 %all-gather.15.cloned.1.call-start = ((), (), s32[]{:S(2)}) async-start(), calls=%async_computation.3 | async-start | bytes 4096000 | tf_op jit(solution)/shard_map/all_gather | solution.py:129
  1110.4 859.9 %all-gather.17.cloned.1.call-start = ((), (), s32[]{:S(2)}) async-start(), calls=%async_computation.4 | async-start | bytes 23040000 | tf_op jit(solution)/shard_map/all_gather | solution.py:101
  1132.3 1286.9 %reduce-scatter.3.cloned.1.call-start = ((), (), s32[]{:S(2)}) async-start(), calls=%async_computation.5 | async-start | bytes 8192000 | tf_op jit(solution)/shard_map/reduce_scatter | solution.py:216
  1133.1 1108.3 %copy-start.31 = (bf16[256]{0:T(256)(128)(2,1)}, bf16[256]{0:T(256)(128)(2,1)S(1)}, u32[]{:S(2)}) copy-start(bf16[256]{0:T(256)(128)(2,1)S(1)} %compare_convert_fusion) | copy-start | bytes 1540
  1681.0 323.2 %copy-start.4 = (bf16[1,256,1600]{1,2,0:T(8,128)(2,1)S(1)}, bf16[1,256,1600]{1,2,0:T(8,128)(2,1)}, u32[]{:S(2)}) copy-start(bf16[1,256,1600]{1,2,0:T(8,128)(2,1)} %param.14) | copy-start | bytes 2457604
  2240.6 181.1 %reduce-scatter.5.cloned.1.call-start = ((), (), s32[]{:S(2)}) async-start(), calls=%async_computation.6 | async-start | bytes 8192000 | tf_op jit(solution)/shard_map/reduce_scatter | solution.py:217
  2241.3 3845.4 %all-reduce.33.cloned.1.call-start = ((), (), s32[]{:S(2)}) async-start(), calls=%async_computation.13 | async-start | bytes 245817344
  2264.1 48.3 copy-start.8
  2474.8 3895.8 %all-reduce.35.cloned.1.call-start = ((), (), s32[]{:S(2)}) async-start(), calls=%async_computation.14 | async-start | bytes 30736384
  6103.8 6.6 copy-start.24
  6103.8 6.6 copy-start.30
  6103.8 6.7 copy-start.29
  6127.8 8.6 copy-start.28
  6136.0 44.8 copy-start.5
  6136.0 44.8 copy-start.26
  6136.1 44.7 copy-start.32
  (16 other events, 61.7 us)
Sparse Core Ops, SparseCore 0:
  13.6 35.2 all-gather.18
  51.3 66.0 all-reduce.28
  119.0 585.7 all-gather.20
  706.9 39.7 all-gather.24
  749.0 147.8 all-gather.22
  901.4 611.6 all-reduce.30
  1515.3 28.8 all-gather.12
  1546.3 29.6 all-gather.14
  1577.7 392.5 all-gather.16
  2240.7 60.0 reduce-scatter.2
  2303.4 60.0 reduce-scatter.4
  2474.9 3611.7 all-reduce.32
  6103.9 266.6 all-reduce.34
where the time goes:
time: 6410 us; the launch traced here: 6390 us
  waiting for transfers between devices  4960 us (77%)
  other arithmetic  434 us (7%)
  local copies, waits for them, and re-layouts  433 us (7%)
  matrix products  418 us (7%)
  blocking collectives  119 us (2%)
    unnamed x17, waiting for transfers between devices  4160 us
    all_gather x1, waiting for transfers between devices, local(): lax.all_gather(part_qkv, 'dp', axis=0, tiled=True)  479 us
    all_gather x1, other arithmetic, local(): lax.all_gather(part_qkv, 'dp', axis=0, tiled=True)  325 us
    all_gather x1, waiting for transfers between devices, local(): lax.all_gather(part_proj, 'dp', axis=0, tiled=True)  289 us
    unnamed x101, local copies, waits for them, and re-layouts  152 us
  transfers between devices with their start and end apart: 13, of which 8 were waited for; matrix products, arithmetic and copies ran while one was open for 15% of the time, Pallas kernels for 0%

commit v1 on v0

v1 whole, which is shorter than its diff:
```python
from functools import partial

import jax
import jax.numpy as jnp
from jax import lax
from jax.experimental import pallas as pl
from jax.experimental.pallas import tpu as pltpu
from jax.sharding import PartitionSpec as P

HD = 64
EPS = 1e-05
LANES = 128
BF = jnp.bfloat16
F32 = jnp.float32


def swap(value, axis, size, bit):
    return lax.ppermute(value, axis, [(i, i ^ bit) for i in range(size)])


def bits_of(size):
    return [1 << k for k in reversed(range(size.bit_length() - 1))]


def gather_relative(value, axis, size):
    pieces = {0: value}
    for bit in bits_of(size):
        for j in list(pieces):
            pieces[j ^ bit] = swap(pieces[j], axis, size, bit)
    return [pieces[j] for j in range(size)]


def gather_dp(value, size):
    if size > 8:
        return lax.all_gather(value, "dp", axis=0, tiled=False)
    mine = lax.axis_index("dp")
    out = jnp.zeros((size, *value.shape), value.dtype)
    for j, piece in enumerate(gather_relative(value, "dp", size)):
        out = lax.dynamic_update_index_in_dim(out, piece, mine ^ j, 0)
    return out


def scatter_dp(value, size):
    if size > 8:
        return lax.psum_scatter(value.astype(BF), "dp", scatter_dimension=0, tiled=False).astype(F32)
    mine = lax.axis_index("dp")
    bits = bits_of(size)
    value = value.reshape((2,) * len(bits) + value.shape[1:])
    for axis in reversed(range(len(bits))):
        bit = bits[axis]
        side = (mine // bit) % 2
        sent = lax.dynamic_index_in_dim(value, 1 - side, axis, keepdims=False).astype(BF)
        kept = lax.dynamic_index_in_dim(value, side, axis, keepdims=False)
        value = kept.astype(F32) + swap(sent, "dp", size, bit).astype(F32)
    return value


def scatter_seq(blocks, size):
    blocks = dict(enumerate(blocks))
    for bit in reversed(bits_of(size)):
        for j in sorted(blocks, reverse=True):
            if j & bit:
                got = swap(blocks.pop(j).astype(BF), "seq", size, bit)
                blocks[j ^ bit] = blocks[j ^ bit].astype(F32) + got.astype(F32)
    return blocks[0]


def pick(pieces, index):
    out = pieces[0]
    for k in range(1, len(pieces)):
        out = jnp.where(index == k, pieces[k], out)
    return out


def exchange_seq(pieces, size):
    mine = lax.axis_index("seq")
    got = []
    for j in range(size):
        sent = pick([pieces[b ^ j] for b in range(size)], mine)
        got.append(sent if j == 0 else swap(sent, "seq", size, j))
    return [pick([got[b ^ m] for m in range(size)], mine) for b in range(size)]


def pack_heads(value, size):
    rows, _, width = value.shape
    heads = width // HD
    own = -(-heads // size)
    value = jnp.pad(value.reshape(rows, 3, heads, HD), ((0, 0), (0, 0), (0, own * size - heads), (0, 0)))
    out = []
    for s in range(size):
        part = value[:, :, s * own : (s + 1) * own]
        even = own - own % 2
        cols = [part[:, :, :even].reshape(rows, -1)]
        if own % 2:
            cols += [part[:, :, even].reshape(rows, -1), jnp.zeros((rows, HD), value.dtype)]
        out.append(jnp.concatenate(cols, axis=1))
    return out


def unpack_heads(pieces, width):
    rows = pieces[0].shape[0]
    heads = width // HD
    own = -(-heads // len(pieces))
    even = own - own % 2
    out = []
    for piece in pieces:
        part = piece[:, : 3 * even * HD].reshape(rows, 3, even * HD)
        if own % 2:
            last = piece[:, 3 * even * HD : 3 * own * HD].reshape(rows, 3, HD)
            part = jnp.concatenate([part, last], axis=2)
        out.append(part)
    return jnp.concatenate(out, axis=2)[:, :, :width].reshape(rows, 3 * width)


def pack_hidden(value, size, dps):
    rows, hidden = value.shape
    value = value.reshape(rows, dps, size, hidden // (dps * size))
    return [value[:, :, s].reshape(rows, hidden // size) for s in range(size)]


def unpack_hidden(pieces, dps):
    rows, own = pieces[0].shape
    parts = [piece.reshape(rows, dps, 1, own // dps) for piece in pieces]
    return jnp.concatenate(parts, axis=2).reshape(rows, own * len(pieces))


def columns_from_rows(flat, rows, pack, size):
    cols = flat.shape[0] * size // rows
    if rows % size == 0:
        return jnp.concatenate(exchange_seq(pack(flat.reshape(rows // size, cols)), size), axis=0)
    full = lax.all_gather(flat, "seq", axis=0, tiled=True).reshape(rows, cols)
    return pick(pack(full), lax.axis_index("seq"))


def rows_from_columns(value, unpack, size):
    rows = value.shape[0]
    value = value.astype(BF)
    if rows % size == 0:
        part = rows // size
        return unpack(exchange_seq([value[b * part : (b + 1) * part] for b in range(size)], size)).reshape(-1)
    full = lax.all_gather(value, "seq", axis=0, tiled=False)
    full = unpack([full[b] for b in range(size)]).reshape(-1)
    count = full.shape[0] // size
    return lax.dynamic_slice_in_dim(full, lax.axis_index("seq") * count, count)


def half_masks():
    lane = lax.broadcasted_iota(jnp.int32, (1, LANES), 1)
    return [lane < HD, lane >= HD]


def row_block(ref, block, rows):
    return ref[pl.ds(pl.multiple_of(block * rows, rows), rows), :]


def attention_forward_kernel(size, pairs, odd, info, q_ref, k_ref, v_ref, o_ref, k_all, v_all):
    mine, length = info[0], info[1]
    count = q_ref.shape[0] // size
    pair = pl.program_id(0)
    last = pair == pairs - 1
    for a in range(size):
        rows = pl.ds(a * count, count)
        keys = row_block(k_ref, mine ^ a, count)
        if odd:
            keys = jnp.where(last, jnp.roll(keys, HD, axis=1), keys)
        k_all[rows, :] = keys
        v_all[rows, :] = row_block(v_ref, mine ^ a, count)
    halves = half_masks()
    zero = jnp.zeros((), BF)

    def one(a, half):
        span = (a + 1) * count
        q = jnp.where(half, row_block(q_ref, mine ^ a, count), zero)
        s = lax.dot_general(q, k_all[:span, :], (((1,), (1,)), ((), ())), preferred_element_type=F32) * 0.125
        limit = jnp.minimum(a * count + lax.broadcasted_iota(jnp.int32, (count, 1), 0), length - 1)
        allowed = lax.broadcasted_iota(jnp.int32, (count, span), 1) <= limit
        s = jnp.where(allowed, s, -1e30)
        e = jnp.exp(s - jnp.max(s, axis=1, keepdims=True))
        p = (e * (1.0 / jnp.sum(e, axis=1, keepdims=True))).astype(BF)
        return jnp.dot(p, v_all[:span, :], preferred_element_type=F32)

    for a in range(size):
        rows = pl.ds(pl.multiple_of((mine ^ a) * count, count), count)
        first = one(a, halves[0])
        if not odd:
            o_ref[rows, :] = jnp.where(halves[0], first, one(a, halves[1])).astype(BF)
            continue
        o_ref[rows, :] = jnp.where(halves[0], first, 0.0).astype(BF)

        @pl.when(jnp.logical_not(last))
        def _():
            o_ref[rows, :] = jnp.where(halves[0], o_ref[rows, :], one(a, halves[1]).astype(BF))


def attention_backward_kernel(size, pairs, odd, info, q_ref, k_ref, v_ref, g_ref, d_ref, k_all, v_all, dq, dk, dv):
    mine, length = info[0], info[1]
    count = q_ref.shape[0] // size
    pair = pl.program_id(0)
    last = pair == pairs - 1
    for a in range(size):
        rows = pl.ds(a * count, count)
        keys = row_block(k_ref, mine ^ a, count)
        if odd:
            keys = jnp.where(last, jnp.roll(keys, HD, axis=1), keys)
        k_all[rows, :] = keys
        v_all[rows, :] = row_block(v_ref, mine ^ a, count)
    dk[...] = jnp.zeros_like(dk)
    dv[...] = jnp.zeros_like(dv)
    halves = half_masks()
    zero = jnp.zeros((), BF)

    def one(a, which):
        half = halves[which]
        span = (a + 1) * count
        rows = pl.ds(a * count, count)
        q = jnp.where(half, row_block(q_ref, mine ^ a, count), zero)
        g = jnp.where(half, row_block(g_ref, mine ^ a, count), zero)
        keys, values = k_all[:span, :], v_all[:span, :]
        contract = (((1,), (1,)), ((), ()))
        s = lax.dot_general(keys, q, contract, preferred_element_type=F32) * 0.125
        limit = jnp.minimum(a * count + lax.broadcasted_iota(jnp.int32, (1, count), 1), length - 1)
        allowed = lax.broadcasted_iota(jnp.int32, (span, count), 0) <= limit
        s = jnp.where(allowed, s, -1e30)
        e = jnp.exp(s - jnp.max(s, axis=0, keepdims=True))
        p = e * (1.0 / jnp.sum(e, axis=0, keepdims=True))
        dp = lax.dot_general(values, g, contract, preferred_element_type=F32)
        inner = jnp.sum(p * dp, axis=0, keepdims=True)
        ds = (p * (dp - inner) * 0.125).astype(BF)
        dv[:span, :] += jnp.dot(p.astype(BF), g, preferred_element_type=F32)
        dk[:span, :] += jnp.dot(ds, q, preferred_element_type=F32)
        part = lax.dot_general(ds, keys, (((0,), (0,)), ((), ())), preferred_element_type=F32)
        if which == 0:
            dq[rows, :] = jnp.where(half, part, 0.0)
        else:
            dq[rows, :] = jnp.where(half, part, dq[rows, :])

    for a in range(size):
        one(a, 0)
    if odd:

        @pl.when(jnp.logical_not(last))
        def _():
            for a in range(size):
                one(a, 1)
    else:
        for a in range(size):
            one(a, 1)

    def store(block, value_of):
        cols = pl.ds(pl.multiple_of(block * LANES, LANES), LANES)
        for a in range(size):
            rows = pl.ds(pl.multiple_of((mine ^ a) * count, count), count)
            d_ref[rows, cols] = value_of(pl.ds(a * count, count)).astype(BF)

    full = pairs - 1 if odd else pairs

    def plain():
        store(pair, lambda r: dq[r, :])
        store(full + pair, lambda r: dk[r, :])
        store(2 * full + pair, lambda r: dv[r, :])

    if not odd:
        plain()
        return
    pl.when(jnp.logical_not(last))(plain)

    @pl.when(last)
    def _():
        store(3 * full, lambda r: jnp.where(halves[0], dq[r, :], jnp.roll(dk[r, :], HD, axis=1)))
        store(3 * full + 1, lambda r: jnp.where(halves[0], dv[r, :], 0.0))


def head_specs(span, pairs, odd):
    full = pairs - 1 if odd else pairs

    def spec(part):
        def index(j, info):
            if not odd:
                return (0, part * full + j)
            return (0, jnp.where(j < full, part * full + j, 3 * full + (part == 2)))

        return pl.BlockSpec((span, LANES), index)

    return [spec(0), spec(1), spec(2)]


def attention_forward(info, mixed, own, size):
    span = mixed.shape[0]
    pairs, odd = -(-own // 2), own % 2
    return pl.pallas_call(
        partial(attention_forward_kernel, size, pairs, odd),
        out_shape=jax.ShapeDtypeStruct((span, pairs * LANES), BF),
        grid_spec=pltpu.PrefetchScalarGridSpec(
            num_scalar_prefetch=1,
            grid=(pairs,),
            in_specs=head_specs(span, pairs, odd),
            out_specs=pl.BlockSpec((span, LANES), lambda j, info: (0, j)),
            scratch_shapes=[pltpu.VMEM((span, LANES), BF)] * 2,
        ),
        compiler_params=pltpu.CompilerParams(vmem_limit_bytes=40 << 20),
        cost_estimate=pl.CostEstimate(
            flops=own * span * span * 256, transcendentals=own * span * span // 2, bytes_accessed=mixed.size * 4
        ),
        name="attention_forward",
    )(info, mixed, mixed, mixed)


def attention_backward(info, mixed, grad, own, size):
    span = mixed.shape[0]
    pairs, odd = -(-own // 2), own % 2
    return pl.pallas_call(
        partial(attention_backward_kernel, size, pairs, odd),
        out_shape=jax.ShapeDtypeStruct(mixed.shape, BF),
        grid_spec=pltpu.PrefetchScalarGridSpec(
            num_scalar_prefetch=1,
            grid=(pairs,),
            in_specs=[*head_specs(span, pairs, odd), pl.BlockSpec((span, LANES), lambda j, info: (0, j))],
            out_specs=pl.BlockSpec(mixed.shape, lambda j, info: (0, 0)),
            scratch_shapes=[pltpu.VMEM((span, LANES), BF)] * 2 + [pltpu.VMEM((span, LANES), F32)] * 3,
        ),
        compiler_params=pltpu.CompilerParams(vmem_limit_bytes=48 << 20),
        cost_estimate=pl.CostEstimate(
            flops=own * span * span * 768, transcendentals=own * span * span // 2, bytes_accessed=mixed.size * 6
        ),
        name="attention_backward",
    )(info, mixed, mixed, mixed, grad)


def normal(value):
    centre = value - jnp.mean(value, axis=-1, keepdims=True)
    scale = lax.rsqrt(jnp.mean(centre * centre, axis=-1, keepdims=True) + EPS)
    return centre * scale, scale


def norm_input_grad(unit, scale, gain, grad):
    scaled = grad * gain
    return scale * (
        scaled
        - jnp.mean(scaled, axis=-1, keepdims=True)
        - unit * jnp.mean(scaled * unit, axis=-1, keepdims=True)
    )


ROOT = 0.7978845608028654
CUBIC = 0.044715


def gelu(u):
    return 0.5 * u * (1.0 + jnp.tanh(ROOT * (u + CUBIC * u * u * u)))


def gelu_slope(u):
    t = jnp.tanh(ROOT * (u + CUBIC * u * u * u))
    return 0.5 * (1.0 + t) + 0.5 * u * (1.0 - t * t) * ROOT * (1.0 + 3.0 * CUBIC * u * u)


def dot(a, b, dims=((1,), (0,))):
    return lax.dot_general(a, b, (dims, ((), ())), preferred_element_type=F32)


def local(size, dps, tokens, cotangent, lengths, w_qkv, w_out, w_fc, w_proj, attention_vectors, block_vectors):
    _, count, width = tokens.shape
    heads = width // HD
    own = -(-heads // size)
    hidden = w_proj.shape[0] * dps * size // width
    rank = lax.axis_index("seq")
    row = lax.axis_index("dp")
    device = row * size + rank
    devices = dps * size
    length = lengths[0]
    info = jnp.stack([rank.astype(jnp.int32), length])
    unit_rows = width // dps

    vectors = lax.all_gather(jnp.stack([attention_vectors, block_vectors]), ("dp", "seq"), axis=1, tiled=True)
    vectors = vectors.astype(F32).reshape(8, width)
    gain1, shift1, bias_q, bias_v, bias_o, gain2, shift2, bias_p = (vectors[k] for k in range(8))

    x_own = tokens[0]
    x_all = jnp.concatenate(gather_relative(x_own, "seq", size), axis=0)
    place = rank * count + jnp.arange(count)
    dy_own = cotangent[0] * (place < length).astype(BF)[:, None]

    pack3 = lambda m: pack_heads(m.reshape(m.shape[0], 3, width), size)
    qkv_part = columns_from_rows(w_qkv, unit_rows, pack3, size)
    qkv_full = gather_dp(qkv_part, dps).reshape(width, -1)

    out_parts = gather_dp(w_out, dps)
    out_parts = gather_relative(out_parts, "seq", size)
    out_full = jnp.stack([pick([out_parts[b ^ m] for m in range(size)], rank) for b in range(size)], axis=1)
    out_full = out_full.reshape(width, width)

    shift = hidden // devices
    tail = -(-shift * devices // LANES) * LANES
    plain = w_fc.shape[0] - shift
    before = lax.ppermute(w_fc[-tail:], ("dp", "seq"), [(i, i + 1) for i in range(devices - 1)])
    fc_flat = lax.dynamic_slice_in_dim(jnp.concatenate([before, w_fc]), tail - shift * device, plain)
    bias_rows = lax.psum(jnp.where(device == devices - 1, w_fc[-hidden:], jnp.zeros((), BF)).astype(F32), ("dp", "seq"))
    pack_fc = lambda m: pack_hidden(m, size, dps)
    fc_part = columns_from_rows(fc_flat, unit_rows, pack_fc, size)
    fc_full = gather_dp(fc_part, dps).reshape(width, -1)
    bias_fc = pick(pack_fc(bias_rows[None]), rank)

    proj_full = gather_dp(w_proj.reshape(-1, width), dps).reshape(-1, width)

    unit1_all, _ = normal(x_all.astype(F32))
    h1 = (unit1_all * gain1 + shift1).astype(BF)
    bias_qkv = pick(pack3(jnp.stack([bias_q, jnp.zeros_like(bias_q), bias_v])[None]), rank)
    mixed = (dot(h1, qkv_full) + bias_qkv).astype(BF)
    o_heads = attention_forward(info, mixed, own, size)
    o_got = [o_heads[:count]] + [
        swap(o_heads[j * count : (j + 1) * count], "seq", size, j) for j in range(1, size)
    ]
    o_own = jnp.concatenate([pick([o_got[b ^ m] for m in range(size)], rank)[:, : own * HD] for b in range(size)], axis=1)
    o_own = o_own[:, :width]
    x2 = x_own.astype(F32) + dot(o_own, out_full) + bias_o
    unit2, scale2 = normal(x2)
    h2_own = (unit2 * gain2 + shift2).astype(BF)
    h2 = jnp.concatenate(gather_relative(h2_own, "seq", size), axis=0)
    dy = jnp.concatenate(gather_relative(dy_own, "seq", size), axis=0)
    u = dot(h2, fc_full) + bias_fc
    a = gelu(u).astype(BF)
    split = lambda m: [m[j * count : (j + 1) * count] for j in range(size)]
    output = (x2 + scatter_seq(split(dot(a, proj_full)), size) + bias_p).astype(BF)

    dy_wide = dy_own.astype(F32)
    grad_proj = scatter_dp(dot(a, dy, ((0,), (0,))).reshape(dps, -1, width), dps).reshape(-1)
    grad_bp = jnp.sum(dy_wide, axis=0)
    du = (dot(dy, proj_full, ((1,), (1,))) * gelu_slope(u)).astype(BF)
    grad_bf = jnp.sum(du.astype(F32), axis=0)
    dh2 = scatter_seq(split(dot(du, fc_full, ((1,), (1,)))), size)
    grad_fc = scatter_dp(dot(h2, du, ((0,), (0,))).reshape(dps, unit_rows, -1), dps)
    grad_g2 = jnp.sum(dh2 * unit2, axis=0)
    grad_c2 = jnp.sum(dh2, axis=0)
    dx2 = dy_wide + norm_input_grad(unit2, scale2, gain2, dh2)
    dz = dx2.astype(BF)
    grad_bo = jnp.sum(dz.astype(F32), axis=0)

    do_own = jnp.pad(dot(dz, out_full, ((1,), (1,))).astype(BF), ((0, 0), (0, own * size * HD - width)))
    do_blocks = [jnp.pad(do_own[:, b * own * HD : (b + 1) * own * HD], ((0, 0), (0, own % 2 * HD))) for b in range(size)]
    do_got = []
    for j in range(size):
        sent = pick([do_blocks[b ^ j] for b in range(size)], rank)
        do_got.append(sent if j == 0 else swap(sent, "seq", size, j))
    do_heads = jnp.concatenate(do_got, axis=0)
    grad_out = dot(o_own, dz, ((0,), (0,)))
    grad_out = grad_out.reshape((dps, size, -1, width) if width % devices == 0 else (dps, size, -1))
    grad_out = scatter_seq([lax.dynamic_index_in_dim(grad_out, rank ^ j, 1, keepdims=False) for j in range(size)], size)
    grad_out = scatter_dp(grad_out, dps).reshape(-1)
    dmixed = attention_backward(info, mixed, do_heads, own, size)
    grad_mixed = jnp.sum(dmixed.astype(F32), axis=0)
    dh1_part = dot(dmixed, qkv_full, ((1,), (1,)))
    grad_c1 = jnp.sum(dh1_part, axis=0)
    grad_g1 = jnp.sum(dh1_part * unit1_all, axis=0)
    dh1 = scatter_seq(split(dh1_part), size)
    grad_qkv = scatter_dp(dot(h1, dmixed, ((0,), (0,))).reshape(dps, unit_rows, -1), dps)
    unit1, scale1 = normal(x_own.astype(F32))
    input_grad = dx2 + norm_input_grad(unit1, scale1, gain1, dh1)

    place_cols = lambda v, pack_size, unpack: unpack([jnp.where(rank == b, v, 0.0)[None] for b in range(pack_size)])[0]
    wide = place_cols(grad_mixed, size, lambda p: unpack_heads(p, width)).reshape(3, width)
    wide_bf = place_cols(grad_bf, size, lambda p: unpack_hidden(p, dps))
    sums = jnp.concatenate(
        [grad_g1, grad_c1, wide[0], wide[2], grad_bo, grad_g2, grad_c2, grad_bp, wide_bf]
    )
    sums = lax.psum(sums, ("dp", "seq"))
    part = attention_vectors.shape[0]
    vec1 = lax.dynamic_slice_in_dim(sums[: 4 * width], device * part, part)
    vec2 = lax.dynamic_slice_in_dim(sums[4 * width : 8 * width], device * part, part)
    sum_bf = sums[8 * width :]

    qkv_flat = rows_from_columns(grad_qkv, lambda p: unpack_heads(p, width), size).astype(F32)
    fc_rows = rows_from_columns(grad_fc, lambda p: unpack_hidden(p, dps), size)
    after = lax.ppermute(fc_rows[:tail], ("dp", "seq"), [(i + 1, i) for i in range(devices - 1)])
    fill = jnp.pad(sum_bf, (0, tail - hidden))
    after = jnp.where(device == devices - 1, fill, after.astype(F32))
    fc_flat_grad = lax.dynamic_slice_in_dim(
        jnp.concatenate([fc_rows.astype(F32), after]), shift * device, w_fc.shape[0]
    )
    return (output[None], input_grad[None], qkv_flat, grad_out, fc_flat_grad, grad_proj, vec1, vec2)


def solution(mesh):
    tokens = P("dp", "seq", None)
    flat = P(("dp", "seq"))
    return jax.shard_map(
        partial(local, mesh.shape["seq"], mesh.shape["dp"]),
        mesh=mesh,
        in_specs=(tokens, tokens, P("dp"), *[flat] * 6),
        out_specs=(tokens, tokens, *[flat] * 6),
        check_vma=False,
    )
```

time: 6410 us -> 885 us (0.14)
  waiting for transfers between devices: 4960 us -> 276 us
  other arithmetic: 434 us -> 65.4 us
  matrix products: 418 us -> 107 us
  local copies, waits for them, and re-layouts: 433 us -> 209 us
  starting transfers between devices: 0.53 us -> 73.4 us
    unnamed x17 -> x1, waiting for transfers between devices: 4160 us -> 0.02 us
    all_gather x7 -> x0, waiting for transfers between devices: 794 us -> none  [the longest x1 479 us: local(): lax.all_gather(part_qkv, 'dp', axis=0, tiled=True)]
    all_gather x3 -> x0, other arithmetic: 375 us -> none  [the longest x1 325 us: local(): lax.all_gather(part_qkv, 'dp', axis=0, tiled=True)]
    dot_general x187 -> x12, matrix products: 418 us -> 107 us  [dot(): return lax.dot_general(a, b, (dims, ((), ())), preferred_element_type=F32)]
    ppermute x0 -> x84, waiting for transfers between devices: none -> 276 us  [the longest x82 276 us: swap(): return lax.ppermute(value, axis, [(i, i ^ bit) for i in range(size)])]
    reshape x11 -> x30, local copies, waits for them, and re-layouts: 225 us -> 36.6 us  [the longest x1 11.4 us: local(): out_full = out_full.reshape(width, width)]
    unnamed x101 -> x105, local copies, waits for them, and re-layouts: 152 us -> 18.6 us
    unnamed x4 -> x0, blocking collectives: 100 us -> none
  transfers between devices with their start and end apart: 13 -> 85, of which waited for: 8 -> 26; matrix products, arithmetic and copies ran while one was open for 15% -> 39% of each run, Pallas kernels for 0% -> 6%
where the time goes in v1:
time: 885 us; the launch traced here: 873 us
  waiting for transfers between devices  276 us (31%)
  local copies, waits for them, and re-layouts  209 us (24%)
  matrix products  107 us (12%)
  blocking collectives  76.8 us (9%)
  starting transfers between devices  73.4 us (8%)
  other arithmetic  65.4 us (7%)
  Pallas kernels  48.8 us (6%)
  between operations  16.9 us (2%)
    ppermute x82, waiting for transfers between devices, swap(): return lax.ppermute(value, axis, [(i, i ^ bit) for i in range(size)])  276 us
    dot_general x12, matrix products, dot(): return lax.dot_general(a, b, (dims, ((), ())), preferred_element_type=F32)  107 us
    dynamic_update_slice x30, local copies, waits for them, and re-layouts, gather_dp(): out = lax.dynamic_update_index_in_dim(out, piece, mine ^ j, 0)  77.3 us
    ppermute x82, starting transfers between devices, swap(): return lax.ppermute(value, axis, [(i, i ^ bit) for i in range(size)])  69.6 us
    all_gather x1, blocking collectives, local(): lax.all_gather(jnp.stack([attention_vectors, block_vectors]), ('dp', 'seq...  39.7 us
    psum x1, blocking collectives, local(): lax.psum(jnp.where(device == devices - 1, w_fc[-hidden:], jnp.zeros((), B...  37 us
    pallas_call x1, Pallas kernels, attention_backward(): pl.pallas_call(partial(attention_backward_kernel, size, pairs, odd), out_...  27.6 us
    pallas_call x1, Pallas kernels, attention_forward(): pl.pallas_call(partial(attention_forward_kernel, size, pairs, odd), out_s...  21.1 us
  transfers between devices with their start and end apart: 85, of which 26 were waited for; matrix products, arithmetic and copies ran while one was open for 39% of the time, Pallas kernels for 6%

profile of v1, /device:TPU:0, one launch (start us, length us, event | category | flops | bytes accessed | tf_op | source)
XLA Modules:
  0.0 873.4 jit_solution(366787926861316032)
XLA Ops:
  22.1 39.7 %all-gather = bf16[32,200,2]{1,2,0:T(2,128)(2,1)S(1)} all-gather(bf16[1,200,2]{1,2,0:T(2,128)(2,1)S(1)} %maximum_bitcast_fusion), channel_id=1, replica_groups=mesh['dp'=8,'seq'=4] {'dp','seq'}, dimensions={0}, use_global_device_ids=true | all-gather | bytes 26400 | tf_op jit(solution)/shard_map/all_gather | solution.py:374
  63.8 37.0 %psum.14 = f32[1,8,4,200]{3,2,1,0:T(4,128)S(1)} all-reduce(f32[1,8,4,200]{3,2,1,0:T(4,128)S(1)} %reshape_broadcast_in_dim.5), channel_id=1, replica_groups=mesh['dp'=8,'seq'=4] {'dp','seq'}, use_global_device_ids=true, to_apply=%region_4.5 | all-reduce | flops 6400 | bytes 51200 | tf_op jit(solution)/shard_map/psum | solution.py:397
  167.3 13.9 %collective-permute-done.21 = bf16[80000]{0:T(1024)(128)(2,1)} collective-permute-done((bf16[80000]{0:T(1024)(128)(2,1)}, bf16[80000]{0:T(1024)(128)(2,1)}, u32[]{:S(2)}, u32[]{:S(2)}) %collective-permute-start.21) | collective-permute-done | bytes 160032 | tf_op jit(solution)/shard_map/ppermute | solution.py:18
  188.1 7.0 dynamic_update_slice.110
  233.6 14.2 %collective-permute-done.7 = bf16[200,1408]{1,0:T(8,128)(2,1)S(1)} collective-permute-done((bf16[200,1408]{1,0:T(8,128)(2,1)}, bf16[200,1408]{1,0:T(8,128)(2,1)S(1)}, u32[]{:S(2)}, u32[]{:S(2)}) %collective-permute-start.7) | collective-permute-done | bytes 563232 | tf_op jit(solution)/shard_map/ppermute | solution.py:18
  253.3 22.3 %collective-permute-done.34 = bf16[200,1600]{1,0:T(8,128)(2,1)S(1)} collective-permute-done((bf16[200,1600]{1,0:T(8,128)(2,1)S(1)}, bf16[200,1600]{1,0:T(8,128)(2,1)S(1)}, u32[]{:S(2)}, u32[]{:S(2)}) %collective-permute-start.34) | collective-permute-done | bytes 640032 | tf_op jit(solution)/shard_map/ppermute | solution.py:18
  280.0 9.4 %collective-permute-done.10 = bf16[200,1408]{1,0:T(8,128)(2,1)S(1)} collective-permute-done((bf16[200,1408]{1,0:T(8,128)(2,1)S(1)}, bf16[200,1408]{1,0:T(8,128)(2,1)S(1)}, u32[]{:S(2)}, u32[]{:S(2)}) %collective-permute-start.10) | collective-permute-done | bytes 563232 | tf_op jit(solution)/shard_map/ppermute | solution.py:18
  298.1 9.4 %collective-permute-done.42 = bf16[200,1600]{1,0:T(8,128)(2,1)S(1)} collective-permute-done((bf16[200,1600]{1,0:T(8,128)(2,1)}, bf16[200,1600]{1,0:T(8,128)(2,1)S(1)}, u32[]{:S(2)}, u32[]{:S(2)}) %collective-permute-start.42) | collective-permute-done | bytes 640032 | tf_op jit(solution)/shard_map/ppermute | solution.py:18
  311.2 7.7 collective-permute-done.44
  319.8 9.7 %collective-permute-done.45 = bf16[200,1600]{1,0:T(8,128)(2,1)S(1)} collective-permute-done((bf16[200,1600]{1,0:T(8,128)(2,1)S(1)}, bf16[200,1600]{1,0:T(8,128)(2,1)S(1)}, u32[]{:S(2)}, u32[]{:S(2)}) %collective-permute-start.45) | collective-permute-done | bytes 640032 | tf_op jit(solution)/shard_map/ppermute | solution.py:18
  337.3 19.7 %collective-permute-done.23 = bf16[8,80000]{1,0:T(8,128)(2,1)} collective-permute-done((bf16[8,80000]{1,0:T(8,128)(2,1)S(1)}, bf16[8,80000]{1,0:T(8,128)(2,1)}, u32[]{:S(2)}, u32[]{:S(2)}) %collective-permute-start.23) | collective-permute-done | bytes 1280032 | tf_op jit(solution)/shard_map/ppermute | solution.py:18
  360.9 7.7 add_convert_fusion.q_ref.k_ref.v_ref
  368.6 21.1 %attention_forward.1 = bf16[1024,512]{1,0:T(8,128)(2,1)S(1)} custom-call(s32[2]{0:T(128)S(1)} %pad_add_fusion.info, bf16[1024,1408]{1,0:T(8,128)(2,1)S(1)} %add_convert_fusion.q_ref.k_ref.v_ref, bf16[1024,1408]{1,0:T(8,128)(2,1)S(1)} %add_convert_fusion.q_ref.k_ref.v_ref, bf16[1024,1408]{1,0:T(8,128)(2,1)S(1)} %add_convert_fusion.q_ref.k_ref.v_ref), custom_call_target="tpu_custom_call" | custom-call | flops 1879048192 | bytes 5767168 | tf_op jit(solution)/shard_map/attention_forward/pallas_call | solution.py:290
  408.5 7.5 collective-permute-done.38
  425.8 11.4 %reshape.433 = bf16[1600,1600]{1,0:T(8,128)(2,1)} reshape(bf16[8,4,80000]{2,1,0:T(4,128)(2,1)} %copy.88) | data formatting | bytes 10240000 | tf_op jit(solution)/shard_map/reshape | solution.py:390
  447.9 15.1 %collective-permute-done.27 = bf16[256,1600]{0,1:T(8,128)(2,1)S(1)} collective-permute-done((bf16[256,1600]{0,1:T(8,128)(2,1)S(1)}, bf16[256,1600]{0,1:T(8,128)(2,1)S(1)}, u32[]{:S(2)}, u32[]{:S(2)}) %collective-permute-start.27) | collective-permute-done | bytes 819232 | tf_op jit(solution)/shard_map/ppermute | solution.py:18
  467.2 11.1 %fusion.60 = f32[1024,1600]{0,1:T(8,128)} fusion(bf16[1600,1600]{1,0:T(8,128)(2,1)} %bitcast.26, bf16[256,1600]{0,1:T(8,128)(2,1)S(1)} %collective-permute-done.28, bf16[256,1600]{0,1:T(8,128)(2,1)S(1)} %collective-permute-done.27, bf16[256,1600]{0,1:T(8,128)(2,1)S(1)} %collective-permute-done.26, bf16[256,1600]{0,1:T(8,128)(2,1)S(1)} %add_convert_fusion.1), kind=kOutput, calls=%fused_computation.155 | convolution fusion | flops 5255987200 | bytes 14950400 | tf_op jit(solution)/shard_map/dot_general | solution.py:358
  478.2 11.3 %fusion.84 = (bf16[1024,1600]{0,1:T(8,128)(2,1)S(1)}, f32[1024,1600]{0,1:T(8,128)}) fusion(bf16[1600,1600]{1,0:T(8,128)(2,1)S(1)} %bitcast.180, f32[1024,1600]{0,1:T(8,128)} %fusion.60, f32[1600]{0:T(1024)S(1)} %select_n.1051), kind=kOutput, calls=%fused_computation.293 | convolution fusion | flops 5260902400 | bytes 21510400 | tf_op jit(solution)/shard_map/dot_general | solution.py:358
  489.5 13.7 %convert_reduce_fusion.1 = (f32[1600]{0:T(1024)S(1)}, bf16[1024,1600]{0,1:T(8,128)(2,1)S(1)}) fusion(f32[1024,1600]{0,1:T(8,128)} %fusion.60, f32[1600]{0:T(1024)S(1)} %select_n.1051, bf16[1600,1600]{1,0:T(8,128)(2,1)S(1)} %bitcast.181, bf16[256,1600]{0,1:T(8,128)(2,1)} %collective-permute-done.52, bf16[256,1600]{0,1:T(8,128)(2,1)} %collective-permute-done.51, ...), kind=kOutput, calls=%fused_computation.19 | convolution fusion | flops 5292030464 | bytes 18240000 | tf_op jit(solution)/shard_map/dot_general | solution.py:358
  503.3 9.8 %fusion.83 = (bf16[1024,1600]{0,1:T(8,128)(2,1)S(1)}, f32[1024,1600]{0,1:T(8,128)}) fusion(bf16[1600,1600]{1,0:T(8,128)(2,1)} %bitcast.26, bf16[1024,1600]{0,1:T(8,128)(2,1)S(1)} %get-tuple-element.136), kind=kOutput, calls=%fused_computation.292 | convolution fusion | flops 5244518400 | bytes 18227200 | tf_op jit(solution)/shard_map/dot_general | solution.py:358
  528.8 15.6 %fusion.58 = f32[1600,1600]{1,0:T(8,128)} fusion(bf16[256,1600]{0,1:T(8,128)(2,1)} %collective-permute-done.52, bf16[256,1600]{0,1:T(8,128)(2,1)} %collective-permute-done.51, bf16[256,1600]{0,1:T(8,128)(2,1)} %collective-permute-done.50, bf16[256,1600]{0,1:T(8,128)(2,1)} %get-tuple-element.35, f32[1024,1600]{0,1:T(8,128)} %fusion.60, f32[1600]{0:T(1024)S(1)} %select_n.1051), kind=kOutput, calls=%fused_computation.153 | convolution fusion | flops 5272371200 | bytes 20076800 | tf_op jit(solution)/shard_map/dot_general | solution.py:358
  556.7 11.2 %collective-permute-done.55 = bf16[256,1600]{0,1:T(8,128)(2,1)S(1)} collective-permute-done((bf16[256,1600]{0,1:T(8,128)(2,1)S(1)}, bf16[256,1600]{0,1:T(8,128)(2,1)S(1)}, u32[]{:S(2)}, u32[]{:S(2)}) %collective-permute-start.55) | collective-permute-done | bytes 819232 | tf_op jit(solution)/shard_map/ppermute | solution.py:18
  570.9 13.9 %collective-permute-done.49 = bf16[256,1600]{0,1:T(8,128)(2,1)S(1)} collective-permute-done((bf16[256,1600]{0,1:T(8,128)(2,1)S(1)}, bf16[256,1600]{0,1:T(8,128)(2,1)S(1)}, u32[]{:S(2)}, u32[]{:S(2)}) %collective-permute-start.49) | collective-permute-done | bytes 819232 | tf_op jit(solution)/shard_map/ppermute | solution.py:18
  598.8 10.7 %reshape.444 = f32[8,4,50,1600]{3,2,1,0:T(8,128)} reshape(f32[1600,1600]{1,0:T(8,128)} %fusion.50) | data formatting | bytes 20480000 | tf_op jit(solution)/shard_map/reshape | solution.py:446
  621.4 27.6 %attention_backward.1 = bf16[1024,1408]{1,0:T(8,128)(2,1)S(1)} custom-call(s32[2]{0:T(128)S(1)} %pad_add_fusion.info, bf16[1024,1408]{1,0:T(8,128)(2,1)} %copy-done, bf16[1024,1408]{1,0:T(8,128)(2,1)} %copy-done, bf16[1024,1408]{1,0:T(8,128)(2,1)} %copy-done, bf16[1024,512]{1,0:T(8,128)(2,1)S(1)} %pad_maximum_fusion.4.g_ref), custom_call_target="tpu_custom_call" | custom-call | flops 5637144576 | bytes 8650752 | tf_op jit(solution)/shard_map/attention_backward/pallas_call | solution.py:311
  649.6 11.0 %fusion.72 = (f32[1600]{0:T(1024)S(1)}, f32[1600]{0:T(1024)S(1)}, bf16[1024,1600]{0,1:T(8,128)(2,1)S(1)}, f32[1024,1600]{0,1:T(8,128)}) fusion(f32[1024]{0:T(1024)S(1)} %add_rsqrt_fusion, f32[1024]{0:T(1024)S(1)} %broadcast_multiply_fusion, bf16[256,1600]{0,1:T(8,128)(2,1)S(1)} %copy-done.23, bf16[256,1600]{0,1:T(8,128)(2,1)S(1)} %copy-done.21, ...), kind=kOutput, calls=%fused_computation.283 | convolution fusion | flops 4636668928 | bytes 20517376 | tf_op jit(solution)/shard_map/dot_general | solution.py:358
  663.5 7.6 fusion.68
  689.1 15.1 %collective-permute-done.61 = bf16[256,1600]{0,1:T(8,128)(2,1)S(1)} collective-permute-done((bf16[256,1600]{0,1:T(8,128)(2,1)S(1)}, bf16[256,1600]{0,1:T(8,128)(2,1)S(1)}, u32[]{:S(2)}, u32[]{:S(2)}) %collective-permute-start.61) | collective-permute-done | bytes 819232 | tf_op jit(solution)/shard_map/ppermute | solution.py:18
  708.6 9.2 %collective-permute-done.75 = bf16[2,200,1600]{2,1,0:T(8,128)(2,1)S(1)} collective-permute-done((bf16[2,200,1600]{2,1,0:T(8,128)(2,1)S(1)}, bf16[2,200,1600]{2,1,0:T(8,128)(2,1)S(1)}, u32[]{:S(2)}, u32[]{:S(2)}) %collective-permute-start.75) | collective-permute-done | bytes 1280032 | tf_op jit(solution)/shard_map/ppermute | solution.py:18
  719.9 39.9 %collective-permute-done.82 = bf16[2,200,1600]{2,1,0:T(8,128)(2,1)S(1)} collective-permute-done((bf16[2,200,1600]{2,1,0:T(8,128)(2,1)S(1)}, bf16[2,200,1600]{2,1,0:T(8,128)(2,1)S(1)}, u32[]{:S(2)}, u32[]{:S(2)}) %collective-permute-start.82) | collective-permute-done | bytes 1280032 | tf_op jit(solution)/shard_map/ppermute | solution.py:18
  823.5 7.5 collective-permute-done.72
  832.2 21.0 %collective-permute-done.64 = bf16[200,1408]{1,0:T(8,128)(2,1)S(1)} collective-permute-done((bf16[200,1408]{1,0:T(8,128)(2,1)S(1)}, bf16[200,1408]{1,0:T(8,128)(2,1)S(1)}, u32[]{:S(2)}, u32[]{:S(2)}) %collective-permute-start.64) | collective-permute-done | bytes 563232 | tf_op jit(solution)/shard_map/ppermute | solution.py:18
  (513 shorter events, 367.0 us)
Async XLA Ops:
  7.2 800.0 %all-reduce.8.cloned.1.call-start = ((), (), s32[]{:S(2)}) async-start(), calls=%async_computation | async-start | bytes 155648 | tf_op jit(solution)/shard_map/psum | solution.py:465
  7.2 132.6 %collective-permute-start.16 = (bf16[80000]{0:T(1024)(128)(2,1)}, bf16[80000]{0:T(1024)(128)(2,1)}, u32[]{:S(2)}, u32[]{:S(2)}) collective-permute-start(bf16[80000]{0:T(1024)(128)(2,1)} %param.13), channel_id=1, source_target_pairs={{0,4},{4,0},{8,12},{12,8},{16,20},{20,16},{24,28},{28,24},{1,5},{5... | collective-permute-start | bytes 480008 | tf_op jit(solution)/shard_map/ppermute | solution.py:18
  10.2 141.4 %collective-permute-start.17 = (bf16[80000]{0:T(1024)(128)(2,1)}, bf16[80000]{0:T(1024)(128)(2,1)}, u32[]{:S(2)}, u32[]{:S(2)}) collective-permute-start(bf16[80000]{0:T(1024)(128)(2,1)} %param.13), channel_id=1, source_target_pairs={{0,8},{4,12},{8,0},{12,4},{16,24},{20,28},{24,16},{28,20},{1,9},{5... | collective-permute-start | bytes 480008 | tf_op jit(solution)/shard_map/ppermute | solution.py:18
  17.2 116.0 %collective-permute-start.4 = (bf16[50,1408]{1,0:T(8,128)(2,1)}, bf16[50,1408]{1,0:T(8,128)(2,1)}, u32[]{:S(2)}, u32[]{:S(2)}) collective-permute-start(bf16[50,1408]{1,0:T(8,128)(2,1)} %get-tuple-element.106), channel_id=1, source_target_pairs={{0,2},{1,3},{2,0},{3,1},{4,6},{5,7},{6,4},{7,5},{8,10},{9,11},{10,... | collective-permute-start | bytes 422408 | tf_op jit(solution)/shard_map/ppermute | solution.py:18
  18.7 117.5 %collective-permute-start.3 = (bf16[50,1408]{1,0:T(8,128)(2,1)}, bf16[50,1408]{1,0:T(8,128)(2,1)}, u32[]{:S(2)}, u32[]{:S(2)}) collective-permute-start(bf16[50,1408]{1,0:T(8,128)(2,1)} %get-tuple-element.107), channel_id=1, source_target_pairs={{0,3},{1,2},{2,1},{3,0},{4,7},{5,6},{6,5},{7,4},{8,11},{9,10},{10,... | collective-permute-start | bytes 422408 | tf_op jit(solution)/shard_map/ppermute | solution.py:18
  19.5 97.0 %collective-permute-start.29 = (bf16[6400]{0:T(1024)(128)(2,1)S(1)}, bf16[6400]{0:T(1024)(128)(2,1)S(1)}, u32[]{:S(2)}, u32[]{:S(2)}) collective-permute-start(bf16[6400]{0:T(1024)(128)(2,1)S(1)} %get-tuple-element.99), channel_id=1, source_target_pairs={{0,1},{1,2},{2,3},{3,4},{4,5},{5,6},{6,7},{7,8},{8,9},{9,10},{10,1... | collective-permute-start | bytes 38408 | tf_op jit(solution)/shard_map/ppermute | solution.py:395
  151.7 71.3 %collective-permute-start.40 = (bf16[200,1600]{1,0:T(8,128)(2,1)}, bf16[200,1600]{1,0:T(8,128)(2,1)}, u32[]{:S(2)}, u32[]{:S(2)}) collective-permute-start(bf16[200,1600]{1,0:T(8,128)(2,1)} %reshape.435), channel_id=1, source_target_pairs={{0,4},{4,0},{8,12},{12,8},{16,20},{20,16},{24,28},{28,24},{1,5},{5... | collective-permute-start | bytes 1920008 | tf_op jit(solution)/shard_map/ppermute | solution.py:18
  160.8 64.5 %collective-permute-start.41 = (bf16[200,1600]{1,0:T(8,128)(2,1)}, bf16[200,1600]{1,0:T(8,128)(2,1)}, u32[]{:S(2)}, u32[]{:S(2)}) collective-permute-start(bf16[200,1600]{1,0:T(8,128)(2,1)} %reshape.435), channel_id=1, source_target_pairs={{0,8},{4,12},{8,0},{12,4},{16,24},{20,28},{24,16},{28,20},{1,9},{5... | collective-permute-start | bytes 1920008 | tf_op jit(solution)/shard_map/ppermute | solution.py:18
  162.3 39.0 %collective-permute-start.20 = (bf16[80000]{0:T(1024)(128)(2,1)}, bf16[80000]{0:T(1024)(128)(2,1)}, u32[]{:S(2)}, u32[]{:S(2)}) collective-permute-start(bf16[80000]{0:T(1024)(128)(2,1)} %collective-permute-done.19), channel_id=1, source_target_pairs={{0,4},{4,0},{8,12},{12,8},{16,20},{20,16},{24,28},{28,24},{1,5},{5... | collective-permute-start | bytes 480008 | tf_op jit(solution)/shard_map/ppermute | solution.py:18
  185.5 123.8 %collective-permute-start.1 = (bf16[256,1600]{0,1:T(8,128)(2,1)S(1)}, bf16[256,1600]{0,1:T(8,128)(2,1)S(1)}, u32[]{:S(2)}, u32[]{:S(2)}) collective-permute-start(bf16[256,1600]{0,1:T(8,128)(2,1)S(1)} %bitcast.166), channel_id=1, source_target_pairs={{0,2},{1,3},{2,0},{3,1},{4,6},{5,7},{6,4},{7,5},{8,10},{9,11},{10,... | collective-permute-start | bytes 2457608 | tf_op jit(solution)/shard_map/ppermute | solution.py:18
  201.3 130.8 %collective-permute-start = (bf16[256,1600]{0,1:T(8,128)(2,1)S(1)}, bf16[256,1600]{0,1:T(8,128)(2,1)}, u32[]{:S(2)}, u32[]{:S(2)}) collective-permute-start(bf16[256,1600]{0,1:T(8,128)(2,1)S(1)} %bitcast.167), channel_id=1, source_target_pairs={{0,1},{1,0},{2,3},{3,2},{4,5},{5,4},{6,7},{7,6},{8,9},{9,8},{10,11... | collective-permute-start | bytes 2457608 | tf_op jit(solution)/shard_map/ppermute | solution.py:18
  253.3 38.6 %collective-permute-start.43 = (bf16[200,1600]{1,0:T(8,128)(2,1)S(1)}, bf16[200,1600]{1,0:T(8,128)(2,1)S(1)}, u32[]{:S(2)}, u32[]{:S(2)}) collective-permute-start(bf16[200,1600]{1,0:T(8,128)(2,1)S(1)} %copy-done.27), channel_id=1, source_target_pairs={{0,16},{4,20},{8,24},{12,28},{16,0},{20,4},{24,8},{28,12},{1,17},{... | collective-permute-start | bytes 1920008 | tf_op jit(solution)/shard_map/ppermute | solution.py:18
  291.9 116.2 %collective-permute-start.51 = (bf16[256,1600]{0,1:T(8,128)(2,1)}, bf16[256,1600]{0,1:T(8,128)(2,1)}, u32[]{:S(2)}, u32[]{:S(2)}) collective-permute-start(bf16[256,1600]{0,1:T(8,128)(2,1)} %get-tuple-element.35), channel_id=1, source_target_pairs={{0,2},{1,3},{2,0},{3,1},{4,6},{5,7},{6,4},{7,5},{8,10},{9,11},{10,... | collective-permute-start | bytes 2457608 | tf_op jit(solution)/shard_map/ppermute | solution.py:18
  309.3 80.6 %collective-permute-start.36 = (bf16[200,1600]{1,0:T(8,128)(2,1)S(1)}, bf16[200,1600]{1,0:T(8,128)(2,1)}, u32[]{:S(2)}, u32[]{:S(2)}) collective-permute-start(bf16[200,1600]{1,0:T(8,128)(2,1)S(1)} %copy-done.29), channel_id=1, source_target_pairs={{0,16},{4,20},{8,24},{12,28},{16,0},{20,4},{24,8},{28,12},{1,17},{... | collective-permute-start | bytes 1920008 | tf_op jit(solution)/shard_map/ppermute | solution.py:18
  332.1 84.1 %collective-permute-start.25 = (bf16[8,80000]{1,0:T(8,128)(2,1)S(1)}, bf16[8,80000]{1,0:T(8,128)(2,1)}, u32[]{:S(2)}, u32[]{:S(2)}) collective-permute-start(bf16[8,80000]{1,0:T(8,128)(2,1)S(1)} %dynamic_update_slice.114), channel_id=1, source_target_pairs={{0,1},{1,0},{2,3},{3,2},{4,5},{5,4},{6,7},{7,6},{8,9},{9,8},{10,11... | collective-permute-start | bytes 3840008 | tf_op jit(solution)/shard_map/ppermute | solution.py:18
  358.7 57.7 %collective-permute-start.24 = (bf16[8,80000]{1,0:T(8,128)(2,1)}, bf16[8,80000]{1,0:T(8,128)(2,1)}, u32[]{:S(2)}, u32[]{:S(2)}) collective-permute-start(bf16[8,80000]{1,0:T(8,128)(2,1)} %collective-permute-done.23), channel_id=1, source_target_pairs={{0,1},{1,0},{2,3},{3,2},{4,5},{5,4},{6,7},{7,6},{8,9},{9,8},{10,11... | collective-permute-start | bytes 3840008 | tf_op jit(solution)/shard_map/ppermute | solution.py:18
  406.2 83.3 %collective-permute-start.50 = (bf16[256,1600]{0,1:T(8,128)(2,1)}, bf16[256,1600]{0,1:T(8,128)(2,1)}, u32[]{:S(2)}, u32[]{:S(2)}) collective-permute-start(bf16[256,1600]{0,1:T(8,128)(2,1)} %get-tuple-element.35), channel_id=1, source_target_pairs={{0,1},{1,0},{2,3},{3,2},{4,5},{5,4},{6,7},{7,6},{8,9},{9,8},{10,11... | collective-permute-start | bytes 2457608 | tf_op jit(solution)/shard_map/ppermute | solution.py:18
  408.1 34.9 %collective-permute-start.37 = (bf16[200,1600]{1,0:T(8,128)(2,1)}, bf16[200,1600]{1,0:T(8,128)(2,1)}, u32[]{:S(2)}, u32[]{:S(2)}) collective-permute-start(bf16[200,1600]{1,0:T(8,128)(2,1)} %collective-permute-done.36), channel_id=1, source_target_pairs={{0,4},{4,0},{8,12},{12,8},{16,20},{20,16},{24,28},{28,24},{1,5},{5... | collective-permute-start | bytes 1920008 | tf_op jit(solution)/shard_map/ppermute | solution.py:18
  416.0 73.5 %collective-permute-start.52 = (bf16[256,1600]{0,1:T(8,128)(2,1)}, bf16[256,1600]{0,1:T(8,128)(2,1)}, u32[]{:S(2)}, u32[]{:S(2)}) collective-permute-start(bf16[256,1600]{0,1:T(8,128)(2,1)} %collective-permute-done.51), channel_id=1, source_target_pairs={{0,1},{1,0},{2,3},{3,2},{4,5},{5,4},{6,7},{7,6},{8,9},{9,8},{10,11... | collective-permute-start | bytes 2457608 | tf_op jit(solution)/shard_map/ppermute | solution.py:18
  416.5 48.5 %collective-permute-start.39 = (bf16[200,1600]{1,0:T(8,128)(2,1)}, bf16[200,1600]{1,0:T(8,128)(2,1)}, u32[]{:S(2)}, u32[]{:S(2)}) collective-permute-start(bf16[200,1600]{1,0:T(8,128)(2,1)} %collective-permute-done.38), channel_id=1, source_target_pairs={{0,4},{4,0},{8,12},{12,8},{16,20},{20,16},{24,28},{28,24},{1,5},{5... | collective-permute-start | bytes 1920008 | tf_op jit(solution)/shard_map/ppermute | solution.py:18
  514.9 40.2 %collective-permute-start.53 = (bf16[256,1600]{0,1:T(8,128)(2,1)}, bf16[256,1600]{0,1:T(8,128)(2,1)}, u32[]{:S(2)}, u32[]{:S(2)}) collective-permute-start(bf16[256,1600]{0,1:T(8,128)(2,1)} %get-tuple-element.63), channel_id=1, source_target_pairs={{0,1},{1,0},{2,3},{3,2},{4,5},{5,4},{6,7},{7,6},{8,9},{9,8},{10,11... | collective-permute-start | bytes 2457608 | tf_op jit(solution)/shard_map/ppermute | solution.py:18
  516.4 54.4 %collective-permute-start.47 = (bf16[256,1600]{0,1:T(8,128)(2,1)S(1)}, bf16[256,1600]{0,1:T(8,128)(2,1)}, u32[]{:S(2)}, u32[]{:S(2)}) collective-permute-start(bf16[256,1600]{0,1:T(8,128)(2,1)S(1)} %get-tuple-element.65), channel_id=1, source_target_pairs={{0,1},{1,0},{2,3},{3,2},{4,5},{5,4},{6,7},{7,6},{8,9},{9,8},{10,11... | collective-permute-start | bytes 2457608 | tf_op jit(solution)/shard_map/ppermute | solution.py:18
  528.4 143.0 %collective-permute-start.74 = (bf16[2,2,200,1600]{3,2,0,1:T(8,128)(2,1)}, bf16[2,2,200,1600]{3,2,0,1:T(8,128)(2,1)}, u32[]{:S(2)}, u32[]{:S(2)}) collective-permute-start(bf16[2,2,200,1600]{3,2,0,1:T(8,128)(2,1)} %fusion.17), channel_id=1, source_target_pairs={{0,4},{4,0},{8,12},{12,8},{16,20},{20,16},{24,28},{28,24},{1,5},{5... | collective-permute-start | bytes 7680008 | tf_op jit(solution)/shard_map/ppermute | solution.py:18
  555.1 121.2 %collective-permute-start.81 = (bf16[2,2,200,1600]{3,2,1,0:T(8,128)(2,1)}, bf16[2,2,200,1600]{3,2,1,0:T(8,128)(2,1)}, u32[]{:S(2)}, u32[]{:S(2)}) collective-permute-start(bf16[2,2,200,1600]{3,2,1,0:T(8,128)(2,1)} %fusion.16), channel_id=1, source_target_pairs={{0,4},{4,0},{8,12},{12,8},{16,20},{20,16},{24,28},{28,24},{1,5},{5... | collective-permute-start | bytes 7680008 | tf_op jit(solution)/shard_map/ppermute | solution.py:18
  620.8 64.3 %collective-permute-start.69 = (bf16[8,50,1600]{2,0,1:T(8,128)(2,1)}, bf16[8,50,1600]{2,0,1:T(8,128)(2,1)}, u32[]{:S(2)}, u32[]{:S(2)}) collective-permute-start(bf16[8,50,1600]{2,0,1:T(8,128)(2,1)} %copy.95), channel_id=1, source_target_pairs={{0,1},{1,0},{2,3},{3,2},{4,5},{5,4},{6,7},{7,6},{8,9},{9,8},{10,11... | collective-permute-start | bytes 3840008 | tf_op jit(solution)/shard_map/ppermute | solution.py:18
  621.0 146.6 %collective-permute-start.68 = (bf16[8,50,1600]{2,0,1:T(8,128)(2,1)}, bf16[8,50,1600]{2,0,1:T(8,128)(2,1)}, u32[]{:S(2)}, u32[]{:S(2)}) collective-permute-start(bf16[8,50,1600]{2,0,1:T(8,128)(2,1)} %copy.93), channel_id=1, source_target_pairs={{0,1},{1,0},{2,3},{3,2},{4,5},{5,4},{6,7},{7,6},{8,9},{9,8},{10,11... | collective-permute-start | bytes 3840008 | tf_op jit(solution)/shard_map/ppermute | solution.py:18
  676.4 85.4 %collective-permute-start.62 = (bf16[2,2,200,1408]{3,2,0,1:T(8,128)(2,1)S(1)}, bf16[2,2,200,1408]{3,2,0,1:T(8,128)(2,1)S(1)}, u32[]{:S(2)}, u32[]{:S(2)}) collective-permute-start(bf16[2,2,200,1408]{3,2,0,1:T(8,128)(2,1)S(1)} %fusion.20), channel_id=1, source_target_pairs={{0,4},{4,0},{8,12},{12,8},{16,20},{20,16},{24,28},{28,24},{1,5},{5... | collective-permute-start | bytes 6758408 | tf_op jit(solution)/shard_map/ppermute | solution.py:18
  687.1 72.7 %collective-permute-start.82 = (bf16[2,200,1600]{2,1,0:T(8,128)(2,1)S(1)}, bf16[2,200,1600]{2,1,0:T(8,128)(2,1)S(1)}, u32[]{:S(2)}, u32[]{:S(2)}) collective-permute-start(bf16[2,200,1600]{2,1,0:T(8,128)(2,1)S(1)} %fusion.44), channel_id=1, source_target_pairs={{0,8},{4,12},{8,0},{12,4},{16,24},{20,28},{24,16},{28,20},{1,9},{5... | collective-permute-start | bytes 3840008 | tf_op jit(solution)/shard_map/ppermute | solution.py:18
  704.2 63.4 %collective-permute-start.70 = (bf16[8,50,1600]{2,0,1:T(8,128)(2,1)S(1)}, bf16[8,50,1600]{2,0,1:T(8,128)(2,1)S(1)}, u32[]{:S(2)}, u32[]{:S(2)}) collective-permute-start(bf16[8,50,1600]{2,0,1:T(8,128)(2,1)S(1)} %fusion.18), channel_id=1, source_target_pairs={{0,2},{1,3},{2,0},{3,1},{4,6},{5,7},{6,4},{7,5},{8,10},{9,11},{10,... | collective-permute-start | bytes 3840008 | tf_op jit(solution)/shard_map/ppermute | solution.py:18
  719.2 58.0 %collective-permute-start.76 = (bf16[200,1600]{1,0:T(8,128)(2,1)}, bf16[200,1600]{1,0:T(8,128)(2,1)S(1)}, u32[]{:S(2)}, u32[]{:S(2)}) collective-permute-start(bf16[200,1600]{1,0:T(8,128)(2,1)} %fusion.53), channel_id=1, source_target_pairs={{0,16},{4,20},{8,24},{12,28},{16,0},{20,4},{24,8},{28,12},{1,17},{... | collective-permute-start | bytes 1920008 | tf_op jit(solution)/shard_map/ppermute | solution.py:18
  761.0 36.8 %collective-permute-start.83 = (bf16[200,1600]{1,0:T(8,128)(2,1)}, bf16[200,1600]{1,0:T(8,128)(2,1)}, u32[]{:S(2)}, u32[]{:S(2)}) collective-permute-start(bf16[200,1600]{1,0:T(8,128)(2,1)} %fusion.54), channel_id=1, source_target_pairs={{0,16},{4,20},{8,24},{12,28},{16,0},{20,4},{24,8},{28,12},{1,17},{... | collective-permute-start | bytes 1920008 | tf_op jit(solution)/shard_map/ppermute | solution.py:18
  765.5 54.8 %collective-permute-start.63 = (bf16[2,200,1408]{2,1,0:T(8,128)(2,1)}, bf16[2,200,1408]{2,1,0:T(8,128)(2,1)}, u32[]{:S(2)}, u32[]{:S(2)}) collective-permute-start(bf16[2,200,1408]{2,1,0:T(8,128)(2,1)} %fusion.47), channel_id=1, source_target_pairs={{0,8},{4,12},{8,0},{12,4},{16,24},{20,28},{24,16},{28,20},{1,9},{5... | collective-permute-start | bytes 3379208 | tf_op jit(solution)/shard_map/ppermute | solution.py:18
  (103 other events, 2522.6 us)
Sparse Core Ops, SparseCore 0:
  663.6 142.6 all-reduce.7

commit v2 on v1

--- a/solution.py
+++ b/solution.py
@@ -14,55 +14,13 @@
 F32 = jnp.float32
 
 
-def swap(value, axis, size, bit):
-    return lax.ppermute(value, axis, [(i, i ^ bit) for i in range(size)])
-
-
 def bits_of(size):
     return [1 << k for k in reversed(range(size.bit_length() - 1))]
 
 
-def gather_relative(value, axis, size):
-    pieces = {0: value}
-    for bit in bits_of(size):
-        for j in list(pieces):
-            pieces[j ^ bit] = swap(pieces[j], axis, size, bit)
-    return [pieces[j] for j in range(size)]
-
-
-def gather_dp(value, size):
-    if size > 8:
-        return lax.all_gather(value, "dp", axis=0, tiled=False)
-    mine = lax.axis_index("dp")
-    out = jnp.zeros((size, *value.shape), value.dtype)
-    for j, piece in enumerate(gather_relative(value, "dp", size)):
-        out = lax.dynamic_update_index_in_dim(out, piece, mine ^ j, 0)
-    return out
-
-
-def scatter_dp(value, size):
-    if size > 8:
-        return lax.psum_scatter(value.astype(BF), "dp", scatter_dimension=0, tiled=False).astype(F32)
-    mine = lax.axis_index("dp")
-    bits = bits_of(size)
-    value = value.reshape((2,) * len(bits) + value.shape[1:])
-    for axis in reversed(range(len(bits))):
-        bit = bits[axis]
-        side = (mine // bit) % 2
-        sent = lax.dynamic_index_in_dim(value, 1 - side, axis, keepdims=False).astype(BF)
-        kept = lax.dynamic_index_in_dim(value, side, axis, keepdims=False)
-        value = kept.astype(F32) + swap(sent, "dp", size, bit).astype(F32)
-    return value
-
-
-def scatter_seq(blocks, size):
-    blocks = dict(enumerate(blocks))
-    for bit in reversed(bits_of(size)):
-        for j in sorted(blocks, reverse=True):
-            if j & bit:
-                got = swap(blocks.pop(j).astype(BF), "seq", size, bit)
-                blocks[j ^ bit] = blocks[j ^ bit].astype(F32) + got.astype(F32)
-    return blocks[0]
+def after(value, *others):
+    others = [o for o in others if o is not None]
+    return lax.optimization_barrier((value, *others))[0] if others else value
 
 
 def pick(pieces, index):
@@ -72,13 +30,105 @@
     return out
 
 
-def exchange_seq(pieces, size):
-    mine = lax.axis_index("seq")
-    got = []
-    for j in range(size):
-        sent = pick([pieces[b ^ j] for b in range(size)], mine)
-        got.append(sent if j == 0 else swap(sent, "seq", size, j))
-    return [pick([got[b ^ m] for m in range(size)], mine) for b in range(size)]
+class Links:
+    def __init__(self, dps, seqs):
+        self.sizes = {"dp": dps, "seq": seqs}
+        self.last = {}
+
+    def ordered(self, value, link, permute):
+        self.last[link] = permute(after(value, self.last.get(link)))
+        return self.last[link]
+
+    def swap(self, value, axis, bits):
+        pairs = [(i, i ^ bits) for i in range(self.sizes[axis])]
+        top = 1 << (bits.bit_length() - 1)
+        return self.ordered(value, (axis, top), lambda v: lax.ppermute(v, axis, pairs))
+
+    def shift(self, value, step):
+        count = self.sizes["dp"] * self.sizes["seq"]
+        pairs = [(i, i + step) for i in range(count) if 0 <= i + step < count]
+        return self.ordered(value, ("seq", 1), lambda v: lax.ppermute(v, ("dp", "seq"), pairs))
+
+    def all_sum(self, value, axes):
+        for axis in axes:
+            for bit in bits_of(self.sizes[axis]):
+                value = value + self.swap(value, axis, bit)
+        return value
+
+    def gather_seq(self, value):
+        pieces = {0: value}
+        for bit in bits_of(self.sizes["seq"]):
+            for j in list(pieces):
+                pieces[j ^ bit] = self.swap(pieces[j], "seq", bit)
+        return [pieces[j] for j in range(len(pieces))]
+
+    def scatter_seq(self, blocks):
+        blocks = dict(enumerate(blocks))
+        for bit in reversed(bits_of(self.sizes["seq"])):
+            for j in sorted(blocks, reverse=True):
+                if j & bit:
+                    got = self.swap(blocks.pop(j).astype(BF), "seq", bit)
+                    blocks[j ^ bit] = blocks[j ^ bit].astype(F32) + got.astype(F32)
+        return blocks[0]
+
+    def exchange_seq(self, pieces):
+        return [pieces[0]] + [self.swap(pieces[j], "seq", j) for j in range(1, len(pieces))]
+
+    def relative(self, pieces, axis="seq"):
+        mine, size = lax.axis_index(axis), len(pieces)
+        return [pick([pieces[j ^ m] for m in range(size)], mine) for j in range(size)]
+
+    def columns_from_rows(self, flat, rows, pack):
+        size = self.sizes["seq"]
+        cols = flat.shape[0] * size // rows
+        if rows % size == 0:
+            pieces = self.relative(pack(flat.reshape(rows // size, cols)))
+            return jnp.concatenate(self.relative(self.exchange_seq(pieces)), axis=0)
+        full = lax.all_gather(flat, "seq", axis=0, tiled=True).reshape(rows, cols)
+        return pick(pack(full), lax.axis_index("seq"))
+
+    def rows_from_columns(self, value, unpack):
+        size = self.sizes["seq"]
+        rows = value.shape[0]
+        value = value.astype(BF)
+        if rows % size == 0:
+            part = rows // size
+            pieces = self.relative([value[b * part : (b + 1) * part] for b in range(size)])
+            return unpack(self.relative(self.exchange_seq(pieces))).reshape(-1)
+        full = lax.all_gather(value, "seq", axis=0, tiled=False)
+        full = unpack([full[b] for b in range(size)]).reshape(-1)
+        count = full.shape[0] // size
+        return lax.dynamic_slice_in_dim(full, lax.axis_index("seq") * count, count)
+
+
+def block(value, j):
+    return lax.dynamic_index_in_dim(value, lax.axis_index("dp") ^ j, 0, keepdims=False)
+
+
+class Ring:
+    def __init__(self, size):
+        self.size = size
+        self.order = [*range(0, size, 2), *range(size - 1, 0, -2)] if size == 8 else list(range(size))
+        self.groups = [self.order] if size == 8 else None
+
+    def gather(self, value):
+        return lax.all_gather(value, "dp", axis=0, tiled=True, axis_index_groups=self.groups)
+
+    def scatter(self, value):
+        total = lax.psum_scatter(value, "dp", scatter_dimension=0, tiled=True, axis_index_groups=self.groups)
+        return lax.optimization_barrier(total).astype(F32)
+
+    def inward(self, value):
+        return self.blocks(value, self.order)
+
+    def outward(self, value):
+        return self.blocks(value, [self.order.index(d) for d in range(self.size)])
+
+    def blocks(self, value, order):
+        if self.groups is None:
+            return value
+        part = value.shape[-1] // self.size
+        return jnp.concatenate([value[..., d * part : (d + 1) * part] for d in order], axis=-1)
 
 
 def pack_heads(value, size):
@@ -112,36 +162,17 @@
     return jnp.concatenate(out, axis=2)[:, :, :width].reshape(rows, 3 * width)
 
 
-def pack_hidden(value, size, dps):
+def pack_hidden(value, size, order):
     rows, hidden = value.shape
-    value = value.reshape(rows, dps, size, hidden // (dps * size))
-    return [value[:, :, s].reshape(rows, hidden // size) for s in range(size)]
-
-
-def unpack_hidden(pieces, dps):
+    value = value.reshape(rows, len(order), size, hidden // (len(order) * size))
+    return [jnp.concatenate([value[:, d, s] for d in order], axis=1) for s in range(size)]
+
+
+def unpack_hidden(pieces, order):
     rows, own = pieces[0].shape
-    parts = [piece.reshape(rows, dps, 1, own // dps) for piece in pieces]
-    return jnp.concatenate(parts, axis=2).reshape(rows, own * len(pieces))
-
-
-def columns_from_rows(flat, rows, pack, size):
-    cols = flat.shape[0] * size // rows
-    if rows % size == 0:
-        return jnp.concatenate(exchange_seq(pack(flat.reshape(rows // size, cols)), size), axis=0)
-    full = lax.all_gather(flat, "seq", axis=0, tiled=True).reshape(rows, cols)
-    return pick(pack(full), lax.axis_index("seq"))
-
-
-def rows_from_columns(value, unpack, size):
-    rows = value.shape[0]
-    value = value.astype(BF)
-    if rows % size == 0:
-        part = rows // size
-        return unpack(exchange_seq([value[b * part : (b + 1) * part] for b in range(size)], size)).reshape(-1)
-    full = lax.all_gather(value, "seq", axis=0, tiled=False)
-    full = unpack([full[b] for b in range(size)]).reshape(-1)
-    count = full.shape[0] // size
-    return lax.dynamic_slice_in_dim(full, lax.axis_index("seq") * count, count)
+    part = own // len(order)
+    cut = lambda piece, k: piece[:, k * part : (k + 1) * part]
+    return jnp.concatenate([cut(piece, order.index(d)) for d in range(len(order)) for piece in pieces], axis=1)
 
 
 def half_masks():
@@ -371,112 +402,139 @@
     info = jnp.stack([rank.astype(jnp.int32), length])
     unit_rows = width // dps
 
-    vectors = lax.all_gather(jnp.stack([attention_vectors, block_vectors]), ("dp", "seq"), axis=1, tiled=True)
-    vectors = vectors.astype(F32).reshape(8, width)
-    gain1, shift1, bias_q, bias_v, bias_o, gain2, shift2, bias_p = (vectors[k] for k in range(8))
-
-    x_own = tokens[0]
-    x_all = jnp.concatenate(gather_relative(x_own, "seq", size), axis=0)
-    place = rank * count + jnp.arange(count)
-    dy_own = cotangent[0] * (place < length).astype(BF)[:, None]
+    links = Links(dps, size)
 
     pack3 = lambda m: pack_heads(m.reshape(m.shape[0], 3, width), size)
-    qkv_part = columns_from_rows(w_qkv, unit_rows, pack3, size)
-    qkv_full = gather_dp(qkv_part, dps).reshape(width, -1)
-
-    out_parts = gather_dp(w_out, dps)
-    out_parts = gather_relative(out_parts, "seq", size)
-    out_full = jnp.stack([pick([out_parts[b ^ m] for m in range(size)], rank) for b in range(size)], axis=1)
-    out_full = out_full.reshape(width, width)
+    ring = Ring(dps)
+    pack_fc = lambda m: pack_hidden(m, size, ring.order)
+    unpack_fc = lambda p: unpack_hidden(p, ring.order)
+
+    split = lambda m: [m[j * count : (j + 1) * count] for j in range(size)]
+
+    aligned = unit_rows % 8 == 0 and unit_rows % size == 0
+    rows = unit_rows // size
+    if aligned:
+        starts = [rows * b // 8 * 8 for b in range(size)]
+        window = max(-(-(rows * (b + 1) - starts[b]) // 8) * 8 for b in range(size))
+        starts = [min(start, unit_rows - window) for start in starts]
+        starts = [pl.multiple_of(v, 8) for v in links.relative([jnp.int32(v) for v in starts])]
+        pieces = jnp.concatenate(links.relative(links.gather_seq(ring.inward(w_out.reshape(rows, width)))), axis=0)
+        out_part = ring.gather(lax.dynamic_slice_in_dim(pieces, starts[0], window, 0)).reshape(dps, window, width)
+    else:
+        out_part = lax.all_gather(w_out, "dp", axis=0, tiled=False)
+    qkv_part = links.columns_from_rows(w_qkv, unit_rows, pack3)
+    qkv_full = ring.gather(qkv_part)
 
     shift = hidden // devices
     tail = -(-shift * devices // LANES) * LANES
+    before = links.shift(w_fc[-tail:], 1)
+    part = attention_vectors.shape[0]
+    last = device == devices - 1
+    small = jnp.zeros((8 * width,), BF)
+    small = lax.dynamic_update_slice_in_dim(small, attention_vectors, device * part, 0)
+    small = lax.dynamic_update_slice_in_dim(small, block_vectors, 4 * width + device * part, 0)
+    small = jnp.concatenate([small, jnp.where(last, w_fc[-hidden:], jnp.zeros((), BF))])
+    small = links.all_sum(small, ("seq", "dp")).astype(F32)
+    gain1, shift1, bias_q, bias_v, bias_o, gain2, shift2, bias_p = (small[k * width : (k + 1) * width] for k in range(8))
+    gain1, shift1, bias_o, gain2, shift2, bias_p = (ring.inward(v) for v in (gain1, shift1, bias_o, gain2, shift2, bias_p))
+    bias_fc = pick(pack_fc(small[None, 8 * width :]), rank)
+    bias_qkv = pick(pack3(jnp.stack([bias_q, jnp.zeros_like(bias_q), bias_v])[None]), rank)
+
+    x_own = ring.inward(tokens[0])
+    x_all = jnp.concatenate(links.gather_seq(x_own), axis=0)
     plain = w_fc.shape[0] - shift
-    before = lax.ppermute(w_fc[-tail:], ("dp", "seq"), [(i, i + 1) for i in range(devices - 1)])
-    fc_flat = lax.dynamic_slice_in_dim(jnp.concatenate([before, w_fc]), tail - shift * device, plain)
-    bias_rows = lax.psum(jnp.where(device == devices - 1, w_fc[-hidden:], jnp.zeros((), BF)).astype(F32), ("dp", "seq"))
-    pack_fc = lambda m: pack_hidden(m, size, dps)
-    fc_part = columns_from_rows(fc_flat, unit_rows, pack_fc, size)
-    fc_full = gather_dp(fc_part, dps).reshape(width, -1)
-    bias_fc = pick(pack_fc(bias_rows[None]), rank)
-
-    proj_full = gather_dp(w_proj.reshape(-1, width), dps).reshape(-1, width)
+    fc_flat = lax.dynamic_slice_in_dim(jnp.concatenate([before, after(w_fc, small)]), tail - shift * device, plain)
+    fc_part = links.columns_from_rows(fc_flat, unit_rows, pack_fc)
+    fc_full = ring.gather(fc_part)
+
+    out_parts = links.gather_seq(out_part)
 
     unit1_all, _ = normal(x_all.astype(F32))
     h1 = (unit1_all * gain1 + shift1).astype(BF)
-    bias_qkv = pick(pack3(jnp.stack([bias_q, jnp.zeros_like(bias_q), bias_v])[None]), rank)
     mixed = (dot(h1, qkv_full) + bias_qkv).astype(BF)
+    proj_full = ring.gather(after(ring.inward(w_proj.reshape(-1, width)), fc_part, mixed))
+    place = rank * count + jnp.arange(count)
+    dy_own = ring.inward(cotangent[0]) * (place < length).astype(BF)[:, None]
+    dy_wide = dy_own.astype(F32)
+    dy = jnp.concatenate(links.gather_seq(after(dy_own, mixed)), axis=0)
     o_heads = attention_forward(info, mixed, own, size)
-    o_got = [o_heads[:count]] + [
-        swap(o_heads[j * count : (j + 1) * count], "seq", size, j) for j in range(1, size)
-    ]
-    o_own = jnp.concatenate([pick([o_got[b ^ m] for m in range(size)], rank)[:, : own * HD] for b in range(size)], axis=1)
-    o_own = o_own[:, :width]
+    out_parts = [after(piece, mixed) for piece in out_parts]
+    if aligned:
+        out_full = jnp.zeros((dps, unit_rows, width), BF)
+        for j in range(size):
+            out_full = lax.dynamic_update_slice_in_dim(out_full, out_parts[j], starts[j], 1)
+    else:
+        out_full = jnp.stack(links.relative(out_parts), axis=1)
+    out_full = out_full.reshape(width, width)
+
+    o_got = links.relative(links.exchange_seq(split(o_heads)))
+    o_own = jnp.concatenate([piece[:, : own * HD] for piece in o_got], axis=1)
+    o_own = ring.inward(o_own[:, :width])
     x2 = x_own.astype(F32) + dot(o_own, out_full) + bias_o
     unit2, scale2 = normal(x2)
-    h2_own = (unit2 * gain2 + shift2).astype(BF)
-    h2 = jnp.concatenate(gather_relative(h2_own, "seq", size), axis=0)
-    dy = jnp.concatenate(gather_relative(dy_own, "seq", size), axis=0)
+    h2 = jnp.concatenate(links.gather_seq((unit2 * gain2 + shift2).astype(BF)), axis=0)
+
     u = dot(h2, fc_full) + bias_fc
     a = gelu(u).astype(BF)
-    split = lambda m: [m[j * count : (j + 1) * count] for j in range(size)]
-    output = (x2 + scatter_seq(split(dot(a, proj_full)), size) + bias_p).astype(BF)
-
-    dy_wide = dy_own.astype(F32)
-    grad_proj = scatter_dp(dot(a, dy, ((0,), (0,))).reshape(dps, -1, width), dps).reshape(-1)
-    grad_bp = jnp.sum(dy_wide, axis=0)
-    du = (dot(dy, proj_full, ((1,), (1,))) * gelu_slope(u)).astype(BF)
-    grad_bf = jnp.sum(du.astype(F32), axis=0)
-    dh2 = scatter_seq(split(dot(du, fc_full, ((1,), (1,)))), size)
-    grad_fc = scatter_dp(dot(h2, du, ((0,), (0,))).reshape(dps, unit_rows, -1), dps)
-    grad_g2 = jnp.sum(dh2 * unit2, axis=0)
-    grad_c2 = jnp.sum(dh2, axis=0)
+    grad_proj = dot(a, dy, ((0,), (0,))).astype(BF)
+    grad_proj_own = ring.scatter(grad_proj)
+    du = (dot(after(dy, grad_proj), proj_full, ((1,), (1,))) * gelu_slope(u)).astype(BF)
+    dh2_part = dot(du, fc_full, ((1,), (1,)))
+    dh2 = links.scatter_seq(split(dh2_part))
+    grad_fc = dot(h2, after(du, dh2_part), ((0,), (0,))).astype(BF)
+    grad_fc = ring.scatter(after(grad_fc, grad_proj_own))
     dx2 = dy_wide + norm_input_grad(unit2, scale2, gain2, dh2)
     dz = dx2.astype(BF)
-    grad_bo = jnp.sum(dz.astype(F32), axis=0)
-
-    do_own = jnp.pad(dot(dz, out_full, ((1,), (1,))).astype(BF), ((0, 0), (0, own * size * HD - width)))
+
+    do_own = jnp.pad(ring.outward(dot(dz, out_full, ((1,), (1,))).astype(BF)), ((0, 0), (0, own * size * HD - width)))
     do_blocks = [jnp.pad(do_own[:, b * own * HD : (b + 1) * own * HD], ((0, 0), (0, own % 2 * HD))) for b in range(size)]
-    do_got = []
-    for j in range(size):
-        sent = pick([do_blocks[b ^ j] for b in range(size)], rank)
-        do_got.append(sent if j == 0 else swap(sent, "seq", size, j))
-    do_heads = jnp.concatenate(do_got, axis=0)
-    grad_out = dot(o_own, dz, ((0,), (0,)))
-    grad_out = grad_out.reshape((dps, size, -1, width) if width % devices == 0 else (dps, size, -1))
-    grad_out = scatter_seq([lax.dynamic_index_in_dim(grad_out, rank ^ j, 1, keepdims=False) for j in range(size)], size)
-    grad_out = scatter_dp(grad_out, dps).reshape(-1)
+    do_heads = jnp.concatenate(links.exchange_seq(links.relative(do_blocks)), axis=0)
+    grad_out = dot(o_own, after(dz, do_own), ((0,), (0,))).astype(BF)
+    output_part = dot(after(a, do_own), proj_full)
+    if aligned:
+        grad_out = grad_out.reshape(dps, unit_rows, width)
+        blocks = [lax.dynamic_slice_in_dim(grad_out, starts[j], window, 1) for j in range(size)]
+    else:
+        grad_out = grad_out.reshape(dps, size, -1)
+        blocks = [lax.dynamic_index_in_dim(grad_out, rank ^ j, 1, keepdims=False) for j in range(size)]
+    do_heads = after(do_heads, output_part, *blocks, grad_proj_own)
     dmixed = attention_backward(info, mixed, do_heads, own, size)
-    grad_mixed = jnp.sum(dmixed.astype(F32), axis=0)
-    dh1_part = dot(dmixed, qkv_full, ((1,), (1,)))
-    grad_c1 = jnp.sum(dh1_part, axis=0)
-    grad_g1 = jnp.sum(dh1_part * unit1_all, axis=0)
-    dh1 = scatter_seq(split(dh1_part), size)
-    grad_qkv = scatter_dp(dot(h1, dmixed, ((0,), (0,))).reshape(dps, unit_rows, -1), dps)
+    grad_out = after(links.scatter_seq(blocks).astype(BF), grad_fc)
+    if aligned:
+        grad_out = ring.outward(ring.scatter(grad_out.reshape(-1, width)))
+        grad_out = lax.dynamic_slice_in_dim(grad_out, rows * rank - starts[0], rows, 0)
+    else:
+        grad_out = lax.psum_scatter(grad_out, "dp", scatter_dimension=0, tiled=True).astype(F32)
+    grad_qkv = dot(h1, after(dmixed, grad_fc), ((0,), (0,))).astype(BF)
+    grad_qkv_own = ring.scatter(grad_qkv)
+    dh1_part = dot(after(dmixed, grad_qkv), qkv_full, ((1,), (1,)))
+    output = ring.outward((x2 + links.scatter_seq(split(output_part)) + bias_p).astype(BF))
+    dh1 = links.scatter_seq(split(dh1_part))
+    fc_rows = links.rows_from_columns(grad_fc, unpack_fc)
+    behind = links.shift(fc_rows[:tail], -1)
     unit1, scale1 = normal(x_own.astype(F32))
-    input_grad = dx2 + norm_input_grad(unit1, scale1, gain1, dh1)
-
-    place_cols = lambda v, pack_size, unpack: unpack([jnp.where(rank == b, v, 0.0)[None] for b in range(pack_size)])[0]
-    wide = place_cols(grad_mixed, size, lambda p: unpack_heads(p, width)).reshape(3, width)
-    wide_bf = place_cols(grad_bf, size, lambda p: unpack_hidden(p, dps))
-    sums = jnp.concatenate(
-        [grad_g1, grad_c1, wide[0], wide[2], grad_bo, grad_g2, grad_c2, grad_bp, wide_bf]
-    )
-    sums = lax.psum(sums, ("dp", "seq"))
-    part = attention_vectors.shape[0]
+    input_grad = ring.outward(dx2 + norm_input_grad(unit1, scale1, gain1, dh1))
+
+    total = lambda m: jnp.sum(m.astype(F32), axis=0)
+    own_sum = lambda m: ring.outward(total(m))
+    place_cols = lambda v, unpack: unpack([jnp.where(rank == b, v, 0.0)[None] for b in range(size)])[0]
+    wide = place_cols(total(dmixed), lambda p: unpack_heads(p, width)).reshape(3, width)
+    wide_bf = place_cols(total(du), unpack_fc)
+    sums = jnp.concatenate([
+        own_sum(dh1_part * unit1_all), own_sum(dh1_part), wide[0], wide[2],
+        own_sum(dz), own_sum(dh2 * unit2), own_sum(dh2), own_sum(dy_wide), wide_bf,
+    ])
+    sums = links.all_sum(sums, ("seq", "dp"))
     vec1 = lax.dynamic_slice_in_dim(sums[: 4 * width], device * part, part)
     vec2 = lax.dynamic_slice_in_dim(sums[4 * width : 8 * width], device * part, part)
     sum_bf = sums[8 * width :]
 
-    qkv_flat = rows_from_columns(grad_qkv, lambda p: unpack_heads(p, width), size).astype(F32)
-    fc_rows = rows_from_columns(grad_fc, lambda p: unpack_hidden(p, dps), size)
-    after = lax.ppermute(fc_rows[:tail], ("dp", "seq"), [(i + 1, i) for i in range(devices - 1)])
-    fill = jnp.pad(sum_bf, (0, tail - hidden))
-    after = jnp.where(device == devices - 1, fill, after.astype(F32))
+    qkv_flat = links.rows_from_columns(grad_qkv_own, lambda p: unpack_heads(p, width)).astype(F32)
+    behind = jnp.where(last, jnp.pad(sum_bf, (0, tail - hidden)), behind.astype(F32))
     fc_flat_grad = lax.dynamic_slice_in_dim(
-        jnp.concatenate([fc_rows.astype(F32), after]), shift * device, w_fc.shape[0]
+        jnp.concatenate([fc_rows.astype(F32), behind]), shift * device, w_fc.shape[0]
     )
-    return (output[None], input_grad[None], qkv_flat, grad_out, fc_flat_grad, grad_proj, vec1, vec2)
+    return (output[None], input_grad[None], qkv_flat, grad_out.reshape(-1), fc_flat_grad, ring.outward(grad_proj_own).reshape(-1), vec1, vec2)
 
 
 def solution(mesh):

time: 885 us -> 585 us (0.66)
  local copies, waits for them, and re-layouts: 209 us -> 112 us
  waiting for transfers between devices: 276 us -> 193 us
  blocking collectives: 76.8 us -> 0 us
  starting transfers between devices: 73.4 us -> 47.5 us
  other arithmetic: 65.4 us -> 47.8 us
    ppermute x84 -> x57, waiting for transfers between devices: 276 us -> 182 us  [the longest x55 181 us: swap(): lax.ppermute(v, axis, pairs)]
    dynamic_update_slice x30 -> x6, local copies, waits for them, and re-layouts: 77.3 us -> 5.49 us  [the longest x4 5.03 us: local(): lax.dynamic_update_slice_in_dim(out_full, out_parts[j], starts[j], 1)]
    all_gather x1 -> x0, blocking collectives: 39.7 us -> none  [local(): lax.all_gather(jnp.stack([attention_vectors, block_vectors]), ('dp', 'seq...]
    psum x1 -> x0, blocking collectives: 37 us -> none  [local(): lax.psum(jnp.where(device == devices - 1, w_fc[-hidden:], jnp.zeros((), B...]
    reshape x12 -> x4, local copies, waits for them, and re-layouts: 35.1 us -> 5.43 us  [the longest x1 1.73 us: local(): ring.outward(grad_proj_own).reshape(-1)]
    ppermute x84 -> x57, starting transfers between devices: 73.4 us -> 46 us  [the longest x55 43 us: swap(): lax.ppermute(v, axis, pairs)]
    convert_element_type x16 -> x1, local copies, waits for them, and re-layouts: 18.4 us -> 1.86 us  [local(): links.rows_from_columns(grad_qkv_own, lambda p: unpack_heads(p, width))]
    concatenate x3 -> x28, local copies, waits for them, and re-layouts: 2.95 us -> 19.5 us  [the longest x16 11.2 us: blocks(): jnp.concatenate([value[..., d * part:(d + 1) * part] for d in order], axi...]
  transfers between devices with their start and end apart: 85 -> 65, of which waited for: 26 -> 30; matrix products, arithmetic and copies ran while one was open for 39% -> 44% of each run, Pallas kernels for 6% -> 8%
where the time goes in v2:
time: 585 us; the launch traced here: 578 us
  waiting for transfers between devices  193 us (33%)
  local copies, waits for them, and re-layouts  112 us (19%)
  matrix products  111 us (19%)
  Pallas kernels  48.6 us (8%)
  other arithmetic  47.8 us (8%)
  starting transfers between devices  47.5 us (8%)
  between operations  17.4 us (3%)
    ppermute x55, waiting for transfers between devices, swap(): lax.ppermute(v, axis, pairs)  181 us
    dot_general x12, matrix products, dot(): return lax.dot_general(a, b, (dims, ((), ())), preferred_element_type=F32)  111 us
    ppermute x55, starting transfers between devices, swap(): lax.ppermute(v, axis, pairs)  43 us
    unnamed x250, local copies, waits for them, and re-layouts  34.2 us
    pallas_call x1, Pallas kernels, attention_backward(): pl.pallas_call(partial(attention_backward_kernel, size, pairs, odd), out_...  27.6 us
    pallas_call x1, Pallas kernels, attention_forward(): pl.pallas_call(partial(attention_forward_kernel, size, pairs, odd), out_s...  21 us
    slice x28, local copies, waits for them, and re-layouts, blocks(): value[..., d * part:(d + 1) * part]  15.1 us
  transfers between devices with their start and end apart: 65, of which 30 were waited for; matrix products, arithmetic and copies ran while one was open for 44% of the time, Pallas kernels for 8%

profile of v2, /device:TPU:0, one launch (start us, length us, event | category | flops | bytes accessed | tf_op | source)
XLA Modules:
  0.0 577.7 jit_solution(14024762076622618395)
XLA Ops:
  21.8 6.0 %collective-permute-done.1 = bf16[50,1408]{1,0:T(8,128)(2,1)S(1)} collective-permute-done((bf16[50,1408]{1,0:T(8,128)(2,1)S(1)}, bf16[50,1408]{1,0:T(8,128)(2,1)S(1)}, u32[]{:S(2)}, u32[]{:S(2)}) %collective-permute-start.1) | collective-permute-done | bytes 140832 | tf_op jit(solution)/shard_map/ppermute | solution.py:45
  40.2 5.7 collective-permute-start.12
  60.7 3.8 reshape_reshape.4
  85.6 5.9 %collective-permute-done.15 = bf16[50,1600]{1,0:T(8,128)(2,1)S(1)} collective-permute-done((bf16[50,1600]{1,0:T(8,128)(2,1)S(1)}, bf16[50,1600]{1,0:T(8,128)(2,1)S(1)}, u32[]{:S(2)}, u32[]{:S(2)}) %collective-permute-start.15) | collective-permute-done | bytes 160032 | tf_op jit(solution)/shard_map/ppermute | solution.py:45
  92.5 5.9 %collective-permute-done.16 = bf16[50,1600]{1,0:T(8,128)(2,1)S(1)} collective-permute-done((bf16[50,1600]{1,0:T(8,128)(2,1)S(1)}, bf16[50,1600]{1,0:T(8,128)(2,1)S(1)}, u32[]{:S(2)}, u32[]{:S(2)}) %collective-permute-start.16) | collective-permute-done | bytes 160032 | tf_op jit(solution)/shard_map/ppermute | solution.py:45
  114.7 31.7 %collective-permute-done.17 = bf16[8,56,1600]{2,1,0:T(8,128)(2,1)} collective-permute-done((bf16[8,56,1600]{2,1,0:T(8,128)(2,1)}, bf16[8,56,1600]{2,1,0:T(8,128)(2,1)}, u32[]{:S(2)}, u32[]{:S(2)}) %collective-permute-start.17) | collective-permute-done | bytes 1433632 | tf_op jit(solution)/shard_map/ppermute | solution.py:45
  146.4 9.7 %add_convert_fusion.q_ref.k_ref.v_ref = bf16[1024,1408]{1,0:T(8,128)(2,1)S(1)} fusion(bf16[1600,1408]{1,0:T(8,128)(2,1)} %all-gather.5.cloned.1.call-done, f32[1408]{0:T(1024)S(1)} %select_select_fusion.43, f32[1600]{0:T(1024)S(1)} %concatenate.309, f32[1600]{0:T(1024)S(1)} %concatenate.308, f32[1024]{0:T(1024)S(1)} %add_rsqrt_fusion, ...), kind=kOutput, calls=%fused_computation.26 | convolution fusion | flops 4637917184 | bytes 10692608 | tf_op jit(solution)/shard_map/dot_general | solution.py:389
  166.9 21.0 %attention_forward.1 = bf16[1024,512]{1,0:T(8,128)(2,1)S(1)} custom-call(s32[2]{0:T(128)S(1)} %pad_add_fusion.info, bf16[1024,1408]{1,0:T(8,128)(2,1)S(1)} %add_convert_fusion.q_ref.k_ref.v_ref, bf16[1024,1408]{1,0:T(8,128)(2,1)S(1)} %add_convert_fusion.q_ref.k_ref.v_ref, bf16[1024,1408]{1,0:T(8,128)(2,1)S(1)} %add_convert_fusion.q_ref.k_ref.v_ref), custom_call_target="tpu_custom_call" | custom-call | flops 1879048192 | bytes 5767168 | tf_op jit(solution)/shard_map/attention_forward/pallas_call | solution.py:321
  193.6 6.0 %collective-permute-done.19 = bf16[256,512]{1,0:T(8,128)(2,1)S(1)} collective-permute-done((bf16[256,512]{1,0:T(8,128)(2,1)S(1)}, bf16[256,512]{1,0:T(8,128)(2,1)S(1)}, u32[]{:S(2)}, u32[]{:S(2)}) %collective-permute-start.19) | collective-permute-done | bytes 262176 | tf_op jit(solution)/shard_map/ppermute | solution.py:45
  203.2 4.8 collective-permute-done.20
  209.6 5.3 fusion.98
  219.4 18.3 %collective-permute-done.28 = bf16[256,1600]{0,1:T(8,128)(2,1)} collective-permute-done((bf16[256,1600]{0,1:T(8,128)(2,1)}, bf16[256,1600]{0,1:T(8,128)(2,1)}, u32[]{:S(2)}, u32[]{:S(2)}) %collective-permute-start.28) | collective-permute-done | bytes 819232 | tf_op jit(solution)/shard_map/ppermute | solution.py:45
  245.2 13.6 %multiply_convert_fusion = (bf16[1024,1600]{0,1:T(8,128)(2,1)S(1)}, f32[1024,1600]{0,1:T(8,128)}) fusion(f32[1600]{0:T(1024)S(1)} %select_select_fusion.42, bf16[1600,1600]{1,0:T(8,128)(2,1)} %all-gather.9.cloned.1.call-done, bf16[256,1600]{0,1:T(8,128)(2,1)} %collective-permute-done.29, bf16[256,1600]{0,1:T(8,128)(2,1)} %collective-permute-done.28, ...), kind=kOutput, calls=%fused_computation.24 | convolution fusion | flops 5272371200 | bytes 18233600 | tf_op jit(solution)/shard_map/dot_general | solution.py:389
  260.5 9.9 %convolution_convert_fusion.2 = bf16[1600,1600]{1,0:T(8,128)(2,1)} fusion(bf16[1024,1600]{0,1:T(8,128)(2,1)S(1)} %get-tuple-element.112, bf16[1024,1600]{0,1:T(8,128)(2,1)} %constant_dynamic-update-slice_fusion), kind=kOutput, calls=%fused_computation.8 | convolution fusion | flops 5245440000 | bytes 11673600 | tf_op jit(solution)/shard_map/dot_general | solution.py:389
  270.5 14.8 %convert_reduce_fusion.1 = (f32[1600]{0:T(1024)S(1)}, bf16[1024,1600]{0,1:T(8,128)(2,1)S(1)}) fusion(f32[1024,1600]{0,1:T(8,128)} %get-tuple-element.493, f32[1600]{0:T(1024)S(1)} %select_select_fusion.42, bf16[1600,1600]{1,0:T(8,128)(2,1)} %all-gather.11.cloned.1.call-done, bf16[1024,1600]{0,1:T(8,128)(2,1)} %constant_dynamic-update-slice_fusion), kind=kOutput, calls=%fused_computation.23 | convolution fusion | flops 5278923264 | bytes 18240000 | tf_op jit(solution)/shard_map/dot_general | solution.py:389
  285.3 8.1 %fusion.99 = (bf16[1024,1600]{0,1:T(8,128)(2,1)S(1)}, f32[1024,1600]{0,1:T(8,128)S(1)}) fusion(bf16[1600,1600]{1,0:T(8,128)(2,1)} %all-gather.9.cloned.1.call-done, bf16[1024,1600]{0,1:T(8,128)(2,1)S(1)} %get-tuple-element.124), kind=kOutput, calls=%fused_computation.314 | convolution fusion | flops 5244518400 | bytes 18227200 | tf_op jit(solution)/shard_map/dot_general | solution.py:389
  297.5 10.6 %convolution_convert_fusion.1 = bf16[1600,1600]{1,0:T(8,128)(2,1)} fusion(bf16[1024,1600]{0,1:T(8,128)(2,1)S(1)} %get-tuple-element.124, bf16[256,1600]{0,1:T(8,128)(2,1)} %collective-permute-done.29, bf16[256,1600]{0,1:T(8,128)(2,1)} %collective-permute-done.28, bf16[256,1600]{0,1:T(8,128)(2,1)} %collective-permute-done.27, ...), kind=kOutput, calls=%fused_computation.7 | convolution fusion | flops 5258547200 | bytes 11673600 | tf_op jit(solution)/shard_map/dot_general | solution.py:389
  308.2 8.9 %collective-permute-done.32 = bf16[256,1600]{0,1:T(8,128)(2,1)} collective-permute-done((bf16[256,1600]{0,1:T(8,128)(2,1)S(1)}, bf16[256,1600]{0,1:T(8,128)(2,1)}, u32[]{:S(2)}, u32[]{:S(2)}) %collective-permute-start.32) | collective-permute-done | bytes 819232 | tf_op jit(solution)/shard_map/ppermute | solution.py:45
  320.3 10.8 %reduce-scatter.17.cloned.1.call-done = bf16[200,1600]{1,0:T(8,128)(2,1)} async-done(((bf16[1600,1600]{1,0:T(8,128)(2,1)}), bf16[200,1600]{1,0:T(8,128)(2,1)}) %reduce-scatter.17.cloned.1.call-update) | async-done | bytes 640016
  333.4 4.7 convolution_convert_fusion.4
  355.4 5.7 collective-permute-done.38
  364.9 4.8 collective-permute-done.39
  370.6 10.8 %fusion.100 = (bf16[1024,1600]{0,1:T(8,128)(2,1)S(1)}, f32[1024,1600]{0,1:T(8,128)}) fusion(bf16[1024,1600]{0,1:T(8,128)(2,1)S(1)} %copy-done.102, bf16[1600,1600]{1,0:T(8,128)(2,1)} %all-gather.11.cloned.1.call-done), kind=kOutput, calls=%fused_computation.315 | convolution fusion | flops 5244518400 | bytes 18227200 | tf_op jit(solution)/shard_map/dot_general | solution.py:389
  386.6 17.9 %collective-permute-done.40 = bf16[8,56,1600]{2,1,0:T(8,128)(2,1)S(1)} collective-permute-done((bf16[8,56,1600]{2,1,0:T(8,128)(2,1)S(1)}, bf16[8,56,1600]{2,1,0:T(8,128)(2,1)S(1)}, u32[]{:S(2)}, u32[]{:S(2)}) %collective-permute-start.40) | collective-permute-done | bytes 1433632 | tf_op jit(solution)/shard_map/ppermute | solution.py:45
  407.6 27.6 %attention_backward.1 = bf16[1024,1408]{1,0:T(8,128)(2,1)S(1)} custom-call(s32[2]{0:T(128)S(1)} %pad_add_fusion.info, bf16[1024,1408]{1,0:T(8,128)(2,1)} %copy-done, bf16[1024,1408]{1,0:T(8,128)(2,1)} %copy-done, bf16[1024,1408]{1,0:T(8,128)(2,1)} %copy-done, bf16[1024,512]{1,0:T(8,128)(2,1)S(1)} %pad_maximum_fusion.2.g_ref), custom_call_target="tpu_custom_call" | custom-call | flops 5637144576 | bytes 8650752 | tf_op jit(solution)/shard_map/attention_backward/pallas_call | solution.py:342
  440.6 8.9 %convolution_convert_fusion = bf16[1600,1408]{1,0:T(8,128)(2,1)} fusion(bf16[1024,1408]{1,0:T(8,128)(2,1)S(1)} %attention_backward.1, f32[1600]{0:T(1024)} %copy-done.69, f32[1600]{0:T(1024)} %copy-done.44, f32[1024]{0:T(1024)} %copy-done.98, f32[1024]{0:T(1024)S(1)} %copy-done.55, bf16[256,1600]{0,1:T(8,128)(2,1)} %copy-done.16, ...), kind=kOutput, calls=%fused_computation.6 | convolution fusion | flops 4637286400 | bytes 10686976 | tf_op jit(solution)/shard_map/dot_general | solution.py:389
  449.5 13.1 %fusion.57 = (f32[1600]{0:T(1024)}, f32[1600]{0:T(1024)}, bf16[1024,1600]{0,1:T(8,128)(2,1)S(1)}, f32[1024,1600]{0,1:T(8,128)}) fusion(f32[1024]{0:T(1024)} %copy-done.98, f32[1024]{0:T(1024)S(1)} %copy-done.55, bf16[256,1600]{0,1:T(8,128)(2,1)} %copy-done.16, bf16[256,1600]{0,1:T(8,128)(2,1)} %copy-done.14, bf16[256,1600]{0,1:T(8,128)(2,1)} %copy-done.15, ...), kind=kOutput, calls=%fused_computation.276 | convolution fusion | flops 4636668928 | bytes 20517376 | tf_op jit(solution)/shard_map/dot_general | solution.py:389
  475.2 12.6 %collective-permute-done.41 = bf16[256,1600]{0,1:T(8,128)(2,1)} collective-permute-done((bf16[256,1600]{0,1:T(8,128)(2,1)}, bf16[256,1600]{0,1:T(8,128)(2,1)}, u32[]{:S(2)}, u32[]{:S(2)}) %collective-permute-start.41) | collective-permute-done | bytes 819232 | tf_op jit(solution)/shard_map/ppermute | solution.py:45
  489.1 18.2 %collective-permute-done.44 = bf16[256,1600]{0,1:T(8,128)(2,1)S(1)} collective-permute-done((bf16[256,1600]{0,1:T(8,128)(2,1)}, bf16[256,1600]{0,1:T(8,128)(2,1)S(1)}, u32[]{:S(2)}, u32[]{:S(2)}) %collective-permute-start.44) | collective-permute-done | bytes 819232 | tf_op jit(solution)/shard_map/ppermute | solution.py:45
  516.5 4.1 collective-permute-done.46
  534.7 4.4 collective-permute-done.54
  560.1 5.4 collective-permute-done.49
  (614 shorter events, 221.5 us)
Async XLA Ops:
  7.2 103.3 %all-gather.7.cloned.1.call-start = ((), (), s32[]{:S(2)}) async-start(), calls=%async_computation.5 | async-start | bytes 1677312 | tf_op jit(solution)/shard_map/all_gather | solution.py:115
  8.7 12.6 %collective-permute-start.4 = (bf16[50,1600]{1,0:T(8,128)(2,1)S(1)}, bf16[50,1600]{1,0:T(8,128)(2,1)}, u32[]{:S(2)}, u32[]{:S(2)}) collective-permute-start(bf16[50,1600]{1,0:T(8,128)(2,1)S(1)} %concatenate.306), channel_id=1, source_target_pairs={{0,1},{1,0},{2,3},{3,2},{4,5},{5,4},{6,7},{7,6},{8,9},{9,8},{10,11... | collective-permute-start | bytes 480008 | tf_op jit(solution)/shard_map/ppermute | solution.py:45
  9.2 12.1 %collective-permute-start = (bf16[50,1600]{1,0:T(8,128)(2,1)S(1)}, bf16[50,1600]{1,0:T(8,128)(2,1)}, u32[]{:S(2)}, u32[]{:S(2)}) collective-permute-start(bf16[50,1600]{1,0:T(8,128)(2,1)S(1)} %concatenate.306), channel_id=1, source_target_pairs={{0,2},{1,3},{2,0},{3,1},{4,6},{5,7},{6,4},{7,5},{8,10},{9,11},{10,... | collective-permute-start | bytes 480008 | tf_op jit(solution)/shard_map/ppermute | solution.py:45
  30.2 116.2 %all-gather.5.cloned.1.call-start = ((), (), s32[]{:S(2)}) async-start(), calls=%async_computation.4 | async-start | bytes 5068800 | tf_op jit(solution)/shard_map/all_gather | solution.py:115
  40.2 8.6 %collective-permute-start.12 = (bf16[19200]{0:T(1024)(128)(2,1)S(1)}, bf16[19200]{0:T(1024)(128)(2,1)S(1)}, u32[]{:S(2)}, u32[]{:S(2)}) collective-permute-start(bf16[19200]{0:T(1024)(128)(2,1)S(1)} %add.239), channel_id=1, source_target_pairs={{0,16},{4,20},{8,24},{12,28},{16,0},{20,4},{24,8},{28,12},{1,17},{... | collective-permute-start | bytes 115208 | tf_op jit(solution)/shard_map/ppermute | solution.py:45
  56.2 189.0 %all-gather.9.cloned.1.call-start = ((), (), s32[]{:S(2)}) async-start(), calls=%async_computation.6 | async-start | bytes 5990400 | tf_op jit(solution)/shard_map/all_gather | solution.py:115
  56.7 23.2 %collective-permute-start.10 = (bf16[256,1600]{0,1:T(8,128)(2,1)S(1)}, bf16[256,1600]{0,1:T(8,128)(2,1)S(1)}, u32[]{:S(2)}, u32[]{:S(2)}) collective-permute-start(bf16[256,1600]{0,1:T(8,128)(2,1)S(1)} %slice_dynamic-update-slice_fusion.22), channel_id=1, source_target_pairs={{0,2},{1,3},{2,0},{3,1},{4,6},{5,7},{6,4},{7,5},{8,10},{9,11},{10,... | collective-permute-start | bytes 2457608 | tf_op jit(solution)/shard_map/ppermute | solution.py:45
  57.2 22.7 %collective-permute-start.9 = (bf16[256,1600]{0,1:T(8,128)(2,1)S(1)}, bf16[256,1600]{0,1:T(8,128)(2,1)S(1)}, u32[]{:S(2)}, u32[]{:S(2)}) collective-permute-start(bf16[256,1600]{0,1:T(8,128)(2,1)S(1)} %slice_dynamic-update-slice_fusion.22), channel_id=1, source_target_pairs={{0,1},{1,0},{2,3},{3,2},{4,5},{5,4},{6,7},{7,6},{8,9},{9,8},{10,11... | collective-permute-start | bytes 2457608 | tf_op jit(solution)/shard_map/ppermute | solution.py:45
  79.9 11.6 %collective-permute-start.11 = (bf16[256,1600]{0,1:T(8,128)(2,1)S(1)}, bf16[256,1600]{0,1:T(8,128)(2,1)S(1)}, u32[]{:S(2)}, u32[]{:S(2)}) collective-permute-start(bf16[256,1600]{0,1:T(8,128)(2,1)S(1)} %collective-permute-done.10), channel_id=1, source_target_pairs={{0,1},{1,0},{2,3},{3,2},{4,5},{5,4},{6,7},{7,6},{8,9},{9,8},{10,11... | collective-permute-start | bytes 2457608 | tf_op jit(solution)/shard_map/ppermute | solution.py:45
  99.6 170.9 %all-gather.11.cloned.1.call-start = ((), (), s32[]{:S(2)}) async-start(), calls=%async_computation.7 | async-start | bytes 5990400 | tf_op jit(solution)/shard_map/all_gather | solution.py:115
  111.4 34.9 %collective-permute-start.17 = (bf16[8,56,1600]{2,1,0:T(8,128)(2,1)}, bf16[8,56,1600]{2,1,0:T(8,128)(2,1)}, u32[]{:S(2)}, u32[]{:S(2)}) collective-permute-start(bf16[8,56,1600]{2,1,0:T(8,128)(2,1)} %bitcast.145), channel_id=1, source_target_pairs={{0,2},{1,3},{2,0},{3,1},{4,6},{5,7},{6,4},{7,5},{8,10},{9,11},{10,... | collective-permute-start | bytes 4300808 | tf_op jit(solution)/shard_map/ppermute | solution.py:45
  146.3 9.8 %collective-permute-start.23 = (bf16[8,56,1600]{2,1,0:T(8,128)(2,1)}, bf16[8,56,1600]{2,1,0:T(8,128)(2,1)}, u32[]{:S(2)}, u32[]{:S(2)}) collective-permute-start(bf16[8,56,1600]{2,1,0:T(8,128)(2,1)} %collective-permute-done.17), channel_id=1, source_target_pairs={{0,1},{1,0},{2,3},{3,2},{4,5},{5,4},{6,7},{7,6},{8,9},{9,8},{10,11... | collective-permute-start | bytes 4300808 | tf_op jit(solution)/shard_map/ppermute | solution.py:45
  156.1 31.8 %collective-permute-start.18 = (bf16[256,1600]{0,1:T(8,128)(2,1)}, bf16[256,1600]{0,1:T(8,128)(2,1)}, u32[]{:S(2)}, u32[]{:S(2)}) collective-permute-start(bf16[256,1600]{0,1:T(8,128)(2,1)} %get-tuple-element.97), channel_id=1, source_target_pairs={{0,2},{1,3},{2,0},{3,1},{4,6},{5,7},{6,4},{7,5},{8,10},{9,11},{10,... | collective-permute-start | bytes 2457608 | tf_op jit(solution)/shard_map/ppermute | solution.py:45
  157.3 30.6 %collective-permute-start.24 = (bf16[256,1600]{0,1:T(8,128)(2,1)}, bf16[256,1600]{0,1:T(8,128)(2,1)}, u32[]{:S(2)}, u32[]{:S(2)}) collective-permute-start(bf16[256,1600]{0,1:T(8,128)(2,1)} %get-tuple-element.97), channel_id=1, source_target_pairs={{0,1},{1,0},{2,3},{3,2},{4,5},{5,4},{6,7},{7,6},{8,9},{9,8},{10,11... | collective-permute-start | bytes 2457608 | tf_op jit(solution)/shard_map/ppermute | solution.py:45
  166.7 164.5 %reduce-scatter.17.cloned.1.call-start = ((), (), s32[]{:S(2)}) async-start(), calls=%async_computation.8 | async-start | bytes 5990400
  187.9 11.9 %collective-permute-start.25 = (bf16[256,1600]{0,1:T(8,128)(2,1)}, bf16[256,1600]{0,1:T(8,128)(2,1)S(1)}, u32[]{:S(2)}, u32[]{:S(2)}) collective-permute-start(bf16[256,1600]{0,1:T(8,128)(2,1)} %collective-permute-done.18), channel_id=1, source_target_pairs={{0,1},{1,0},{2,3},{3,2},{4,5},{5,4},{6,7},{7,6},{8,9},{9,8},{10,11... | collective-permute-start | bytes 2457608 | tf_op jit(solution)/shard_map/ppermute | solution.py:45
  216.7 21.0 %collective-permute-start.28 = (bf16[256,1600]{0,1:T(8,128)(2,1)}, bf16[256,1600]{0,1:T(8,128)(2,1)}, u32[]{:S(2)}, u32[]{:S(2)}) collective-permute-start(bf16[256,1600]{0,1:T(8,128)(2,1)} %add_convert_fusion.3), channel_id=1, source_target_pairs={{0,2},{1,3},{2,0},{3,1},{4,6},{5,7},{6,4},{7,5},{8,10},{9,11},{10,... | collective-permute-start | bytes 2457608 | tf_op jit(solution)/shard_map/ppermute | solution.py:45
  270.4 170.1 %reduce-scatter.19.cloned.1.call-start = ((), (), s32[]{:S(2)}) async-start(), calls=%async_computation.9 | async-start | bytes 5990400
  296.4 20.7 %collective-permute-start.32 = (bf16[256,1600]{0,1:T(8,128)(2,1)S(1)}, bf16[256,1600]{0,1:T(8,128)(2,1)}, u32[]{:S(2)}, u32[]{:S(2)}) collective-permute-start(bf16[256,1600]{0,1:T(8,128)(2,1)S(1)} %fusion.33), channel_id=1, source_target_pairs={{0,2},{1,3},{2,0},{3,1},{4,6},{5,7},{6,4},{7,5},{8,10},{9,11},{10,... | collective-permute-start | bytes 2457608 | tf_op jit(solution)/shard_map/ppermute | solution.py:45
  297.4 19.7 %collective-permute-start.31 = (bf16[256,1600]{0,1:T(8,128)(2,1)S(1)}, bf16[256,1600]{0,1:T(8,128)(2,1)}, u32[]{:S(2)}, u32[]{:S(2)}) collective-permute-start(bf16[256,1600]{0,1:T(8,128)(2,1)S(1)} %get-tuple-element.110), channel_id=1, source_target_pairs={{0,1},{1,0},{2,3},{3,2},{4,5},{5,4},{6,7},{7,6},{8,9},{9,8},{10,11... | collective-permute-start | bytes 2457608 | tf_op jit(solution)/shard_map/ppermute | solution.py:45
  331.1 220.2 %reduce-scatter.23.cloned.1.call-start = ((), (), s32[]{:S(2)}) async-start(), calls=%async_computation.11 | async-start | bytes 1677312
  349.7 11.7 %collective-permute-start.34 = (bf16[8,56,1600]{2,1,0:T(8,128)(2,1)}, bf16[8,56,1600]{2,1,0:T(8,128)(2,1)}, u32[]{:S(2)}, u32[]{:S(2)}) collective-permute-start(bf16[8,56,1600]{2,1,0:T(8,128)(2,1)} %get-tuple-element.115), channel_id=1, source_target_pairs={{0,1},{1,0},{2,3},{3,2},{4,5},{5,4},{6,7},{7,6},{8,9},{9,8},{10,11... | collective-permute-start | bytes 4300808 | tf_op jit(solution)/shard_map/ppermute | solution.py:45
  361.1 8.6 %collective-permute-start.39 = (bf16[256,512]{1,0:T(8,128)(2,1)S(1)}, bf16[256,512]{1,0:T(8,128)(2,1)S(1)}, u32[]{:S(2)}, u32[]{:S(2)}) collective-permute-start(bf16[256,512]{1,0:T(8,128)(2,1)S(1)} %get-tuple-element.120), channel_id=1, source_target_pairs={{0,3},{1,2},{2,1},{3,0},{4,7},{5,6},{6,5},{7,4},{8,11},{9,10},{10,... | collective-permute-start | bytes 786440 | tf_op jit(solution)/shard_map/ppermute | solution.py:45
  361.4 25.1 %collective-permute-start.35 = (bf16[8,56,1600]{2,1,0:T(8,128)(2,1)}, bf16[8,56,1600]{2,1,0:T(8,128)(2,1)S(1)}, u32[]{:S(2)}, u32[]{:S(2)}) collective-permute-start(bf16[8,56,1600]{2,1,0:T(8,128)(2,1)} %get-tuple-element.116), channel_id=1, source_target_pairs={{0,1},{1,0},{2,3},{3,2},{4,5},{5,4},{6,7},{7,6},{8,9},{9,8},{10,11... | collective-permute-start | bytes 4300808 | tf_op jit(solution)/shard_map/ppermute | solution.py:45
  369.7 34.8 %collective-permute-start.40 = (bf16[8,56,1600]{2,1,0:T(8,128)(2,1)S(1)}, bf16[8,56,1600]{2,1,0:T(8,128)(2,1)S(1)}, u32[]{:S(2)}, u32[]{:S(2)}) collective-permute-start(bf16[8,56,1600]{2,1,0:T(8,128)(2,1)S(1)} %add_convert_fusion.2), channel_id=1, source_target_pairs={{0,2},{1,3},{2,0},{3,1},{4,6},{5,7},{6,4},{7,5},{8,10},{9,11},{10,... | collective-permute-start | bytes 4300808 | tf_op jit(solution)/shard_map/ppermute | solution.py:45
  386.5 54.0 %collective-permute-start.36 = (bf16[256,1600]{0,1:T(8,128)(2,1)S(1)}, bf16[256,1600]{0,1:T(8,128)(2,1)}, u32[]{:S(2)}, u32[]{:S(2)}) collective-permute-start(bf16[256,1600]{0,1:T(8,128)(2,1)S(1)} %get-tuple-element.117), channel_id=1, source_target_pairs={{0,1},{1,0},{2,3},{3,2},{4,5},{5,4},{6,7},{7,6},{8,9},{9,8},{10,11... | collective-permute-start | bytes 2457608 | tf_op jit(solution)/shard_map/ppermute | solution.py:45
  440.5 23.4 %collective-permute-start.37 = (bf16[256,1600]{0,1:T(8,128)(2,1)}, bf16[256,1600]{0,1:T(8,128)(2,1)}, u32[]{:S(2)}, u32[]{:S(2)}) collective-permute-start(bf16[256,1600]{0,1:T(8,128)(2,1)} %get-tuple-element.118), channel_id=1, source_target_pairs={{0,1},{1,0},{2,3},{3,2},{4,5},{5,4},{6,7},{7,6},{8,9},{9,8},{10,11... | collective-permute-start | bytes 2457608 | tf_op jit(solution)/shard_map/ppermute | solution.py:45
  440.6 111.8 %reduce-scatter.21.cloned.1.call-start = ((), (), s32[]{:S(2)}) async-start(), calls=%async_computation.10 | async-start | bytes 5068800
  467.2 20.6 %collective-permute-start.41 = (bf16[256,1600]{0,1:T(8,128)(2,1)}, bf16[256,1600]{0,1:T(8,128)(2,1)}, u32[]{:S(2)}, u32[]{:S(2)}) collective-permute-start(bf16[256,1600]{0,1:T(8,128)(2,1)} %fusion.28), channel_id=1, source_target_pairs={{0,2},{1,3},{2,0},{3,1},{4,6},{5,7},{6,4},{7,5},{8,10},{9,11},{10,... | collective-permute-start | bytes 2457608 | tf_op jit(solution)/shard_map/ppermute | solution.py:45
  487.8 19.5 %collective-permute-start.44 = (bf16[256,1600]{0,1:T(8,128)(2,1)}, bf16[256,1600]{0,1:T(8,128)(2,1)S(1)}, u32[]{:S(2)}, u32[]{:S(2)}) collective-permute-start(bf16[256,1600]{0,1:T(8,128)(2,1)} %fusion.25), channel_id=1, source_target_pairs={{0,2},{1,3},{2,0},{3,1},{4,6},{5,7},{6,4},{7,5},{8,10},{9,11},{10,... | collective-permute-start | bytes 2457608 | tf_op jit(solution)/shard_map/ppermute | solution.py:45
  488.2 19.5 %collective-permute-start.43 = (bf16[256,1600]{0,1:T(8,128)(2,1)}, bf16[256,1600]{0,1:T(8,128)(2,1)S(1)}, u32[]{:S(2)}, u32[]{:S(2)}) collective-permute-start(bf16[256,1600]{0,1:T(8,128)(2,1)} %get-tuple-element.129), channel_id=1, source_target_pairs={{0,1},{1,0},{2,3},{3,2},{4,5},{5,4},{6,7},{7,6},{8,9},{9,8},{10,11... | collective-permute-start | bytes 2457608 | tf_op jit(solution)/shard_map/ppermute | solution.py:45
  509.8 12.3 %collective-permute-start.50 = (bf16[50,1600]{1,0:T(8,128)(2,1)S(1)}, bf16[50,1600]{1,0:T(8,128)(2,1)S(1)}, u32[]{:S(2)}, u32[]{:S(2)}) collective-permute-start(bf16[50,1600]{1,0:T(8,128)(2,1)S(1)} %get-tuple-element.136), channel_id=1, source_target_pairs={{0,1},{1,0},{2,3},{3,2},{4,5},{5,4},{6,7},{7,6},{8,9},{9,8},{10,11... | collective-permute-start | bytes 480008 | tf_op jit(solution)/shard_map/ppermute | solution.py:45
  (136 other events, 2209.9 us)
Sparse Core Ops, SparseCore 0:
  30.3 34.3 all-gather.6
  66.8 50.3 all-gather.4
  118.7 58.5 all-gather.8
  178.7 58.4 all-gather.10
  270.6 60.5 reduce-scatter.16
  333.3 59.7 reduce-scatter.18
  440.7 32.3 reduce-scatter.22
  475.5 51.0 reduce-scatter.20

commit v3 on v2

--- a/solution.py
+++ b/solution.py
@@ -39,8 +39,10 @@
         self.last[link] = permute(after(value, self.last.get(link)))
         return self.last[link]
 
-    def swap(self, value, axis, bits):
+    def swap(self, value, axis, bits, free=False):
         pairs = [(i, i ^ bits) for i in range(self.sizes[axis])]
+        if free:
+            return lax.ppermute(value, axis, pairs)
         top = 1 << (bits.bit_length() - 1)
         return self.ordered(value, (axis, top), lambda v: lax.ppermute(v, axis, pairs))
 
@@ -49,60 +51,122 @@
         pairs = [(i, i + step) for i in range(count) if 0 <= i + step < count]
         return self.ordered(value, ("seq", 1), lambda v: lax.ppermute(v, ("dp", "seq"), pairs))
 
-    def all_sum(self, value, axes):
+    def all_sum(self, value, axes, free=False):
         for axis in axes:
             for bit in bits_of(self.sizes[axis]):
-                value = value + self.swap(value, axis, bit)
+                value = value + self.swap(value, axis, bit, free)
         return value
 
-    def gather_seq(self, value):
+    def gather_seq(self, value, free=False):
         pieces = {0: value}
         for bit in bits_of(self.sizes["seq"]):
             for j in list(pieces):
-                pieces[j ^ bit] = self.swap(pieces[j], "seq", bit)
+                pieces[j ^ bit] = self.swap(pieces[j], "seq", bit, free)
         return [pieces[j] for j in range(len(pieces))]
 
-    def scatter_seq(self, blocks):
+    def scatter_seq(self, blocks, last=None, free=False):
         blocks = dict(enumerate(blocks))
         for bit in reversed(bits_of(self.sizes["seq"])):
             for j in sorted(blocks, reverse=True):
                 if j & bit:
-                    got = self.swap(blocks.pop(j).astype(BF), "seq", bit)
+                    got = after(self.swap(blocks.pop(j).astype(BF), "seq", bit, free), last if j == bit and j > 1 else None)
                     blocks[j ^ bit] = blocks[j ^ bit].astype(F32) + got.astype(F32)
         return blocks[0]
 
     def exchange_seq(self, pieces):
-        return [pieces[0]] + [self.swap(pieces[j], "seq", j) for j in range(1, len(pieces))]
+        return [pieces[0]] + [self.swap(pieces[j], "seq", j, True) for j in range(1, len(pieces))]
 
     def relative(self, pieces, axis="seq"):
         mine, size = lax.axis_index(axis), len(pieces)
         return [pick([pieces[j ^ m] for m in range(size)], mine) for j in range(size)]
 
-    def columns_from_rows(self, flat, rows, pack):
-        size = self.sizes["seq"]
-        cols = flat.shape[0] * size // rows
+    def columns_from_rows(self, flats, rows, columns):
+        size, rank = self.sizes["seq"], lax.axis_index("seq")
+        shape = lambda flat: (-1, flat.shape[0] * size // rows)
+        own = sum(count for _, _, count in columns(0))
         if rows % size == 0:
-            pieces = self.relative(pack(flat.reshape(rows // size, cols)))
+            part = rows // size
+            plans = [[in_columns(columns(q ^ j), part) for j in range(size)] for q in range(size)]
+            pieces = rearrange([flat.reshape(shape(flat)) for flat in flats], [(part, own)] * size, plans, rank)
             return jnp.concatenate(self.relative(self.exchange_seq(pieces)), axis=0)
-        full = lax.all_gather(flat, "seq", axis=0, tiled=True).reshape(rows, cols)
-        return pick(pack(full), lax.axis_index("seq"))
-
-    def rows_from_columns(self, value, unpack):
-        size = self.sizes["seq"]
+        full = [lax.all_gather(flat, "seq", axis=0, tiled=True).reshape(shape(flat)) for flat in flats]
+        return rearrange(full, [(rows, own)], [[in_columns(columns(q), rows)] for q in range(size)], rank)[0]
+
+    def rows_from_columns(self, value, widths, columns):
+        size, rank = self.sizes["seq"], lax.axis_index("seq")
         rows = value.shape[0]
         value = value.astype(BF)
         if rows % size == 0:
             part = rows // size
             pieces = self.relative([value[b * part : (b + 1) * part] for b in range(size)])
-            return unpack(self.relative(self.exchange_seq(pieces))).reshape(-1)
+            plans = [from_columns([columns(q ^ j) for j in range(size)], part, len(widths)) for q in range(size)]
+            out = rearrange(self.exchange_seq(pieces), [(part, w) for w in widths], plans, rank, F32)
+            return [matrix.reshape(-1) for matrix in out]
         full = lax.all_gather(value, "seq", axis=0, tiled=False)
-        full = unpack([full[b] for b in range(size)]).reshape(-1)
-        count = full.shape[0] // size
-        return lax.dynamic_slice_in_dim(full, lax.axis_index("seq") * count, count)
-
-
-def block(value, j):
-    return lax.dynamic_index_in_dim(value, lax.axis_index("dp") ^ j, 0, keepdims=False)
+        plans = [from_columns([columns(b) for b in range(size)], rows, len(widths))]
+        out = []
+        for matrix in rearrange([full[b] for b in range(size)], [(rows, w) for w in widths], plans, dtype=F32):
+            count = matrix.size // size
+            out.append(lax.dynamic_slice_in_dim(matrix.reshape(-1), rank * count, count))
+        return out
+
+
+def in_columns(columns, rows):
+    copies, place = [], 0
+    for matrix, first, count in columns:
+        copies.append((matrix, first, place, rows, count))
+        place += count
+    return copies
+
+
+def from_columns(columns_of, rows, matrices):
+    out = [[] for _ in range(matrices)]
+    for which, columns in enumerate(columns_of):
+        place = 0
+        for matrix, first, count in columns:
+            if matrix is not None:
+                out[matrix].append((which, place, first, rows, count))
+            place += count
+    return out
+
+
+def rearrange_kernel(plans, count, info, *refs):
+    inputs, outputs = refs[:count], refs[count:]
+
+    def run(plan):
+        for out, copies in zip(outputs, plan):
+            for which, first, place, rows, columns in copies:
+                if which is None:
+                    value = jnp.zeros((rows, columns), out.dtype)
+                else:
+                    value = inputs[which][:rows, first : first + columns].astype(out.dtype)
+                out[:rows, place : place + columns] = value
+
+    if len(plans) == 1:
+        run(plans[0])
+        return
+    for rank, plan in enumerate(plans):
+        pl.when(info[0] == rank)(partial(run, plan))
+
+
+def rearrange(inputs, shapes, plans, rank=0, dtype=None):
+    dtype = dtype or inputs[0].dtype
+    spec = lambda shape: pl.BlockSpec(shape, lambda i, info: (0, 0))
+    return pl.pallas_call(
+        partial(rearrange_kernel, plans, len(inputs)),
+        out_shape=[jax.ShapeDtypeStruct(shape, dtype) for shape in shapes],
+        grid_spec=pltpu.PrefetchScalarGridSpec(
+            num_scalar_prefetch=1,
+            grid=(1,),
+            in_specs=[spec(value.shape) for value in inputs],
+            out_specs=[spec(shape) for shape in shapes],
+        ),
+        compiler_params=pltpu.CompilerParams(vmem_limit_bytes=40 << 20),
+        cost_estimate=pl.CostEstimate(
+            flops=0, transcendentals=0, bytes_accessed=2 * sum(value.size * value.dtype.itemsize for value in inputs)
+        ),
+        name="rearrange",
+    )(jnp.asarray(rank, jnp.int32).reshape(1), *inputs)
 
 
 class Ring:
@@ -118,61 +182,52 @@
         total = lax.psum_scatter(value, "dp", scatter_dimension=0, tiled=True, axis_index_groups=self.groups)
         return lax.optimization_barrier(total).astype(F32)
 
-    def inward(self, value):
-        return self.blocks(value, self.order)
-
-    def outward(self, value):
-        return self.blocks(value, [self.order.index(d) for d in range(self.size)])
-
-    def blocks(self, value, order):
+    def inward(self, value, small=False):
+        return self.blocks(value, self.order, small)
+
+    def outward(self, value, small=False):
+        return self.blocks(value, [self.order.index(d) for d in range(self.size)], small)
+
+    def blocks(self, value, order, small):
         if self.groups is None:
             return value
-        part = value.shape[-1] // self.size
-        return jnp.concatenate([value[..., d * part : (d + 1) * part] for d in order], axis=-1)
-
-
-def pack_heads(value, size):
-    rows, _, width = value.shape
-    heads = width // HD
-    own = -(-heads // size)
-    value = jnp.pad(value.reshape(rows, 3, heads, HD), ((0, 0), (0, 0), (0, own * size - heads), (0, 0)))
-    out = []
-    for s in range(size):
-        part = value[:, :, s * own : (s + 1) * own]
-        even = own - own % 2
-        cols = [part[:, :, :even].reshape(rows, -1)]
-        if own % 2:
-            cols += [part[:, :, even].reshape(rows, -1), jnp.zeros((rows, HD), value.dtype)]
-        out.append(jnp.concatenate(cols, axis=1))
+        rows, width = value.shape
+        part = width // self.size
+        if small:
+            plan = [(0, d * part, k * part, rows, part) for k, d in enumerate(order)]
+            return rearrange([value], [value.shape], [[plan]])[0]
+        return jnp.concatenate([value[:, d * part : (d + 1) * part] for d in order], axis=1)
+
+
+def head_columns(index, size, width):
+    own = -(-(width // HD) // size)
+    even = own - own % 2
+
+    def heads(part, first, count):
+        start = min((index * own + first) * HD, width)
+        stop = min(start + count * HD, width)
+        out = [(0, part * width + start, stop - start), (None, 0, count * HD - stop + start)]
+        return [entry for entry in out if entry[2]]
+
+    out = [entry for part in range(3) for entry in heads(part, 0, even)]
+    if own % 2:
+        out += [entry for part in range(3) for entry in heads(part, even, 1)] + [(None, 0, HD)]
     return out
 
 
-def unpack_heads(pieces, width):
-    rows = pieces[0].shape[0]
-    heads = width // HD
-    own = -(-heads // len(pieces))
-    even = own - own % 2
-    out = []
-    for piece in pieces:
-        part = piece[:, : 3 * even * HD].reshape(rows, 3, even * HD)
-        if own % 2:
-            last = piece[:, 3 * even * HD : 3 * own * HD].reshape(rows, 3, HD)
-            part = jnp.concatenate([part, last], axis=2)
-        out.append(part)
-    return jnp.concatenate(out, axis=2)[:, :, :width].reshape(rows, 3 * width)
-
-
-def pack_hidden(value, size, order):
-    rows, hidden = value.shape
-    value = value.reshape(rows, len(order), size, hidden // (len(order) * size))
-    return [jnp.concatenate([value[:, d, s] for d in order], axis=1) for s in range(size)]
-
-
-def unpack_hidden(pieces, order):
-    rows, own = pieces[0].shape
-    part = own // len(order)
-    cut = lambda piece, k: piece[:, k * part : (k + 1) * part]
-    return jnp.concatenate([cut(piece, order.index(d)) for d in range(len(order)) for piece in pieces], axis=1)
+def hidden_columns(index, size, order, hidden):
+    part = hidden // (len(order) * size)
+    return [(0, (d * size + index) * part, part) for d in order]
+
+
+def feature_columns(index, size, order, width, matrix):
+    own, part = width // size, width // len(order)
+    out, place = [], index * own
+    while place < (index + 1) * own:
+        stop = min((index + 1) * own, (place // part + 1) * part)
+        out.append((matrix, order[place // part] * part + place % part, stop - place))
+        place = stop
+    return out
 
 
 def half_masks():
@@ -330,7 +385,7 @@
         ),
         compiler_params=pltpu.CompilerParams(vmem_limit_bytes=40 << 20),
         cost_estimate=pl.CostEstimate(
-            flops=own * span * span * 256, transcendentals=own * span * span // 2, bytes_accessed=mixed.size * 4
+            flops=own * span * span * 3400, transcendentals=0, bytes_accessed=mixed.size * 4
         ),
         name="attention_forward",
     )(info, mixed, mixed, mixed)
@@ -351,7 +406,7 @@
         ),
         compiler_params=pltpu.CompilerParams(vmem_limit_bytes=48 << 20),
         cost_estimate=pl.CostEstimate(
-            flops=own * span * span * 768, transcendentals=own * span * span // 2, bytes_accessed=mixed.size * 6
+            flops=own * span * span * 3400, transcendentals=0, bytes_accessed=mixed.size * 6
         ),
         name="attention_backward",
     )(info, mixed, mixed, mixed, grad)
@@ -376,13 +431,10 @@
 CUBIC = 0.044715
 
 
-def gelu(u):
-    return 0.5 * u * (1.0 + jnp.tanh(ROOT * (u + CUBIC * u * u * u)))
-
-
-def gelu_slope(u):
+def gelu_and_slope(u):
     t = jnp.tanh(ROOT * (u + CUBIC * u * u * u))
-    return 0.5 * (1.0 + t) + 0.5 * u * (1.0 - t * t) * ROOT * (1.0 + 3.0 * CUBIC * u * u)
+    half = 0.5 * (1.0 + t)
+    return u * half, half + 0.5 * u * (1.0 - t * t) * ROOT * (1.0 + 3.0 * CUBIC * u * u)
 
 
 def dot(a, b, dims=((1,), (0,))):
@@ -404,26 +456,32 @@
 
     links = Links(dps, size)
 
-    pack3 = lambda m: pack_heads(m.reshape(m.shape[0], 3, width), size)
     ring = Ring(dps)
-    pack_fc = lambda m: pack_hidden(m, size, ring.order)
-    unpack_fc = lambda p: unpack_hidden(p, ring.order)
+    quarter = width // size
+    columns_qkv = lambda b: head_columns(b, size, width)
+    columns_fc = lambda b: hidden_columns(b, size, ring.order, hidden)
+    columns_attention = lambda b: columns_qkv(b) + feature_columns(b, size, ring.order, width, 1)
+
+    def own_columns(value, columns):
+        count = sum(entry[2] for entry in columns(0))
+        plans = [[in_columns(columns(q), 1)] for q in range(size)]
+        return rearrange([value.reshape(1, -1)], [(1, count)], plans, rank)[0][0]
+
+    def all_columns(value, total, columns):
+        plans = []
+        for q in range(size):
+            copies = from_columns([columns(q)], 1, 1)[0]
+            for b in range(size):
+                if b != q:
+                    copies += [(None, 0, first, 1, count) for matrix, first, count in columns(b) if matrix is not None]
+            plans.append([copies])
+        return rearrange([value.reshape(1, -1)], [(1, total)], plans, rank)[0][0]
 
     split = lambda m: [m[j * count : (j + 1) * count] for j in range(size)]
 
-    aligned = unit_rows % 8 == 0 and unit_rows % size == 0
-    rows = unit_rows // size
-    if aligned:
-        starts = [rows * b // 8 * 8 for b in range(size)]
-        window = max(-(-(rows * (b + 1) - starts[b]) // 8) * 8 for b in range(size))
-        starts = [min(start, unit_rows - window) for start in starts]
-        starts = [pl.multiple_of(v, 8) for v in links.relative([jnp.int32(v) for v in starts])]
-        pieces = jnp.concatenate(links.relative(links.gather_seq(ring.inward(w_out.reshape(rows, width)))), axis=0)
-        out_part = ring.gather(lax.dynamic_slice_in_dim(pieces, starts[0], window, 0)).reshape(dps, window, width)
-    else:
-        out_part = lax.all_gather(w_out, "dp", axis=0, tiled=False)
-    qkv_part = links.columns_from_rows(w_qkv, unit_rows, pack3)
-    qkv_full = ring.gather(qkv_part)
+    attention_part = links.columns_from_rows([w_qkv, w_out], unit_rows, columns_attention)
+    attention_full = ring.gather(attention_part)
+    qkv_full, out_part = attention_full[:, :-quarter], lax.optimization_barrier(attention_full[:, -quarter:])
 
     shift = hidden // devices
     tail = -(-shift * devices // LANES) * LANES
@@ -434,107 +492,95 @@
     small = lax.dynamic_update_slice_in_dim(small, attention_vectors, device * part, 0)
     small = lax.dynamic_update_slice_in_dim(small, block_vectors, 4 * width + device * part, 0)
     small = jnp.concatenate([small, jnp.where(last, w_fc[-hidden:], jnp.zeros((), BF))])
-    small = links.all_sum(small, ("seq", "dp")).astype(F32)
-    gain1, shift1, bias_q, bias_v, bias_o, gain2, shift2, bias_p = (small[k * width : (k + 1) * width] for k in range(8))
-    gain1, shift1, bias_o, gain2, shift2, bias_p = (ring.inward(v) for v in (gain1, shift1, bias_o, gain2, shift2, bias_p))
-    bias_fc = pick(pack_fc(small[None, 8 * width :]), rank)
-    bias_qkv = pick(pack3(jnp.stack([bias_q, jnp.zeros_like(bias_q), bias_v])[None]), rank)
+    small = links.all_sum(after(small, attention_part), ("seq", "dp")).astype(F32)
+    natural = small[: 8 * width].reshape(8, width)
+    gain1, shift1, _, _, bias_o, gain2, shift2, bias_p = ring.inward(natural, small=True)
+    bias_fc = own_columns(small[8 * width :], columns_fc)
+    bias_qkv = own_columns(jnp.concatenate([natural[2], jnp.zeros_like(natural[2]), natural[3]]), columns_qkv)
 
     x_own = ring.inward(tokens[0])
-    x_all = jnp.concatenate(links.gather_seq(x_own), axis=0)
-    plain = w_fc.shape[0] - shift
-    fc_flat = lax.dynamic_slice_in_dim(jnp.concatenate([before, after(w_fc, small)]), tail - shift * device, plain)
-    fc_part = links.columns_from_rows(fc_flat, unit_rows, pack_fc)
-    fc_full = ring.gather(fc_part)
-
-    out_parts = links.gather_seq(out_part)
-
-    unit1_all, _ = normal(x_all.astype(F32))
-    h1 = (unit1_all * gain1 + shift1).astype(BF)
-    mixed = (dot(h1, qkv_full) + bias_qkv).astype(BF)
-    proj_full = ring.gather(after(ring.inward(w_proj.reshape(-1, width)), fc_part, mixed))
+    x_all = jnp.concatenate(links.gather_seq(after(x_own, attention_part)), axis=0)
     place = rank * count + jnp.arange(count)
     dy_own = ring.inward(cotangent[0]) * (place < length).astype(BF)[:, None]
     dy_wide = dy_own.astype(F32)
-    dy = jnp.concatenate(links.gather_seq(after(dy_own, mixed)), axis=0)
+    dy = jnp.concatenate(links.gather_seq(after(dy_own, small, x_all)), axis=0)
+    plain = w_fc.shape[0] - shift
+    fc_flat = lax.dynamic_slice_in_dim(jnp.concatenate([before, after(w_fc, attention_part, dy)]), tail - shift * device, plain)
+    fc_part = links.columns_from_rows([fc_flat], unit_rows, columns_fc)
+    fc_full = ring.gather(fc_part)
+
+    out_parts = links.gather_seq(out_part, free=True)
+
+    unit1_all, _ = normal(x_all.astype(F32))
+    h1 = (unit1_all * gain1 + shift1).astype(BF)
+    mixed = (dot(after(h1, dy), qkv_full) + bias_qkv).astype(BF)
+    proj_full = ring.gather(after(ring.inward(w_proj.reshape(-1, width), small=True), fc_part, mixed))
     o_heads = attention_forward(info, mixed, own, size)
     out_parts = [after(piece, mixed) for piece in out_parts]
-    if aligned:
-        out_full = jnp.zeros((dps, unit_rows, width), BF)
-        for j in range(size):
-            out_full = lax.dynamic_update_slice_in_dim(out_full, out_parts[j], starts[j], 1)
-    else:
-        out_full = jnp.stack(links.relative(out_parts), axis=1)
-    out_full = out_full.reshape(width, width)
-
     o_got = links.relative(links.exchange_seq(split(o_heads)))
     o_own = jnp.concatenate([piece[:, : own * HD] for piece in o_got], axis=1)
     o_own = ring.inward(o_own[:, :width])
-    x2 = x_own.astype(F32) + dot(o_own, out_full) + bias_o
+    projected = links.relative([dot(o_own, piece) for piece in out_parts])
+    x2 = x_own.astype(F32) + jnp.concatenate(projected, axis=1) + bias_o
     unit2, scale2 = normal(x2)
     h2 = jnp.concatenate(links.gather_seq((unit2 * gain2 + shift2).astype(BF)), axis=0)
 
     u = dot(h2, fc_full) + bias_fc
-    a = gelu(u).astype(BF)
+    a, slope = gelu_and_slope(u)
+    a, slope = a.astype(BF), slope.astype(BF)
     grad_proj = dot(a, dy, ((0,), (0,))).astype(BF)
     grad_proj_own = ring.scatter(grad_proj)
-    du = (dot(after(dy, grad_proj), proj_full, ((1,), (1,))) * gelu_slope(u)).astype(BF)
+    du = (dot(after(dy, grad_proj), proj_full, ((1,), (1,))) * slope.astype(F32)).astype(BF)
     dh2_part = dot(du, fc_full, ((1,), (1,)))
     dh2 = links.scatter_seq(split(dh2_part))
     grad_fc = dot(h2, after(du, dh2_part), ((0,), (0,))).astype(BF)
+    output_part = dot(after(a, grad_fc), proj_full)
+    dh2 = after(dh2, output_part)
     grad_fc = ring.scatter(after(grad_fc, grad_proj_own))
     dx2 = dy_wide + norm_input_grad(unit2, scale2, gain2, dh2)
     dz = dx2.astype(BF)
 
-    do_own = jnp.pad(ring.outward(dot(dz, out_full, ((1,), (1,))).astype(BF)), ((0, 0), (0, own * size * HD - width)))
+    dz_parts = links.relative([dz[:, b * quarter : (b + 1) * quarter] for b in range(size)])
+    do_own = sum(dot(dz_part, piece, ((1,), (1,))) for dz_part, piece in zip(dz_parts, out_parts))
+    do_own = jnp.pad(ring.outward(do_own.astype(BF)), ((0, 0), (0, own * size * HD - width)))
     do_blocks = [jnp.pad(do_own[:, b * own * HD : (b + 1) * own * HD], ((0, 0), (0, own % 2 * HD))) for b in range(size)]
     do_heads = jnp.concatenate(links.exchange_seq(links.relative(do_blocks)), axis=0)
-    grad_out = dot(o_own, after(dz, do_own), ((0,), (0,))).astype(BF)
-    output_part = dot(after(a, do_own), proj_full)
-    if aligned:
-        grad_out = grad_out.reshape(dps, unit_rows, width)
-        blocks = [lax.dynamic_slice_in_dim(grad_out, starts[j], window, 1) for j in range(size)]
-    else:
-        grad_out = grad_out.reshape(dps, size, -1)
-        blocks = [lax.dynamic_index_in_dim(grad_out, rank ^ j, 1, keepdims=False) for j in range(size)]
-    do_heads = after(do_heads, output_part, *blocks, grad_proj_own)
+    grad_out = [dot(after(o_own, do_own), dz_part, ((0,), (0,))).astype(BF) for dz_part in dz_parts]
+    do_heads = after(do_heads, *grad_out, grad_proj_own)
     dmixed = attention_backward(info, mixed, do_heads, own, size)
-    grad_out = after(links.scatter_seq(blocks).astype(BF), grad_fc)
-    if aligned:
-        grad_out = ring.outward(ring.scatter(grad_out.reshape(-1, width)))
-        grad_out = lax.dynamic_slice_in_dim(grad_out, rows * rank - starts[0], rows, 0)
-    else:
-        grad_out = lax.psum_scatter(grad_out, "dp", scatter_dimension=0, tiled=True).astype(F32)
+    grad_out = links.scatter_seq(grad_out, dmixed, free=True).astype(BF)
     grad_qkv = dot(h1, after(dmixed, grad_fc), ((0,), (0,))).astype(BF)
-    grad_qkv_own = ring.scatter(grad_qkv)
-    dh1_part = dot(after(dmixed, grad_qkv), qkv_full, ((1,), (1,)))
-    output = ring.outward((x2 + links.scatter_seq(split(output_part)) + bias_p).astype(BF))
+    grad_attention = jnp.concatenate([grad_qkv, grad_out], axis=1)
+    dmixed = after(dmixed, grad_attention)
+    grad_attention = ring.scatter(grad_attention)
+    dh1_part = dot(dmixed, qkv_full, ((1,), (1,)))
+    output = ring.outward((x2 + links.scatter_seq(split(after(output_part, dmixed)), free=True) + bias_p).astype(BF))
     dh1 = links.scatter_seq(split(dh1_part))
-    fc_rows = links.rows_from_columns(grad_fc, unpack_fc)
-    behind = links.shift(fc_rows[:tail], -1)
+    fc_rows = links.rows_from_columns(grad_fc, [hidden], columns_fc)[0]
+    behind = links.shift(fc_rows[:tail].astype(BF), -1)
     unit1, scale1 = normal(x_own.astype(F32))
     input_grad = ring.outward(dx2 + norm_input_grad(unit1, scale1, gain1, dh1))
 
     total = lambda m: jnp.sum(m.astype(F32), axis=0)
-    own_sum = lambda m: ring.outward(total(m))
-    place_cols = lambda v, unpack: unpack([jnp.where(rank == b, v, 0.0)[None] for b in range(size)])[0]
-    wide = place_cols(total(dmixed), lambda p: unpack_heads(p, width)).reshape(3, width)
-    wide_bf = place_cols(total(du), unpack_fc)
+    wide = all_columns(total(dmixed), 3 * width, columns_qkv)
+    inner = [total(dh1_part * unit1_all), total(dh1_part), total(dz), total(dh2 * unit2), total(dh2), total(dy_wide)]
+    grad_g1, grad_c1, grad_bo, grad_g2, grad_c2, grad_bp = ring.outward(jnp.stack(inner), small=True)
     sums = jnp.concatenate([
-        own_sum(dh1_part * unit1_all), own_sum(dh1_part), wide[0], wide[2],
-        own_sum(dz), own_sum(dh2 * unit2), own_sum(dh2), own_sum(dy_wide), wide_bf,
+        grad_g1, grad_c1, wide[:width], wide[2 * width :], grad_bo, grad_g2, grad_c2, grad_bp,
+        all_columns(total(du), hidden, columns_fc),
     ])
-    sums = links.all_sum(sums, ("seq", "dp"))
+    sums = links.all_sum(sums, ("seq", "dp"), free=True)
     vec1 = lax.dynamic_slice_in_dim(sums[: 4 * width], device * part, part)
     vec2 = lax.dynamic_slice_in_dim(sums[4 * width : 8 * width], device * part, part)
     sum_bf = sums[8 * width :]
 
-    qkv_flat = links.rows_from_columns(grad_qkv_own, lambda p: unpack_heads(p, width)).astype(F32)
     behind = jnp.where(last, jnp.pad(sum_bf, (0, tail - hidden)), behind.astype(F32))
     fc_flat_grad = lax.dynamic_slice_in_dim(
-        jnp.concatenate([fc_rows.astype(F32), behind]), shift * device, w_fc.shape[0]
+        jnp.concatenate([fc_rows, behind]), shift * device, w_fc.shape[0]
     )
-    return (output[None], input_grad[None], qkv_flat, grad_out.reshape(-1), fc_flat_grad, ring.outward(grad_proj_own).reshape(-1), vec1, vec2)
+    grad_attention = after(grad_attention, input_grad, fc_flat_grad, vec1, vec2, output)
+    qkv_flat, out_flat = links.rows_from_columns(grad_attention, [3 * width, width], columns_attention)
+    return (output[None], input_grad[None], qkv_flat, out_flat, fc_flat_grad, ring.outward(grad_proj_own, small=True).reshape(-1), vec1, vec2)
 
 
 def solution(mesh):

time: 585 us -> 514 us (0.88)
  waiting for transfers between devices: 193 us -> 146 us
  local copies, waits for them, and re-layouts: 112 us -> 67.9 us
  other arithmetic: 47.8 us -> 62.3 us
  matrix products: 111 us -> 117 us
    ppermute x55 -> x20, waiting for transfers between devices: 181 us -> 75.2 us  [swap(): lax.ppermute(v, axis, pairs)]
    ppermute x0 -> x32, waiting for transfers between devices: none -> 70.6 us  [swap(): return lax.ppermute(value, axis, pairs)]
    ppermute x55 -> x20, starting transfers between devices: 43 us -> 11.5 us  [swap(): lax.ppermute(v, axis, pairs)]
    ppermute x0 -> x32, starting transfers between devices: none -> 26.8 us  [swap(): return lax.ppermute(value, axis, pairs)]
    slice x64 -> x11, local copies, waits for them, and re-layouts: 24.8 us -> 5.86 us  [the longest x4 3.29 us: blocks(): value[:, d * part:(d + 1) * part]]
    concatenate x47 -> x10, local copies, waits for them, and re-layouts: 23.2 us -> 9.3 us  [the longest x6 6.88 us: blocks(): jnp.concatenate([value[:, d * part:(d + 1) * part] for d in order], axis=1)]
    unnamed x12 -> x8, waiting for transfers between devices: 11 us -> 0.1 us
    unnamed x250 -> x164, local copies, waits for them, and re-layouts: 34.2 us -> 23.9 us
  transfers between devices with their start and end apart: 65 -> 60, of which waited for: 30 -> 30; matrix products, arithmetic and copies ran while one was open for 44% -> 46% of each run, Pallas kernels for 8% -> 10%
where the time goes in v3:
time: 514 us; the launch traced here: 505 us
  waiting for transfers between devices  146 us (28%)
  matrix products  117 us (23%)
  local copies, waits for them, and re-layouts  67.9 us (13%)
  other arithmetic  62.3 us (12%)
  Pallas kernels  52 us (10%)
  starting transfers between devices  43.5 us (8%)
  between operations  16.3 us (3%)
    dot_general x21, matrix products, dot(): return lax.dot_general(a, b, (dims, ((), ())), preferred_element_type=F32)  117 us
    ppermute x20, waiting for transfers between devices, swap(): lax.ppermute(v, axis, pairs)  75.2 us
    ppermute x32, waiting for transfers between devices, swap(): return lax.ppermute(value, axis, pairs)  70.6 us
    pallas_call x1, Pallas kernels, attention_backward(): pl.pallas_call(partial(attention_backward_kernel, size, pairs, odd), out_...  27.2 us
    ppermute x32, starting transfers between devices, swap(): return lax.ppermute(value, axis, pairs)  26.8 us
    unnamed x164, local copies, waits for them, and re-layouts  23.9 us
    pallas_call x1, Pallas kernels, attention_forward(): pl.pallas_call(partial(attention_forward_kernel, size, pairs, odd), out_s...  20.9 us
    ppermute x20, starting transfers between devices, swap(): lax.ppermute(v, axis, pairs)  11.5 us
  transfers between devices with their start and end apart: 60, of which 30 were waited for; matrix products, arithmetic and copies ran while one was open for 46% of the time, Pallas kernels for 10%

profile of v3, /device:TPU:0, one launch (start us, length us, event | category | flops | bytes accessed | tf_op | source)
XLA Modules:
  0.0 505.5 jit_solution(7455164753540638839)
XLA Ops:
  40.8 4.0 collective-permute-done.9
  52.4 4.7 collective-permute-done.7
  62.7 18.3 %collective-permute-done.13 = bf16[256,1600]{0,1:T(8,128)(2,1)S(1)} collective-permute-done((bf16[256,1600]{0,1:T(8,128)(2,1)S(1)}, bf16[256,1600]{0,1:T(8,128)(2,1)S(1)}, u32[]{:S(2)}, u32[]{:S(2)}) %collective-permute-start.13) | collective-permute-done | bytes 819232 | tf_op jit(solution)/shard_map/ppermute | solution.py:47
  90.8 4.8 collective-permute-done.24
  95.6 4.3 collective-permute-done.25
  109.6 4.0 fusion.5
  118.4 10.1 %add_convert_fusion.q_ref.k_ref.v_ref = bf16[1024,1408]{1,0:T(8,128)(2,1)} fusion(bf16[1024,1600]{0,1:T(8,128)(2,1)} %fusion.5, bf16[1600,1808]{1,0:T(8,128)(2,1)} %all-gather.4.cloned.1.call-done, f32[1408]{0:T(1024)S(1)} %reduce.2), kind=kOutput, calls=%fused_computation.27 | convolution fusion | flops 4616617984 | bytes 10671616 | tf_op jit(solution)/shard_map/dot_general | solution.py:441
  130.8 20.9 %attention_forward.1 = bf16[1024,512]{1,0:T(8,128)(2,1)S(1)} custom-call(s32[2]{0:T(128)S(1)} %pad_add_fusion.info, bf16[1024,1408]{1,0:T(8,128)(2,1)S(1)} %copy-done.2, bf16[1024,1408]{1,0:T(8,128)(2,1)S(1)} %copy-done.2, bf16[1024,1408]{1,0:T(8,128)(2,1)S(1)} %copy-done.2), custom_call_target="tpu_custom_call" | custom-call | flops 24956108800 | bytes 5767168 | tf_op jit(solution)/shard_map/attention_forward/pallas_call | solution.py:376
  154.3 6.7 %collective-permute-done.16 = bf16[256,512]{1,0:T(8,128)(2,1)S(1)} collective-permute-done((bf16[256,512]{1,0:T(8,128)(2,1)S(1)}, bf16[256,512]{1,0:T(8,128)(2,1)S(1)}, u32[]{:S(2)}, u32[]{:S(2)}) %collective-permute-start.16) | collective-permute-done | bytes 262176 | tf_op jit(solution)/shard_map/ppermute | solution.py:45
  161.0 4.7 collective-permute-done.15
  182.7 18.4 %collective-permute-done.22 = bf16[256,1600]{0,1:T(8,128)(2,1)} collective-permute-done((bf16[256,1600]{0,1:T(8,128)(2,1)S(1)}, bf16[256,1600]{0,1:T(8,128)(2,1)}, u32[]{:S(2)}, u32[]{:S(2)}) %collective-permute-start.22) | collective-permute-done | bytes 819232 | tf_op jit(solution)/shard_map/ppermute | solution.py:47
  203.8 13.3 %multiply_convert_fusion.1 = (bf16[1024,1600]{0,1:T(8,128)(2,1)S(1)}, f32[1024,1600]{0,1:T(8,128)}) fusion(f32[1600]{0:T(1024)S(1)} %reduce.6, bf16[1600,1600]{1,0:T(8,128)(2,1)} %all-gather.6.cloned.1.call-done, bf16[256,1600]{0,1:T(8,128)(2,1)} %collective-permute-done.23, bf16[256,1600]{0,1:T(8,128)(2,1)} %collective-permute-done.22, ...), kind=kOutput, calls=%fused_computation.23 | convolution fusion | flops 5272371200 | bytes 18233600 | tf_op jit(solution)/shard_map/dot_general | solution.py:441
  218.8 7.9 %convolution_convert_fusion.2 = bf16[1600,1600]{1,0:T(8,128)(2,1)} fusion(bf16[1024,1600]{0,1:T(8,128)(2,1)S(1)} %get-tuple-element.86, bf16[1024,1600]{0,1:T(8,128)(2,1)S(1)} %copy-done.33), kind=kOutput, calls=%fused_computation.8 | convolution fusion | flops 5245440000 | bytes 11673600 | tf_op jit(solution)/shard_map/dot_general | solution.py:441
  227.0 14.6 %convert_reduce_fusion.1 = (f32[1600]{0:T(1024)S(1)}, bf16[1024,1600]{0,1:T(8,128)(2,1)S(1)}) fusion(f32[1024,1600]{0,1:T(8,128)} %get-tuple-element.196, f32[1600]{0:T(1024)S(1)} %reduce.6, bf16[1600,1600]{1,0:T(8,128)(2,1)} %all-gather.8.cloned.1.call-done, bf16[1024,1600]{0,1:T(8,128)(2,1)} %copy-done.32), kind=kOutput, calls=%fused_computation.21 | convolution fusion | flops 5282200064 | bytes 18240000 | tf_op jit(solution)/shard_map/dot_general | solution.py:441
  241.6 9.7 %fusion.67 = (bf16[1024,1600]{0,1:T(8,128)(2,1)S(1)}, f32[1024,1600]{0,1:T(8,128)}) fusion(bf16[1600,1600]{1,0:T(8,128)(2,1)} %all-gather.6.cloned.1.call-done, bf16[1024,1600]{0,1:T(8,128)(2,1)S(1)} %get-tuple-element.85), kind=kOutput, calls=%fused_computation.221 | convolution fusion | flops 5244518400 | bytes 18227200 | tf_op jit(solution)/shard_map/dot_general | solution.py:441
  253.1 10.2 %convolution_convert_fusion.1 = bf16[1600,1600]{1,0:T(8,128)(2,1)} fusion(bf16[1024,1600]{0,1:T(8,128)(2,1)S(1)} %get-tuple-element.85, bf16[256,1600]{0,1:T(8,128)(2,1)} %collective-permute-done.23, bf16[256,1600]{0,1:T(8,128)(2,1)} %collective-permute-done.22, bf16[256,1600]{0,1:T(8,128)(2,1)S(1)} %copy-done.62, bf16[256,1600]{0,1:T(8,128)(2,1)S(1)} %copy-done.28), kind=kOutput, calls=%fused_computation.7 | convolution fusion | flops 5258547200 | bytes 11673600 | tf_op jit(solution)/shard_map/dot_general | solution.py:441
  267.3 10.9 %fusion.71 = f32[1024,1600]{0,1:T(8,128)} fusion(bf16[1024,1600]{0,1:T(8,128)(2,1)S(1)} %copy-done.66, bf16[1600,1600]{1,0:T(8,128)(2,1)} %all-gather.8.cloned.1.call-done), kind=kOutput, calls=%fused_computation.225 | convolution fusion | flops 5242880000 | bytes 14950400 | tf_op jit(solution)/shard_map/dot_general | solution.py:441
  279.0 7.4 %collective-permute-done.29 = bf16[256,1600]{0,1:T(8,128)(2,1)S(1)} collective-permute-done((bf16[256,1600]{0,1:T(8,128)(2,1)}, bf16[256,1600]{0,1:T(8,128)(2,1)S(1)}, u32[]{:S(2)}, u32[]{:S(2)}) %collective-permute-start.29) | collective-permute-done | bytes 819232 | tf_op jit(solution)/shard_map/ppermute | solution.py:47
  317.5 5.4 %collective-permute-done.31 = bf16[256,512]{1,0:T(8,128)(2,1)S(1)} collective-permute-done((bf16[256,512]{1,0:T(8,128)(2,1)S(1)}, bf16[256,512]{1,0:T(8,128)(2,1)S(1)}, u32[]{:S(2)}, u32[]{:S(2)}) %collective-permute-start.31) | collective-permute-done | bytes 262176 | tf_op jit(solution)/shard_map/ppermute | solution.py:45
  322.9 3.9 collective-permute-done.32
  330.1 27.2 %attention_backward.1 = bf16[1024,1408]{1,0:T(8,128)(2,1)S(1)} custom-call(s32[2]{0:T(128)S(1)} %pad_add_fusion.info, bf16[1024,1408]{1,0:T(8,128)(2,1)} %add_convert_fusion.q_ref.k_ref.v_ref, bf16[1024,1408]{1,0:T(8,128)(2,1)} %add_convert_fusion.q_ref.k_ref.v_ref, bf16[1024,1408]{1,0:T(8,128)(2,1)} %add_convert_fusion.q_ref.k_ref.v_ref, ...), custom_call_target="tpu_custom_call" | custom-call | flops 24956108800 | bytes 8650752 | tf_op jit(solution)/shard_map/attention_backward/pallas_call | solution.py:397
  362.5 3.4 copy.31
  365.9 8.0 %convolution_convert_fusion = bf16[1600,1408]{1,0:T(8,128)(2,1)S(1)} fusion(bf16[1024,1600]{0,1:T(8,128)(2,1)} %fusion.5, bf16[1024,1408]{1,0:T(8,128)(2,1)} %copy-done), kind=kOutput, calls=%fused_computation.6 | convolution fusion | flops 4615987200 | bytes 10665984 | tf_op jit(solution)/shard_map/dot_general | solution.py:441
  379.8 11.5 %fusion.51 = (f32[1600]{0:T(1024)S(1)}, f32[1600]{0:T(1024)S(1)}, bf16[1024,1600]{0,1:T(8,128)(2,1)}, f32[1024,1600]{0,1:T(8,128)}) fusion(f32[1024]{0:T(1024)S(1)} %copy-done.52, f32[1024]{0:T(1024)S(1)} %copy-done.39, bf16[1024,1600]{0,1:T(8,128)(2,1)} %constant_dynamic-update-slice_fusion, bf16[1024,1408]{1,0:T(8,128)(2,1)S(1)} %copy-done.1, ...), kind=kOutput, calls=%fused_computation.209 | convolution fusion | flops 4625200128 | bytes 20517376 | tf_op jit(solution)/shard_map/dot_general | solution.py:441
  395.7 3.4 convert.16
  405.5 4.3 collective-permute-done.47
  422.3 12.6 %collective-permute-done.41 = bf16[256,1600]{0,1:T(8,128)(2,1)} collective-permute-done((bf16[256,1600]{0,1:T(8,128)(2,1)}, bf16[256,1600]{0,1:T(8,128)(2,1)}, u32[]{:S(2)}, u32[]{:S(2)}) %collective-permute-start.41) | collective-permute-done | bytes 819232 | tf_op jit(solution)/shard_map/ppermute | solution.py:47
  437.6 13.7 %collective-permute-done.38 = bf16[256,1600]{0,1:T(8,128)(2,1)S(1)} collective-permute-done((bf16[256,1600]{0,1:T(8,128)(2,1)S(1)}, bf16[256,1600]{0,1:T(8,128)(2,1)S(1)}, u32[]{:S(2)}, u32[]{:S(2)}) %collective-permute-start.38) | collective-permute-done | bytes 819232 | tf_op jit(solution)/shard_map/ppermute | solution.py:45
  467.3 3.3 collective-permute-done.43.refs_2_
  476.7 3.3 fusion.33
  487.7 3.3 collective-permute-done.53.refs_3_
  491.0 4.7 collective-permute-done.52.refs_2_
  (414 shorter events, 206.0 us)
Async XLA Ops:
  7.2 106.5 %all-gather.4.cloned.1.call-start = ((), (), s32[]{:S(2)}) async-start(), calls=%async_computation.3 | async-start | bytes 6912000 | tf_op jit(solution)/shard_map/all_gather | solution.py:179
  8.7 26.0 %collective-permute-start.4 = (bf16[6400]{0:T(1024)(128)(2,1)}, bf16[6400]{0:T(1024)(128)(2,1)}, u32[]{:S(2)}, u32[]{:S(2)}) collective-permute-start(bf16[6400]{0:T(1024)(128)(2,1)} %get-tuple-element.184), channel_id=1, source_target_pairs={{0,1},{1,2},{2,3},{3,4},{4,5},{5,6},{6,7},{7,8},{8,9},{9,10},{10,1... | collective-permute-start | bytes 38408 | tf_op jit(solution)/shard_map/ppermute | solution.py:52
  14.6 12.4 %collective-permute-start = (bf16[50,1808]{1,0:T(8,128)(2,1)S(1)}, bf16[50,1808]{1,0:T(8,128)(2,1)S(1)}, u32[]{:S(2)}, u32[]{:S(2)}) collective-permute-start(bf16[50,1808]{1,0:T(8,128)(2,1)S(1)} %get-tuple-element.56), channel_id=1, source_target_pairs={{0,3},{1,2},{2,1},{3,0},{4,7},{5,6},{6,5},{7,4},{8,11},{9,10},{10,... | collective-permute-start | bytes 542408 | tf_op jit(solution)/shard_map/ppermute | solution.py:45
  17.7 10.6 %collective-permute-start.1 = (bf16[50,1808]{1,0:T(8,128)(2,1)S(1)}, bf16[50,1808]{1,0:T(8,128)(2,1)}, u32[]{:S(2)}, u32[]{:S(2)}) collective-permute-start(bf16[50,1808]{1,0:T(8,128)(2,1)S(1)} %get-tuple-element.57), channel_id=1, source_target_pairs={{0,2},{1,3},{2,0},{3,1},{4,6},{5,7},{6,4},{7,5},{8,10},{9,11},{10,... | collective-permute-start | bytes 542408 | tf_op jit(solution)/shard_map/ppermute | solution.py:45
  30.6 172.5 %all-gather.6.cloned.1.call-start = ((), (), s32[]{:S(2)}) async-start(), calls=%async_computation.4 | async-start | bytes 5990400 | tf_op jit(solution)/shard_map/all_gather | solution.py:179
  36.4 20.7 %collective-permute-start.7 = (bf16[256,1600]{0,1:T(8,128)(2,1)S(1)}, bf16[256,1600]{0,1:T(8,128)(2,1)S(1)}, u32[]{:S(2)}, u32[]{:S(2)}) collective-permute-start(bf16[256,1600]{0,1:T(8,128)(2,1)S(1)} %slice_dynamic-update-slice_fusion.22), channel_id=1, source_target_pairs={{0,2},{1,3},{2,0},{3,1},{4,6},{5,7},{6,4},{7,5},{8,10},{9,11},{10,... | collective-permute-start | bytes 2457608 | tf_op jit(solution)/shard_map/ppermute | solution.py:47
  37.0 20.1 %collective-permute-start.6 = (bf16[256,1600]{0,1:T(8,128)(2,1)S(1)}, bf16[256,1600]{0,1:T(8,128)(2,1)S(1)}, u32[]{:S(2)}, u32[]{:S(2)}) collective-permute-start(bf16[256,1600]{0,1:T(8,128)(2,1)S(1)} %slice_dynamic-update-slice_fusion.22), channel_id=1, source_target_pairs={{0,1},{1,0},{2,3},{3,2},{4,5},{5,4},{6,7},{7,6},{8,9},{9,8},{10,11... | collective-permute-start | bytes 2457608 | tf_op jit(solution)/shard_map/ppermute | solution.py:47
  60.7 20.4 %collective-permute-start.13 = (bf16[256,1600]{0,1:T(8,128)(2,1)S(1)}, bf16[256,1600]{0,1:T(8,128)(2,1)S(1)}, u32[]{:S(2)}, u32[]{:S(2)}) collective-permute-start(bf16[256,1600]{0,1:T(8,128)(2,1)S(1)} %get-tuple-element.68), channel_id=1, source_target_pairs={{0,2},{1,3},{2,0},{3,1},{4,6},{5,7},{6,4},{7,5},{8,10},{9,11},{10,... | collective-permute-start | bytes 2457608 | tf_op jit(solution)/shard_map/ppermute | solution.py:47
  89.3 10.7 %collective-permute-start.25 = (bf16[50,1600]{1,0:T(8,128)(2,1)S(1)}, bf16[50,1600]{1,0:T(8,128)(2,1)S(1)}, u32[]{:S(2)}, u32[]{:S(2)}) collective-permute-start(bf16[50,1600]{1,0:T(8,128)(2,1)S(1)} %get-tuple-element.80), channel_id=1, source_target_pairs={{0,2},{1,3},{2,0},{3,1},{4,6},{5,7},{6,4},{7,5},{8,10},{9,11},{10,... | collective-permute-start | bytes 480008 | tf_op jit(solution)/shard_map/ppermute | solution.py:45
  101.1 125.9 %all-gather.8.cloned.1.call-start = ((), (), s32[]{:S(2)}) async-start(), calls=%async_computation.5 | async-start | bytes 5990400 | tf_op jit(solution)/shard_map/all_gather | solution.py:179
  117.6 48.2 %collective-permute-start.18 = (bf16[1600,400]{0,1:T(8,128)(2,1)}, bf16[1600,400]{0,1:T(8,128)(2,1)}, u32[]{:S(2)}, u32[]{:S(2)}) collective-permute-start(bf16[1600,400]{0,1:T(8,128)(2,1)} %copy.25), channel_id=1, source_target_pairs={{0,2},{1,3},{2,0},{3,1},{4,6},{5,7},{6,4},{7,5},{8,10},{9,11},{10,... | collective-permute-start | bytes 3840008 | tf_op jit(solution)/shard_map/ppermute | solution.py:45
  128.6 168.6 %reduce-scatter.13.cloned.1.call-start = ((), (), s32[]{:S(2)}) async-start(), calls=%async_computation.6 | async-start | bytes 5990400
  153.0 12.7 %collective-permute-start.15 = (bf16[256,512]{1,0:T(8,128)(2,1)S(1)}, bf16[256,512]{1,0:T(8,128)(2,1)S(1)}, u32[]{:S(2)}, u32[]{:S(2)}) collective-permute-start(bf16[256,512]{1,0:T(8,128)(2,1)S(1)} %get-tuple-element.156), channel_id=1, source_target_pairs={{0,3},{1,2},{2,1},{3,0},{4,7},{5,6},{6,5},{7,4},{8,11},{9,10},{10,... | collective-permute-start | bytes 786440 | tf_op jit(solution)/shard_map/ppermute | solution.py:45
  153.9 18.7 %collective-permute-start.20 = (bf16[1600,400]{0,1:T(8,128)(2,1)}, bf16[1600,400]{0,1:T(8,128)(2,1)}, u32[]{:S(2)}, u32[]{:S(2)}) collective-permute-start(bf16[1600,400]{0,1:T(8,128)(2,1)} %copy.25), channel_id=1, source_target_pairs={{0,1},{1,0},{2,3},{3,2},{4,5},{5,4},{6,7},{7,6},{8,9},{9,8},{10,11... | collective-permute-start | bytes 3840008 | tf_op jit(solution)/shard_map/ppermute | solution.py:45
  165.8 10.6 %collective-permute-start.19 = (bf16[1600,400]{0,1:T(8,128)(2,1)}, bf16[1600,400]{0,1:T(8,128)(2,1)}, u32[]{:S(2)}, u32[]{:S(2)}) collective-permute-start(bf16[1600,400]{0,1:T(8,128)(2,1)} %collective-permute-done.18), channel_id=1, source_target_pairs={{0,1},{1,0},{2,3},{3,2},{4,5},{5,4},{6,7},{7,6},{8,9},{9,8},{10,11... | collective-permute-start | bytes 3840008 | tf_op jit(solution)/shard_map/ppermute | solution.py:45
  180.6 20.5 %collective-permute-start.22 = (bf16[256,1600]{0,1:T(8,128)(2,1)S(1)}, bf16[256,1600]{0,1:T(8,128)(2,1)}, u32[]{:S(2)}, u32[]{:S(2)}) collective-permute-start(bf16[256,1600]{0,1:T(8,128)(2,1)S(1)} %add_convert_fusion.5), channel_id=1, source_target_pairs={{0,2},{1,3},{2,0},{3,1},{4,6},{5,7},{6,4},{7,5},{8,10},{9,11},{10,... | collective-permute-start | bytes 2457608 | tf_op jit(solution)/shard_map/ppermute | solution.py:47
  226.7 232.1 %reduce-scatter.17.cloned.1.call-start = ((), (), s32[]{:S(2)}) async-start(), calls=%async_computation.8 | async-start | bytes 5990400
  252.4 10.9 %collective-permute-start.27 = (bf16[256,1600]{0,1:T(8,128)(2,1)S(1)}, bf16[256,1600]{0,1:T(8,128)(2,1)}, u32[]{:S(2)}, u32[]{:S(2)}) collective-permute-start(bf16[256,1600]{0,1:T(8,128)(2,1)S(1)} %get-tuple-element.87), channel_id=1, source_target_pairs={{0,1},{1,0},{2,3},{3,2},{4,5},{5,4},{6,7},{7,6},{8,9},{9,8},{10,11... | collective-permute-start | bytes 2457608 | tf_op jit(solution)/shard_map/ppermute | solution.py:47
  266.2 20.3 %collective-permute-start.29 = (bf16[256,1600]{0,1:T(8,128)(2,1)}, bf16[256,1600]{0,1:T(8,128)(2,1)S(1)}, u32[]{:S(2)}, u32[]{:S(2)}) collective-permute-start(bf16[256,1600]{0,1:T(8,128)(2,1)} %fusion.31), channel_id=1, source_target_pairs={{0,2},{1,3},{2,0},{3,1},{4,6},{5,7},{6,4},{7,5},{8,10},{9,11},{10,... | collective-permute-start | bytes 2457608 | tf_op jit(solution)/shard_map/ppermute | solution.py:47
  267.3 19.1 %collective-permute-start.28 = (bf16[256,1600]{0,1:T(8,128)(2,1)}, bf16[256,1600]{0,1:T(8,128)(2,1)}, u32[]{:S(2)}, u32[]{:S(2)}) collective-permute-start(bf16[256,1600]{0,1:T(8,128)(2,1)} %get-tuple-element.88), channel_id=1, source_target_pairs={{0,1},{1,0},{2,3},{3,2},{4,5},{5,4},{6,7},{7,6},{8,9},{9,8},{10,11... | collective-permute-start | bytes 2457608 | tf_op jit(solution)/shard_map/ppermute | solution.py:47
  298.4 181.6 %reduce-scatter.15.cloned.1.call-start = ((), (), s32[]{:S(2)}) async-start(), calls=%async_computation.7 | async-start | bytes 6912000
  303.5 23.4 %collective-permute-start.34 = (bf16[1600,400]{0,1:T(8,128)(2,1)}, bf16[1600,400]{0,1:T(8,128)(2,1)}, u32[]{:S(2)}, u32[]{:S(2)}) collective-permute-start(bf16[1600,400]{0,1:T(8,128)(2,1)} %convolution_convert_fusion.3), channel_id=1, source_target_pairs={{0,1},{1,0},{2,3},{3,2},{4,5},{5,4},{6,7},{7,6},{8,9},{9,8},{10,11... | collective-permute-start | bytes 3840008 | tf_op jit(solution)/shard_map/ppermute | solution.py:45
  315.4 11.4 %collective-permute-start.32 = (bf16[256,512]{1,0:T(8,128)(2,1)S(1)}, bf16[256,512]{1,0:T(8,128)(2,1)S(1)}, u32[]{:S(2)}, u32[]{:S(2)}) collective-permute-start(bf16[256,512]{1,0:T(8,128)(2,1)S(1)} %select_select_fusion.4), channel_id=1, source_target_pairs={{0,3},{1,2},{2,1},{3,0},{4,7},{5,6},{6,5},{7,4},{8,11},{9,10},{10,... | collective-permute-start | bytes 786440 | tf_op jit(solution)/shard_map/ppermute | solution.py:45
  316.2 44.7 %collective-permute-start.33 = (bf16[1600,400]{0,1:T(8,128)(2,1)S(1)}, bf16[1600,400]{0,1:T(8,128)(2,1)S(1)}, u32[]{:S(2)}, u32[]{:S(2)}) collective-permute-start(bf16[1600,400]{0,1:T(8,128)(2,1)S(1)} %convolution_convert_fusion.5), channel_id=1, source_target_pairs={{0,1},{1,0},{2,3},{3,2},{4,5},{5,4},{6,7},{7,6},{8,9},{9,8},{10,11... | collective-permute-start | bytes 3840008 | tf_op jit(solution)/shard_map/ppermute | solution.py:45
  328.8 32.1 %collective-permute-start.35 = (bf16[1600,400]{0,1:T(8,128)(2,1)S(1)}, bf16[1600,400]{0,1:T(8,128)(2,1)S(1)}, u32[]{:S(2)}, u32[]{:S(2)}) collective-permute-start(bf16[1600,400]{0,1:T(8,128)(2,1)S(1)} %add_convert_fusion.2), channel_id=1, source_target_pairs={{0,2},{1,3},{2,0},{3,1},{4,6},{5,7},{6,4},{7,5},{8,10},{9,11},{10,... | collective-permute-start | bytes 3840008 | tf_op jit(solution)/shard_map/ppermute | solution.py:45
  394.0 16.6 %collective-permute-start.39 = (bf16[256,1600]{0,1:T(8,128)(2,1)S(1)}, bf16[256,1600]{0,1:T(8,128)(2,1)}, u32[]{:S(2)}, u32[]{:S(2)}) collective-permute-start(bf16[256,1600]{0,1:T(8,128)(2,1)S(1)} %get-tuple-element.96), channel_id=1, source_target_pairs={{0,1},{1,0},{2,3},{3,2},{4,5},{5,4},{6,7},{7,6},{8,9},{9,8},{10,11... | collective-permute-start | bytes 2457608 | tf_op jit(solution)/shard_map/ppermute | solution.py:47
  400.4 17.2 %collective-permute-start.37 = (bf16[256,1600]{0,1:T(8,128)(2,1)}, bf16[256,1600]{0,1:T(8,128)(2,1)}, u32[]{:S(2)}, u32[]{:S(2)}) collective-permute-start(bf16[256,1600]{0,1:T(8,128)(2,1)} %get-tuple-element.139), channel_id=1, source_target_pairs={{0,1},{1,0},{2,3},{3,2},{4,5},{5,4},{6,7},{7,6},{8,9},{9,8},{10,11... | collective-permute-start | bytes 2457608 | tf_op jit(solution)/shard_map/ppermute | solution.py:45
  413.4 21.5 %collective-permute-start.41 = (bf16[256,1600]{0,1:T(8,128)(2,1)}, bf16[256,1600]{0,1:T(8,128)(2,1)}, u32[]{:S(2)}, u32[]{:S(2)}) collective-permute-start(bf16[256,1600]{0,1:T(8,128)(2,1)} %fusion.28), channel_id=1, source_target_pairs={{0,2},{1,3},{2,0},{3,1},{4,6},{5,7},{6,4},{7,5},{8,10},{9,11},{10,... | collective-permute-start | bytes 2457608 | tf_op jit(solution)/shard_map/ppermute | solution.py:47
  414.5 20.4 %collective-permute-start.40 = (bf16[256,1600]{0,1:T(8,128)(2,1)}, bf16[256,1600]{0,1:T(8,128)(2,1)}, u32[]{:S(2)}, u32[]{:S(2)}) collective-permute-start(bf16[256,1600]{0,1:T(8,128)(2,1)} %get-tuple-element.97), channel_id=1, source_target_pairs={{0,1},{1,0},{2,3},{3,2},{4,5},{5,4},{6,7},{7,6},{8,9},{9,8},{10,11... | collective-permute-start | bytes 2457608 | tf_op jit(solution)/shard_map/ppermute | solution.py:47
  414.5 23.0 %collective-permute-start.36 = (bf16[256,1600]{0,1:T(8,128)(2,1)}, bf16[256,1600]{0,1:T(8,128)(2,1)S(1)}, u32[]{:S(2)}, u32[]{:S(2)}) collective-permute-start(bf16[256,1600]{0,1:T(8,128)(2,1)} %get-tuple-element.138), channel_id=1, source_target_pairs={{0,1},{1,0},{2,3},{3,2},{4,5},{5,4},{6,7},{7,6},{8,9},{9,8},{10,11... | collective-permute-start | bytes 2457608 | tf_op jit(solution)/shard_map/ppermute | solution.py:45
  419.4 31.8 %collective-permute-start.38 = (bf16[256,1600]{0,1:T(8,128)(2,1)S(1)}, bf16[256,1600]{0,1:T(8,128)(2,1)S(1)}, u32[]{:S(2)}, u32[]{:S(2)}) collective-permute-start(bf16[256,1600]{0,1:T(8,128)(2,1)S(1)} %add_convert_fusion.4), channel_id=1, source_target_pairs={{0,2},{1,3},{2,0},{3,1},{4,6},{5,7},{6,4},{7,5},{8,10},{9,11},{10,... | collective-permute-start | bytes 2457608 | tf_op jit(solution)/shard_map/ppermute | solution.py:45
  485.3 10.4 %collective-permute-start.52 = (bf16[50,1808]{1,0:T(8,128)(2,1)}, bf16[50,1808]{1,0:T(8,128)(2,1)S(1)}, u32[]{:S(2)}, u32[]{:S(2)}) collective-permute-start(bf16[50,1808]{1,0:T(8,128)(2,1)} %get-tuple-element.175), channel_id=1, source_target_pairs={{0,2},{1,3},{2,0},{3,1},{4,6},{5,7},{6,4},{7,5},{8,10},{9,11},{10,... | collective-permute-start | bytes 542408 | tf_op jit(solution)/shard_map/ppermute | solution.py:45
  (95 other events, 955.9 us)
Sparse Core Ops, SparseCore 0:
  30.7 67.2 all-gather.3
  101.2 57.9 all-gather.5
  160.7 58.5 all-gather.7
  226.9 60.0 reduce-scatter.12
  298.6 60.0 reduce-scatter.16
  405.7 66.8 reduce-scatter.14

commit v4 on v3

--- a/solution.py
+++ b/solution.py
@@ -34,6 +34,7 @@
     def __init__(self, dps, seqs):
         self.sizes = {"dp": dps, "seq": seqs}
         self.last = {}
+        self.sent = []
 
     def ordered(self, value, link, permute):
         self.last[link] = permute(after(value, self.last.get(link)))
@@ -64,12 +65,14 @@
                 pieces[j ^ bit] = self.swap(pieces[j], "seq", bit, free)
         return [pieces[j] for j in range(len(pieces))]
 
-    def scatter_seq(self, blocks, last=None, free=False):
+    def scatter_seq(self, blocks, last=None, free=False, hold=None):
         blocks = dict(enumerate(blocks))
         for bit in reversed(bits_of(self.sizes["seq"])):
             for j in sorted(blocks, reverse=True):
                 if j & bit:
-                    got = after(self.swap(blocks.pop(j).astype(BF), "seq", bit, free), last if j == bit and j > 1 else None)
+                    final = j == bit and j > 1
+                    sent = after(blocks.pop(j).astype(BF), hold if final else None)
+                    got = after(self.swap(sent, "seq", bit, free), last if final else None)
                     blocks[j ^ bit] = blocks[j ^ bit].astype(F32) + got.astype(F32)
         return blocks[0]
 
@@ -99,6 +102,7 @@
         if rows % size == 0:
             part = rows // size
             pieces = self.relative([value[b * part : (b + 1) * part] for b in range(size)])
+            self.sent = pieces
             plans = [from_columns([columns(q ^ j) for j in range(size)], part, len(widths)) for q in range(size)]
             out = rearrange(self.exchange_seq(pieces), [(part, w) for w in widths], plans, rank, F32)
             return [matrix.reshape(-1) for matrix in out]
@@ -485,7 +489,7 @@
 
     shift = hidden // devices
     tail = -(-shift * devices // LANES) * LANES
-    before = links.shift(w_fc[-tail:], 1)
+    before = links.shift(after(w_fc[-tail:], attention_part), 1)
     part = attention_vectors.shape[0]
     last = device == devices - 1
     small = jnp.zeros((8 * width,), BF)
@@ -504,15 +508,15 @@
     dy_own = ring.inward(cotangent[0]) * (place < length).astype(BF)[:, None]
     dy_wide = dy_own.astype(F32)
     dy = jnp.concatenate(links.gather_seq(after(dy_own, small, x_all)), axis=0)
+    unit1_all, _ = normal(x_all.astype(F32))
+    h1 = (unit1_all * gain1 + shift1).astype(BF)
     plain = w_fc.shape[0] - shift
-    fc_flat = lax.dynamic_slice_in_dim(jnp.concatenate([before, after(w_fc, attention_part, dy)]), tail - shift * device, plain)
+    fc_flat = lax.dynamic_slice_in_dim(jnp.concatenate([before, after(w_fc, attention_part, dy, h1)]), tail - shift * device, plain)
     fc_part = links.columns_from_rows([fc_flat], unit_rows, columns_fc)
     fc_full = ring.gather(fc_part)
 
     out_parts = links.gather_seq(out_part, free=True)
 
-    unit1_all, _ = normal(x_all.astype(F32))
-    h1 = (unit1_all * gain1 + shift1).astype(BF)
     mixed = (dot(after(h1, dy), qkv_full) + bias_qkv).astype(BF)
     proj_full = ring.gather(after(ring.inward(w_proj.reshape(-1, width), small=True), fc_part, mixed))
     o_heads = attention_forward(info, mixed, own, size)
@@ -549,18 +553,15 @@
     do_heads = after(do_heads, *grad_out, grad_proj_own)
     dmixed = attention_backward(info, mixed, do_heads, own, size)
     grad_out = links.scatter_seq(grad_out, dmixed, free=True).astype(BF)
-    grad_qkv = dot(h1, after(dmixed, grad_fc), ((0,), (0,))).astype(BF)
+    dh1_part = dot(dmixed, qkv_full, ((1,), (1,)))
+    grad_qkv = dot(h1, after(dmixed, dh1_part), ((0,), (0,))).astype(BF)
     grad_attention = jnp.concatenate([grad_qkv, grad_out], axis=1)
-    dmixed = after(dmixed, grad_attention)
+    dh1_part, dmixed, grad_fc = (after(value, grad_attention) for value in (dh1_part, dmixed, grad_fc))
+    output = links.scatter_seq(split(output_part), free=True, hold=grad_attention)
+    output = ring.outward((x2 + output + bias_p).astype(BF))
     grad_attention = ring.scatter(grad_attention)
-    dh1_part = dot(dmixed, qkv_full, ((1,), (1,)))
-    output = ring.outward((x2 + links.scatter_seq(split(after(output_part, dmixed)), free=True) + bias_p).astype(BF))
-    dh1 = links.scatter_seq(split(dh1_part))
     fc_rows = links.rows_from_columns(grad_fc, [hidden], columns_fc)[0]
     behind = links.shift(fc_rows[:tail].astype(BF), -1)
-    unit1, scale1 = normal(x_own.astype(F32))
-    input_grad = ring.outward(dx2 + norm_input_grad(unit1, scale1, gain1, dh1))
-
     total = lambda m: jnp.sum(m.astype(F32), axis=0)
     wide = all_columns(total(dmixed), 3 * width, columns_qkv)
     inner = [total(dh1_part * unit1_all), total(dh1_part), total(dz), total(dh2 * unit2), total(dh2), total(dy_wide)]
@@ -569,7 +570,14 @@
         grad_g1, grad_c1, wide[:width], wide[2 * width :], grad_bo, grad_g2, grad_c2, grad_bp,
         all_columns(total(du), hidden, columns_fc),
     ])
-    sums = links.all_sum(sums, ("seq", "dp"), free=True)
+    sums = links.all_sum(sums, ("seq",), free=True)
+    dh1 = links.scatter_seq(split(dh1_part), free=True, hold=sums)
+    qkv_flat, out_flat = links.rows_from_columns(grad_attention, [3 * width, width], columns_attention)
+    dh1 = after(dh1, *links.sent)
+    unit1, scale1 = normal(x_own.astype(F32))
+    input_grad = ring.outward(dx2 + norm_input_grad(unit1, scale1, gain1, dh1))
+
+    sums = links.all_sum(sums, ("dp",), free=True)
     vec1 = lax.dynamic_slice_in_dim(sums[: 4 * width], device * part, part)
     vec2 = lax.dynamic_slice_in_dim(sums[4 * width : 8 * width], device * part, part)
     sum_bf = sums[8 * width :]
@@ -579,7 +587,6 @@
         jnp.concatenate([fc_rows, behind]), shift * device, w_fc.shape[0]
     )
     grad_attention = after(grad_attention, input_grad, fc_flat_grad, vec1, vec2, output)
-    qkv_flat, out_flat = links.rows_from_columns(grad_attention, [3 * width, width], columns_attention)
     return (output[None], input_grad[None], qkv_flat, out_flat, fc_flat_grad, ring.outward(grad_proj_own, small=True).reshape(-1), vec1, vec2)
 
 

time: 514 us -> 498 us (0.969)
  waiting for transfers between devices: 146 us -> 127 us
  starting transfers between devices: 43.5 us -> 58 us
  local copies, waits for them, and re-layouts: 67.9 us -> 57.5 us
  matrix products: 117 us -> 110 us
    ppermute x20 -> x17, waiting for transfers between devices: 75.2 us -> 58.9 us  [swap(): lax.ppermute(v, axis, pairs)]
    ppermute x32 -> x35, starting transfers between devices: 26.8 us -> 40.3 us  [swap(): return lax.ppermute(value, axis, pairs)]
    ppermute x32 -> x35, waiting for transfers between devices: 70.6 us -> 58.2 us  [swap(): return lax.ppermute(value, axis, pairs)]
    reduce_sum x4 -> x5, other arithmetic: 7.13 us -> 16.7 us  [local(): total = lambda m: jnp.sum(m.astype(F32), axis=0)]
    all_gather x3, waiting for transfers between devices: 0.05 us -> 8.96 us  [gather(): lax.all_gather(value, 'dp', axis=0, tiled=True, axis_index_groups=self.gr...]
    dot_general x21, matrix products: 117 us -> 110 us  [dot(): return lax.dot_general(a, b, (dims, ((), ())), preferred_element_type=F32)]
    unnamed x164 -> x148, local copies, waits for them, and re-layouts: 23.9 us -> 21.6 us
    ppermute x20 -> x17, starting transfers between devices: 11.5 us -> 13.3 us  [swap(): lax.ppermute(v, axis, pairs)]
  transfers between devices with their start and end apart: 60 -> 60, of which waited for: 30 -> 24; matrix products, arithmetic and copies ran while one was open for 46% -> 44% of each run, Pallas kernels for 10% -> 11%
where the time goes in v4:
time: 498 us; the launch traced here: 488 us
  waiting for transfers between devices  127 us (26%)
  matrix products  110 us (22%)
  other arithmetic  67.2 us (13%)
  starting transfers between devices  58 us (12%)
  local copies, waits for them, and re-layouts  57.5 us (12%)
  Pallas kernels  52 us (10%)
  between operations  16.7 us (3%)
    dot_general x21, matrix products, dot(): return lax.dot_general(a, b, (dims, ((), ())), preferred_element_type=F32)  110 us
    ppermute x17, waiting for transfers between devices, swap(): lax.ppermute(v, axis, pairs)  58.9 us
    ppermute x35, waiting for transfers between devices, swap(): return lax.ppermute(value, axis, pairs)  58.2 us
    ppermute x35, starting transfers between devices, swap(): return lax.ppermute(value, axis, pairs)  40.3 us
    pallas_call x1, Pallas kernels, attention_backward(): pl.pallas_call(partial(attention_backward_kernel, size, pairs, odd), out_...  27.2 us
    unnamed x148, local copies, waits for them, and re-layouts  21.6 us
    pallas_call x1, Pallas kernels, attention_forward(): pl.pallas_call(partial(attention_forward_kernel, size, pairs, odd), out_s...  20.9 us
    reduce_sum x5, other arithmetic, local(): total = lambda m: jnp.sum(m.astype(F32), axis=0)  16.7 us
  transfers between devices with their start and end apart: 60, of which 24 were waited for; matrix products, arithmetic and copies ran while one was open for 44% of the time, Pallas kernels for 11%

profile of v4, /device:TPU:0, one launch (start us, length us, event | category | flops | bytes accessed | tf_op | source)
XLA Modules:
  0.0 488.0 jit_solution(17702370060668151358)
XLA Ops:
  47.4 7.4 %collective-permute-done.7 = bf16[256,1600]{0,1:T(8,128)(2,1)} collective-permute-done((bf16[256,1600]{0,1:T(8,128)(2,1)}, bf16[256,1600]{0,1:T(8,128)(2,1)}, u32[]{:S(2)}, u32[]{:S(2)}) %collective-permute-start.7) | collective-permute-done | bytes 819232 | tf_op jit(solution)/shard_map/ppermute | solution.py:48
  63.1 17.3 %collective-permute-done.13 = bf16[256,1600]{0,1:T(8,128)(2,1)S(1)} collective-permute-done((bf16[256,1600]{0,1:T(8,128)(2,1)S(1)}, bf16[256,1600]{0,1:T(8,128)(2,1)S(1)}, u32[]{:S(2)}, u32[]{:S(2)}) %collective-permute-start.13) | collective-permute-done | bytes 819232 | tf_op jit(solution)/shard_map/ppermute | solution.py:48
  89.2 4.4 collective-permute-done.24
  93.6 4.5 collective-permute-done.25
  109.4 10.2 %add_convert_fusion.q_ref.k_ref.v_ref = bf16[1024,1408]{1,0:T(8,128)(2,1)} fusion(bf16[1024,1600]{0,1:T(8,128)(2,1)} %fusion.5, bf16[1600,1808]{1,0:T(8,128)(2,1)} %all-gather.4.cloned.1.call-done, f32[1408]{0:T(1024)S(1)} %reduce.2), kind=kOutput, calls=%fused_computation.27 | convolution fusion | flops 4616617984 | bytes 10671616 | tf_op jit(solution)/shard_map/dot_general | solution.py:445
  121.6 20.9 %attention_forward.1 = bf16[1024,512]{1,0:T(8,128)(2,1)S(1)} custom-call(s32[2]{0:T(128)S(1)} %pad_add_fusion.info, bf16[1024,1408]{1,0:T(8,128)(2,1)S(1)} %copy-done.1, bf16[1024,1408]{1,0:T(8,128)(2,1)S(1)} %copy-done.1, bf16[1024,1408]{1,0:T(8,128)(2,1)S(1)} %copy-done.1), custom_call_target="tpu_custom_call" | custom-call | flops 24956108800 | bytes 5767168 | tf_op jit(solution)/shard_map/attention_forward/pallas_call | solution.py:380
  146.2 5.5 %collective-permute-done.16 = bf16[256,512]{1,0:T(8,128)(2,1)S(1)} collective-permute-done((bf16[256,512]{1,0:T(8,128)(2,1)S(1)}, bf16[256,512]{1,0:T(8,128)(2,1)S(1)}, u32[]{:S(2)}, u32[]{:S(2)}) %collective-permute-start.16) | collective-permute-done | bytes 262176 | tf_op jit(solution)/shard_map/ppermute | solution.py:46
  151.8 4.7 collective-permute-done.15
  173.9 18.4 %collective-permute-done.22 = bf16[256,1600]{0,1:T(8,128)(2,1)} collective-permute-done((bf16[256,1600]{0,1:T(8,128)(2,1)S(1)}, bf16[256,1600]{0,1:T(8,128)(2,1)}, u32[]{:S(2)}, u32[]{:S(2)}) %collective-permute-start.22) | collective-permute-done | bytes 819232 | tf_op jit(solution)/shard_map/ppermute | solution.py:48
  195.0 12.7 %multiply_convert_fusion.1 = (bf16[1024,1600]{0,1:T(8,128)(2,1)S(1)}, f32[1024,1600]{0,1:T(8,128)}) fusion(f32[1600]{0:T(1024)S(1)} %reduce.6, bf16[1600,1600]{1,0:T(8,128)(2,1)} %all-gather.6.cloned.1.call-done, bf16[256,1600]{0,1:T(8,128)(2,1)} %collective-permute-done.23, bf16[256,1600]{0,1:T(8,128)(2,1)} %collective-permute-done.22, ...), kind=kOutput, calls=%fused_computation.23 | convolution fusion | flops 5272371200 | bytes 18233600 | tf_op jit(solution)/shard_map/dot_general | solution.py:445
  209.4 7.8 %convolution_convert_fusion.2 = bf16[1600,1600]{1,0:T(8,128)(2,1)} fusion(bf16[1024,1600]{0,1:T(8,128)(2,1)S(1)} %get-tuple-element.89, bf16[1024,1600]{0,1:T(8,128)(2,1)S(1)} %copy-done.34), kind=kOutput, calls=%fused_computation.8 | convolution fusion | flops 5245440000 | bytes 11673600 | tf_op jit(solution)/shard_map/dot_general | solution.py:445
  217.5 6.7 %all-gather.8.cloned.1.call-done = bf16[1600,1600]{1,0:T(8,128)(2,1)} async-done(((bf16[200,1600]{1,0:T(8,128)(2,1)}), bf16[1600,1600]{1,0:T(8,128)(2,1)}) %all-gather.8.cloned.1.call-update) | async-done | bytes 5120016 | tf_op jit(solution)/shard_map/all_gather | solution.py:183
  224.2 14.6 %convert_reduce_fusion.1 = (f32[1600]{0:T(1024)S(1)}, bf16[1024,1600]{0,1:T(8,128)(2,1)S(1)}) fusion(f32[1024,1600]{0,1:T(8,128)} %get-tuple-element.199, f32[1600]{0:T(1024)S(1)} %reduce.6, bf16[1600,1600]{1,0:T(8,128)(2,1)} %all-gather.8.cloned.1.call-done, bf16[1024,1600]{0,1:T(8,128)(2,1)} %copy-done.33), kind=kOutput, calls=%fused_computation.21 | convolution fusion | flops 5282200064 | bytes 18240000 | tf_op jit(solution)/shard_map/dot_general | solution.py:445
  238.8 9.9 %fusion.67 = (bf16[1024,1600]{0,1:T(8,128)(2,1)S(1)}, f32[1024,1600]{0,1:T(8,128)}) fusion(bf16[1600,1600]{1,0:T(8,128)(2,1)} %all-gather.6.cloned.1.call-done, bf16[1024,1600]{0,1:T(8,128)(2,1)S(1)} %get-tuple-element.88), kind=kOutput, calls=%fused_computation.223 | convolution fusion | flops 5244518400 | bytes 18227200 | tf_op jit(solution)/shard_map/dot_general | solution.py:445
  250.1 10.2 %convolution_convert_fusion.1 = bf16[1600,1600]{1,0:T(8,128)(2,1)} fusion(bf16[1024,1600]{0,1:T(8,128)(2,1)S(1)} %get-tuple-element.88, bf16[256,1600]{0,1:T(8,128)(2,1)} %collective-permute-done.23, bf16[256,1600]{0,1:T(8,128)(2,1)} %collective-permute-done.22, bf16[256,1600]{0,1:T(8,128)(2,1)S(1)} %copy-done.54, bf16[256,1600]{0,1:T(8,128)(2,1)S(1)} %copy-done.28), kind=kOutput, calls=%fused_computation.7 | convolution fusion | flops 5258547200 | bytes 11673600 | tf_op jit(solution)/shard_map/dot_general | solution.py:445
  263.8 11.8 %fusion.68 = (bf16[1024,1600]{0,1:T(8,128)(2,1)}, f32[1024,1600]{0,1:T(8,128)}) fusion(bf16[1024,1600]{0,1:T(8,128)(2,1)S(1)} %copy-done.58, bf16[1600,1600]{1,0:T(8,128)(2,1)} %all-gather.8.cloned.1.call-done), kind=kOutput, calls=%fused_computation.224 | convolution fusion | flops 5244518400 | bytes 18227200 | tf_op jit(solution)/shard_map/dot_general | solution.py:445
  275.6 6.9 %collective-permute-done.31 = bf16[256,1600]{0,1:T(8,128)(2,1)S(1)} collective-permute-done((bf16[256,1600]{0,1:T(8,128)(2,1)S(1)}, bf16[256,1600]{0,1:T(8,128)(2,1)S(1)}, u32[]{:S(2)}, u32[]{:S(2)}) %collective-permute-start.31) | collective-permute-done | bytes 819232 | tf_op jit(solution)/shard_map/ppermute | solution.py:48
  309.9 5.4 %collective-permute-done.33 = bf16[256,512]{1,0:T(8,128)(2,1)S(1)} collective-permute-done((bf16[256,512]{1,0:T(8,128)(2,1)S(1)}, bf16[256,512]{1,0:T(8,128)(2,1)S(1)}, u32[]{:S(2)}, u32[]{:S(2)}) %collective-permute-start.33) | collective-permute-done | bytes 262176 | tf_op jit(solution)/shard_map/ppermute | solution.py:46
  315.3 3.9 collective-permute-done.34
  322.7 27.2 %attention_backward.1 = bf16[1024,1408]{1,0:T(8,128)(2,1)S(1)} custom-call(s32[2]{0:T(128)S(1)} %pad_add_fusion.info, bf16[1024,1408]{1,0:T(8,128)(2,1)} %add_convert_fusion.q_ref.k_ref.v_ref, bf16[1024,1408]{1,0:T(8,128)(2,1)} %add_convert_fusion.q_ref.k_ref.v_ref, bf16[1024,1408]{1,0:T(8,128)(2,1)} %add_convert_fusion.q_ref.k_ref.v_ref, ...), custom_call_target="tpu_custom_call" | custom-call | flops 24956108800 | bytes 8650752 | tf_op jit(solution)/shard_map/attention_backward/pallas_call | solution.py:401
  349.8 10.6 %fusion.14 = f32[1024,1600]{0,1:T(8,128)} fusion(bf16[1024,1408]{1,0:T(8,128)(2,1)S(1)} %attention_backward.1, bf16[1600,1808]{1,0:T(8,128)(2,1)} %all-gather.4.cloned.1.call-done), kind=kOutput, calls=%fused_computation.28 | convolution fusion | flops 4613734400 | bytes 13942784 | tf_op jit(solution)/shard_map/dot_general | solution.py:445
  364.7 7.8 %convolution_convert_fusion = bf16[1600,1408]{1,0:T(8,128)(2,1)S(1)} fusion(bf16[1024,1600]{0,1:T(8,128)(2,1)} %fusion.5, bf16[1024,1408]{1,0:T(8,128)(2,1)} %copy-done), kind=kOutput, calls=%fused_computation.6 | convolution fusion | flops 4615987200 | bytes 10665984 | tf_op jit(solution)/shard_map/dot_general | solution.py:445
  372.5 3.0 pad_maximum_fusion
  378.8 9.1 %fusion.53 = (f32[1600]{0:T(1024)S(1)}, f32[1600]{0:T(1024)S(1)}, bf16[1024,1600]{0,1:T(8,128)(2,1)}) fusion(f32[1024,1600]{0,1:T(8,128)} %fusion.14, f32[1024]{0:T(1024)S(1)} %copy-done.43, f32[1024]{0:T(1024)S(1)} %copy-done.41, bf16[1024,1600]{0,1:T(8,128)(2,1)} %copy-done.2), kind=kLoop, calls=%fused_computation.212 | loop fusion | flops 11465600 | bytes 13128192 | tf_op jit(solution)/shard_map/reduce_sum | solution.py:565
  389.0 4.5 collective-permute-done.41
  398.8 7.1 %collective-permute-done.50 = f32[19200]{0:T(1024)S(1)} collective-permute-done((f32[19200]{0:T(1024)S(1)}, f32[19200]{0:T(1024)S(1)}, u32[]{:S(2)}, u32[]{:S(2)}) %collective-permute-start.50) | collective-permute-done | bytes 76832 | tf_op jit(solution)/shard_map/ppermute | solution.py:46
  409.2 3.3 collective-permute-done.51
  421.4 2.7 fusion.30
  427.0 12.5 %collective-permute-done.49.refs_3_ = bf16[50,1600]{1,0:T(8,128)(2,1)S(1)} collective-permute-done((bf16[50,1600]{1,0:T(8,128)(2,1)}, bf16[50,1600]{1,0:T(8,128)(2,1)S(1)}, u32[]{:S(2)}, u32[]{:S(2)}) %collective-permute-start.49) | collective-permute-done | bytes 160032 | tf_op jit(solution)/shard_map/ppermute | solution.py:46
  445.2 3.3 convert_add_fusion.2
  455.9 12.4 %collective-permute-start.44 = (bf16[50,1808]{1,0:T(8,128)(2,1)S(1)}, bf16[50,1808]{1,0:T(8,128)(2,1)S(1)}, u32[]{:S(2)}, u32[]{:S(2)}) collective-permute-start(bf16[50,1808]{1,0:T(8,128)(2,1)S(1)} %get-tuple-element.177), channel_id=1, source_target_pairs={{0,1},{1,0},{2,3},{3,2},{4,5},{5,4},{6,7},{7,6},{8,9},{9,8},{10,11... | collective-permute-start | bytes 542408 | tf_op jit(solution)/shard_map/ppermute | solution.py:46
  472.0 3.5 fusion.25
  (399 shorter events, 181.3 us)
Async XLA Ops:
  7.2 96.9 %all-gather.4.cloned.1.call-start = ((), (), s32[]{:S(2)}) async-start(), calls=%async_computation.3 | async-start | bytes 6912000 | tf_op jit(solution)/shard_map/all_gather | solution.py:183
  10.3 14.1 %collective-permute-start = (bf16[50,1808]{1,0:T(8,128)(2,1)S(1)}, bf16[50,1808]{1,0:T(8,128)(2,1)S(1)}, u32[]{:S(2)}, u32[]{:S(2)}) collective-permute-start(bf16[50,1808]{1,0:T(8,128)(2,1)S(1)} %get-tuple-element.58), channel_id=1, source_target_pairs={{0,3},{1,2},{2,1},{3,0},{4,7},{5,6},{6,5},{7,4},{8,11},{9,10},{10,... | collective-permute-start | bytes 542408 | tf_op jit(solution)/shard_map/ppermute | solution.py:46
  12.8 11.6 %collective-permute-start.1 = (bf16[50,1808]{1,0:T(8,128)(2,1)S(1)}, bf16[50,1808]{1,0:T(8,128)(2,1)}, u32[]{:S(2)}, u32[]{:S(2)}) collective-permute-start(bf16[50,1808]{1,0:T(8,128)(2,1)S(1)} %get-tuple-element.59), channel_id=1, source_target_pairs={{0,2},{1,3},{2,0},{3,1},{4,6},{5,7},{6,4},{7,5},{8,10},{9,11},{10,... | collective-permute-start | bytes 542408 | tf_op jit(solution)/shard_map/ppermute | solution.py:46
  34.0 20.8 %collective-permute-start.7 = (bf16[256,1600]{0,1:T(8,128)(2,1)}, bf16[256,1600]{0,1:T(8,128)(2,1)}, u32[]{:S(2)}, u32[]{:S(2)}) collective-permute-start(bf16[256,1600]{0,1:T(8,128)(2,1)} %slice_dynamic-update-slice_fusion.22), channel_id=1, source_target_pairs={{0,2},{1,3},{2,0},{3,1},{4,6},{5,7},{6,4},{7,5},{8,10},{9,11},{10,... | collective-permute-start | bytes 2457608 | tf_op jit(solution)/shard_map/ppermute | solution.py:48
  35.5 19.3 %collective-permute-start.6 = (bf16[256,1600]{0,1:T(8,128)(2,1)}, bf16[256,1600]{0,1:T(8,128)(2,1)}, u32[]{:S(2)}, u32[]{:S(2)}) collective-permute-start(bf16[256,1600]{0,1:T(8,128)(2,1)} %slice_dynamic-update-slice_fusion.22), channel_id=1, source_target_pairs={{0,1},{1,0},{2,3},{3,2},{4,5},{5,4},{6,7},{7,6},{8,9},{9,8},{10,11... | collective-permute-start | bytes 2457608 | tf_op jit(solution)/shard_map/ppermute | solution.py:48
  38.2 155.2 %all-gather.6.cloned.1.call-start = ((), (), s32[]{:S(2)}) async-start(), calls=%async_computation.4 | async-start | bytes 5990400 | tf_op jit(solution)/shard_map/all_gather | solution.py:183
  60.2 20.2 %collective-permute-start.13 = (bf16[256,1600]{0,1:T(8,128)(2,1)S(1)}, bf16[256,1600]{0,1:T(8,128)(2,1)S(1)}, u32[]{:S(2)}, u32[]{:S(2)}) collective-permute-start(bf16[256,1600]{0,1:T(8,128)(2,1)S(1)} %copy-done.10), channel_id=1, source_target_pairs={{0,2},{1,3},{2,0},{3,1},{4,6},{5,7},{6,4},{7,5},{8,10},{9,11},{10,... | collective-permute-start | bytes 2457608 | tf_op jit(solution)/shard_map/ppermute | solution.py:48
  99.2 125.0 %all-gather.8.cloned.1.call-start = ((), (), s32[]{:S(2)}) async-start(), calls=%async_computation.5 | async-start | bytes 5990400 | tf_op jit(solution)/shard_map/all_gather | solution.py:183
  108.0 48.6 %collective-permute-start.18 = (bf16[1600,400]{0,1:T(8,128)(2,1)}, bf16[1600,400]{0,1:T(8,128)(2,1)S(1)}, u32[]{:S(2)}, u32[]{:S(2)}) collective-permute-start(bf16[1600,400]{0,1:T(8,128)(2,1)} %copy.25), channel_id=1, source_target_pairs={{0,2},{1,3},{2,0},{3,1},{4,6},{5,7},{6,4},{7,5},{8,10},{9,11},{10,... | collective-permute-start | bytes 3840008 | tf_op jit(solution)/shard_map/ppermute | solution.py:46
  119.6 166.6 %reduce-scatter.13.cloned.1.call-start = ((), (), s32[]{:S(2)}) async-start(), calls=%async_computation.6 | async-start | bytes 5990400
  143.0 13.5 %collective-permute-start.15 = (bf16[256,512]{1,0:T(8,128)(2,1)S(1)}, bf16[256,512]{1,0:T(8,128)(2,1)S(1)}, u32[]{:S(2)}, u32[]{:S(2)}) collective-permute-start(bf16[256,512]{1,0:T(8,128)(2,1)S(1)} %get-tuple-element.159), channel_id=1, source_target_pairs={{0,3},{1,2},{2,1},{3,0},{4,7},{5,6},{6,5},{7,4},{8,11},{9,10},{10,... | collective-permute-start | bytes 786440 | tf_op jit(solution)/shard_map/ppermute | solution.py:46
  145.8 18.9 %collective-permute-start.20 = (bf16[1600,400]{0,1:T(8,128)(2,1)}, bf16[1600,400]{0,1:T(8,128)(2,1)}, u32[]{:S(2)}, u32[]{:S(2)}) collective-permute-start(bf16[1600,400]{0,1:T(8,128)(2,1)} %copy.25), channel_id=1, source_target_pairs={{0,1},{1,0},{2,3},{3,2},{4,5},{5,4},{6,7},{7,6},{8,9},{9,8},{10,11... | collective-permute-start | bytes 3840008 | tf_op jit(solution)/shard_map/ppermute | solution.py:46
  171.8 20.6 %collective-permute-start.22 = (bf16[256,1600]{0,1:T(8,128)(2,1)S(1)}, bf16[256,1600]{0,1:T(8,128)(2,1)}, u32[]{:S(2)}, u32[]{:S(2)}) collective-permute-start(bf16[256,1600]{0,1:T(8,128)(2,1)S(1)} %add_convert_fusion.4), channel_id=1, source_target_pairs={{0,2},{1,3},{2,0},{3,1},{4,6},{5,7},{6,4},{7,5},{8,10},{9,11},{10,... | collective-permute-start | bytes 2457608 | tf_op jit(solution)/shard_map/ppermute | solution.py:48
  217.2 199.7 %reduce-scatter.17.cloned.1.call-start = ((), (), s32[]{:S(2)}) async-start(), calls=%async_computation.8 | async-start | bytes 5990400
  248.9 11.4 %collective-permute-start.29 = (bf16[256,1600]{0,1:T(8,128)(2,1)S(1)}, bf16[256,1600]{0,1:T(8,128)(2,1)}, u32[]{:S(2)}, u32[]{:S(2)}) collective-permute-start(bf16[256,1600]{0,1:T(8,128)(2,1)S(1)} %get-tuple-element.90), channel_id=1, source_target_pairs={{0,1},{1,0},{2,3},{3,2},{4,5},{5,4},{6,7},{7,6},{8,9},{9,8},{10,11... | collective-permute-start | bytes 2457608 | tf_op jit(solution)/shard_map/ppermute | solution.py:48
  262.3 20.2 %collective-permute-start.31 = (bf16[256,1600]{0,1:T(8,128)(2,1)S(1)}, bf16[256,1600]{0,1:T(8,128)(2,1)S(1)}, u32[]{:S(2)}, u32[]{:S(2)}) collective-permute-start(bf16[256,1600]{0,1:T(8,128)(2,1)S(1)} %fusion.28), channel_id=1, source_target_pairs={{0,2},{1,3},{2,0},{3,1},{4,6},{5,7},{6,4},{7,5},{8,10},{9,11},{10,... | collective-permute-start | bytes 2457608 | tf_op jit(solution)/shard_map/ppermute | solution.py:48
  263.8 18.7 %collective-permute-start.30 = (bf16[256,1600]{0,1:T(8,128)(2,1)S(1)}, bf16[256,1600]{0,1:T(8,128)(2,1)S(1)}, u32[]{:S(2)}, u32[]{:S(2)}) collective-permute-start(bf16[256,1600]{0,1:T(8,128)(2,1)S(1)} %get-tuple-element.91), channel_id=1, source_target_pairs={{0,1},{1,0},{2,3},{3,2},{4,5},{5,4},{6,7},{7,6},{8,9},{9,8},{10,11... | collective-permute-start | bytes 2457608 | tf_op jit(solution)/shard_map/ppermute | solution.py:48
  287.5 165.3 %reduce-scatter.15.cloned.1.call-start = ((), (), s32[]{:S(2)}) async-start(), calls=%async_computation.7 | async-start | bytes 6912000
  300.4 18.9 %collective-permute-start.36 = (bf16[1600,400]{0,1:T(8,128)(2,1)}, bf16[1600,400]{0,1:T(8,128)(2,1)}, u32[]{:S(2)}, u32[]{:S(2)}) collective-permute-start(bf16[1600,400]{0,1:T(8,128)(2,1)} %convolution_convert_fusion.3), channel_id=1, source_target_pairs={{0,1},{1,0},{2,3},{3,2},{4,5},{5,4},{6,7},{7,6},{8,9},{9,8},{10,11... | collective-permute-start | bytes 3840008 | tf_op jit(solution)/shard_map/ppermute | solution.py:46
  308.0 11.2 %collective-permute-start.34 = (bf16[256,512]{1,0:T(8,128)(2,1)S(1)}, bf16[256,512]{1,0:T(8,128)(2,1)S(1)}, u32[]{:S(2)}, u32[]{:S(2)}) collective-permute-start(bf16[256,512]{1,0:T(8,128)(2,1)S(1)} %select_select_fusion.4), channel_id=1, source_target_pairs={{0,3},{1,2},{2,1},{3,0},{4,7},{5,6},{6,5},{7,4},{8,11},{9,10},{10,... | collective-permute-start | bytes 786440 | tf_op jit(solution)/shard_map/ppermute | solution.py:46
  308.6 51.8 %collective-permute-start.35 = (bf16[1600,400]{0,1:T(8,128)(2,1)S(1)}, bf16[1600,400]{0,1:T(8,128)(2,1)S(1)}, u32[]{:S(2)}, u32[]{:S(2)}) collective-permute-start(bf16[1600,400]{0,1:T(8,128)(2,1)S(1)} %convolution_convert_fusion.5), channel_id=1, source_target_pairs={{0,1},{1,0},{2,3},{3,2},{4,5},{5,4},{6,7},{7,6},{8,9},{9,8},{10,11... | collective-permute-start | bytes 3840008 | tf_op jit(solution)/shard_map/ppermute | solution.py:46
  321.2 39.3 %collective-permute-start.37 = (bf16[1600,400]{0,1:T(8,128)(2,1)S(1)}, bf16[1600,400]{0,1:T(8,128)(2,1)S(1)}, u32[]{:S(2)}, u32[]{:S(2)}) collective-permute-start(bf16[1600,400]{0,1:T(8,128)(2,1)S(1)} %add_convert_fusion.2), channel_id=1, source_target_pairs={{0,2},{1,3},{2,0},{3,1},{4,6},{5,7},{6,4},{7,5},{8,10},{9,11},{10,... | collective-permute-start | bytes 3840008 | tf_op jit(solution)/shard_map/ppermute | solution.py:46
  396.1 17.7 %collective-permute-start.40 = (bf16[256,1600]{0,1:T(8,128)(2,1)S(1)}, bf16[256,1600]{0,1:T(8,128)(2,1)S(1)}, u32[]{:S(2)}, u32[]{:S(2)}) collective-permute-start(bf16[256,1600]{0,1:T(8,128)(2,1)S(1)} %get-tuple-element.140), channel_id=1, source_target_pairs={{0,1},{1,0},{2,3},{3,2},{4,5},{5,4},{6,7},{7,6},{8,9},{9,8},{10,11... | collective-permute-start | bytes 2457608 | tf_op jit(solution)/shard_map/ppermute | solution.py:46
  408.7 36.4 %collective-permute-start.39 = (bf16[256,1600]{0,1:T(8,128)(2,1)}, bf16[256,1600]{0,1:T(8,128)(2,1)}, u32[]{:S(2)}, u32[]{:S(2)}) collective-permute-start(bf16[256,1600]{0,1:T(8,128)(2,1)} %get-tuple-element.139), channel_id=1, source_target_pairs={{0,1},{1,0},{2,3},{3,2},{4,5},{5,4},{6,7},{7,6},{8,9},{9,8},{10,11... | collective-permute-start | bytes 2457608 | tf_op jit(solution)/shard_map/ppermute | solution.py:46
  416.4 28.8 %collective-permute-start.43 = (bf16[256,1600]{0,1:T(8,128)(2,1)}, bf16[256,1600]{0,1:T(8,128)(2,1)}, u32[]{:S(2)}, u32[]{:S(2)}) collective-permute-start(bf16[256,1600]{0,1:T(8,128)(2,1)} %add_convert_fusion.3), channel_id=1, source_target_pairs={{0,2},{1,3},{2,0},{3,1},{4,6},{5,7},{6,4},{7,5},{8,10},{9,11},{10,... | collective-permute-start | bytes 2457608 | tf_op jit(solution)/shard_map/ppermute | solution.py:46
  419.3 20.3 %collective-permute-start.49 = (bf16[50,1600]{1,0:T(8,128)(2,1)}, bf16[50,1600]{1,0:T(8,128)(2,1)S(1)}, u32[]{:S(2)}, u32[]{:S(2)}) collective-permute-start(bf16[50,1600]{1,0:T(8,128)(2,1)} %get-tuple-element.183), channel_id=1, source_target_pairs={{0,3},{1,2},{2,1},{3,0},{4,7},{5,6},{6,5},{7,4},{8,11},{9,10},{10,... | collective-permute-start | bytes 480008 | tf_op jit(solution)/shard_map/ppermute | solution.py:46
  419.3 22.1 %collective-permute-start.47 = (bf16[50,1600]{1,0:T(8,128)(2,1)}, bf16[50,1600]{1,0:T(8,128)(2,1)S(1)}, u32[]{:S(2)}, u32[]{:S(2)}) collective-permute-start(bf16[50,1600]{1,0:T(8,128)(2,1)} %get-tuple-element.185), channel_id=1, source_target_pairs={{0,1},{1,0},{2,3},{3,2},{4,5},{5,4},{6,7},{7,6},{8,9},{9,8},{10,11... | collective-permute-start | bytes 480008 | tf_op jit(solution)/shard_map/ppermute | solution.py:46
  420.8 22.4 %collective-permute-start.48 = (bf16[50,1600]{1,0:T(8,128)(2,1)}, bf16[50,1600]{1,0:T(8,128)(2,1)S(1)}, u32[]{:S(2)}, u32[]{:S(2)}) collective-permute-start(bf16[50,1600]{1,0:T(8,128)(2,1)} %get-tuple-element.186), channel_id=1, source_target_pairs={{0,2},{1,3},{2,0},{3,1},{4,6},{5,7},{6,4},{7,5},{8,10},{9,11},{10,... | collective-permute-start | bytes 480008 | tf_op jit(solution)/shard_map/ppermute | solution.py:46
  439.5 32.4 %collective-permute-start.27 = (bf16[256,1600]{0,1:T(8,128)(2,1)}, bf16[256,1600]{0,1:T(8,128)(2,1)}, u32[]{:S(2)}, u32[]{:S(2)}) collective-permute-start(bf16[256,1600]{0,1:T(8,128)(2,1)} %get-tuple-element.141), channel_id=1, source_target_pairs={{0,1},{1,0},{2,3},{3,2},{4,5},{5,4},{6,7},{7,6},{8,9},{9,8},{10,11... | collective-permute-start | bytes 2457608 | tf_op jit(solution)/shard_map/ppermute | solution.py:46
  441.4 30.6 %collective-permute-start.38 = (bf16[256,1600]{0,1:T(8,128)(2,1)}, bf16[256,1600]{0,1:T(8,128)(2,1)}, u32[]{:S(2)}, u32[]{:S(2)}) collective-permute-start(bf16[256,1600]{0,1:T(8,128)(2,1)} %fusion.30), channel_id=1, source_target_pairs={{0,2},{1,3},{2,0},{3,1},{4,6},{5,7},{6,4},{7,5},{8,10},{9,11},{10,... | collective-permute-start | bytes 2457608 | tf_op jit(solution)/shard_map/ppermute | solution.py:46
  454.4 21.4 %collective-permute-start.46 = (bf16[50,1808]{1,0:T(8,128)(2,1)S(1)}, bf16[50,1808]{1,0:T(8,128)(2,1)S(1)}, u32[]{:S(2)}, u32[]{:S(2)}) collective-permute-start(bf16[50,1808]{1,0:T(8,128)(2,1)S(1)} %get-tuple-element.175), channel_id=1, source_target_pairs={{0,3},{1,2},{2,1},{3,0},{4,7},{5,6},{6,5},{7,4},{8,11},{9,10},{10,... | collective-permute-start | bytes 542408 | tf_op jit(solution)/shard_map/ppermute | solution.py:46
  455.9 19.9 %collective-permute-start.44 = (bf16[50,1808]{1,0:T(8,128)(2,1)S(1)}, bf16[50,1808]{1,0:T(8,128)(2,1)S(1)}, u32[]{:S(2)}, u32[]{:S(2)}) collective-permute-start(bf16[50,1808]{1,0:T(8,128)(2,1)S(1)} %get-tuple-element.177), channel_id=1, source_target_pairs={{0,1},{1,0},{2,3},{3,2},{4,5},{5,4},{6,7},{7,6},{8,9},{9,8},{10,11... | collective-permute-start | bytes 542408 | tf_op jit(solution)/shard_map/ppermute | solution.py:46
  (87 other events, 701.3 us)
Sparse Core Ops, SparseCore 0:
  38.4 65.6 all-gather.3
  105.6 58.4 all-gather.5
  165.7 58.4 all-gather.7
  226.4 59.8 reduce-scatter.12
  288.4 59.8 reduce-scatter.16
  375.7 69.8 reduce-scatter.14

commit v5 on v4

--- a/solution.py
+++ b/solution.py
@@ -568,7 +568,7 @@
     grad_g1, grad_c1, grad_bo, grad_g2, grad_c2, grad_bp = ring.outward(jnp.stack(inner), small=True)
     sums = jnp.concatenate([
         grad_g1, grad_c1, wide[:width], wide[2 * width :], grad_bo, grad_g2, grad_c2, grad_bp,
-        all_columns(total(du), hidden, columns_fc),
+        all_columns(total(after(du, grad_fc)), hidden, columns_fc),
     ])
     sums = links.all_sum(sums, ("seq",), free=True)
     dh1 = links.scatter_seq(split(dh1_part), free=True, hold=sums)

time: 498 us -> 480 us (0.964)
  starting transfers between devices: 58 us -> 45.1 us
    ppermute x35, starting transfers between devices: 40.3 us -> 27.6 us  [swap(): return lax.ppermute(value, axis, pairs)]
    unnamed x148 -> x150, local copies, waits for them, and re-layouts: 21.6 us -> 19.2 us
    reduce_sum x5 -> x6, other arithmetic: 16.7 us -> 15.7 us  [local(): total = lambda m: jnp.sum(m.astype(F32), axis=0)]
  transfers between devices with their start and end apart: 60 -> 60, of which waited for: 24 -> 25; matrix products, arithmetic and copies ran while one was open for 44% -> 45% of each run, Pallas kernels for 11% -> 11%
where the time goes in v5:
time: 480 us; the launch traced here: 471 us
  waiting for transfers between devices  126 us (26%)
  matrix products  109 us (23%)
  other arithmetic  65.9 us (14%)
  local copies, waits for them, and re-layouts  55.8 us (12%)
  Pallas kernels  52.2 us (11%)
  starting transfers between devices  45.1 us (9%)
  between operations  16.5 us (3%)
    dot_general x21, matrix products, dot(): return lax.dot_general(a, b, (dims, ((), ())), preferred_element_type=F32)  109 us
    ppermute x17, waiting for transfers between devices, swap(): lax.ppermute(v, axis, pairs)  59 us
    ppermute x35, waiting for transfers between devices, swap(): return lax.ppermute(value, axis, pairs)  56.6 us
    ppermute x35, starting transfers between devices, swap(): return lax.ppermute(value, axis, pairs)  27.6 us
    pallas_call x1, Pallas kernels, attention_backward(): pl.pallas_call(partial(attention_backward_kernel, size, pairs, odd), out_...  27.1 us
    pallas_call x1, Pallas kernels, attention_forward(): pl.pallas_call(partial(attention_forward_kernel, size, pairs, odd), out_s...  20.9 us
    unnamed x150, local copies, waits for them, and re-layouts  19.2 us
    reduce_sum x6, other arithmetic, local(): total = lambda m: jnp.sum(m.astype(F32), axis=0)  15.7 us
  transfers between devices with their start and end apart: 60, of which 25 were waited for; matrix products, arithmetic and copies ran while one was open for 45% of the time, Pallas kernels for 11%

profile of v5, /device:TPU:0, one launch (start us, length us, event | category | flops | bytes accessed | tf_op | source)
XLA Modules:
  0.0 470.6 jit_solution(12134788378389496749)
XLA Ops:
  47.5 7.4 %collective-permute-done.7 = bf16[256,1600]{0,1:T(8,128)(2,1)} collective-permute-done((bf16[256,1600]{0,1:T(8,128)(2,1)}, bf16[256,1600]{0,1:T(8,128)(2,1)}, u32[]{:S(2)}, u32[]{:S(2)}) %collective-permute-start.7) | collective-permute-done | bytes 819232 | tf_op jit(solution)/shard_map/ppermute | solution.py:48
  63.1 17.3 %collective-permute-done.13 = bf16[256,1600]{0,1:T(8,128)(2,1)S(1)} collective-permute-done((bf16[256,1600]{0,1:T(8,128)(2,1)S(1)}, bf16[256,1600]{0,1:T(8,128)(2,1)S(1)}, u32[]{:S(2)}, u32[]{:S(2)}) %collective-permute-start.13) | collective-permute-done | bytes 819232 | tf_op jit(solution)/shard_map/ppermute | solution.py:48
  80.4 2.7 fusion.5
  89.2 4.4 collective-permute-done.24
  93.6 4.5 collective-permute-done.25
  109.4 10.2 %add_convert_fusion.q_ref.k_ref.v_ref = bf16[1024,1408]{1,0:T(8,128)(2,1)} fusion(bf16[1024,1600]{0,1:T(8,128)(2,1)} %fusion.5, bf16[1600,1808]{1,0:T(8,128)(2,1)} %all-gather.4.cloned.1.call-done, f32[1408]{0:T(1024)S(1)} %reduce.2), kind=kOutput, calls=%fused_computation.27 | convolution fusion | flops 4616617984 | bytes 10671616 | tf_op jit(solution)/shard_map/dot_general | solution.py:445
  121.5 20.9 %attention_forward.1 = bf16[1024,512]{1,0:T(8,128)(2,1)S(1)} custom-call(s32[2]{0:T(128)S(1)} %pad_add_fusion.info, bf16[1024,1408]{1,0:T(8,128)(2,1)S(1)} %copy-done.2, bf16[1024,1408]{1,0:T(8,128)(2,1)S(1)} %copy-done.2, bf16[1024,1408]{1,0:T(8,128)(2,1)S(1)} %copy-done.2), custom_call_target="tpu_custom_call" | custom-call | flops 24956108800 | bytes 5767168 | tf_op jit(solution)/shard_map/attention_forward/pallas_call | solution.py:380
  146.2 5.5 %collective-permute-done.16 = bf16[256,512]{1,0:T(8,128)(2,1)S(1)} collective-permute-done((bf16[256,512]{1,0:T(8,128)(2,1)S(1)}, bf16[256,512]{1,0:T(8,128)(2,1)S(1)}, u32[]{:S(2)}, u32[]{:S(2)}) %collective-permute-start.16) | collective-permute-done | bytes 262176 | tf_op jit(solution)/shard_map/ppermute | solution.py:46
  151.7 4.7 %collective-permute-done.15 = bf16[256,512]{1,0:T(8,128)(2,1)S(1)} collective-permute-done((bf16[256,512]{1,0:T(8,128)(2,1)S(1)}, bf16[256,512]{1,0:T(8,128)(2,1)S(1)}, u32[]{:S(2)}, u32[]{:S(2)}) %collective-permute-start.15) | collective-permute-done | bytes 262176 | tf_op jit(solution)/shard_map/ppermute | solution.py:46
  173.6 18.4 %collective-permute-done.22 = bf16[256,1600]{0,1:T(8,128)(2,1)} collective-permute-done((bf16[256,1600]{0,1:T(8,128)(2,1)S(1)}, bf16[256,1600]{0,1:T(8,128)(2,1)}, u32[]{:S(2)}, u32[]{:S(2)}) %collective-permute-start.22) | collective-permute-done | bytes 819232 | tf_op jit(solution)/shard_map/ppermute | solution.py:48
  194.7 12.7 %multiply_convert_fusion.1 = (bf16[1024,1600]{0,1:T(8,128)(2,1)S(1)}, f32[1024,1600]{0,1:T(8,128)}) fusion(f32[1600]{0:T(1024)S(1)} %reduce.6, bf16[1600,1600]{1,0:T(8,128)(2,1)} %all-gather.6.cloned.1.call-done, bf16[256,1600]{0,1:T(8,128)(2,1)} %collective-permute-done.23, bf16[256,1600]{0,1:T(8,128)(2,1)} %collective-permute-done.22, ...), kind=kOutput, calls=%fused_computation.23 | convolution fusion | flops 5272371200 | bytes 18233600 | tf_op jit(solution)/shard_map/dot_general | solution.py:445
  209.1 7.8 %convolution_convert_fusion.2 = bf16[1600,1600]{1,0:T(8,128)(2,1)} fusion(bf16[1024,1600]{0,1:T(8,128)(2,1)S(1)} %get-tuple-element.90, bf16[1024,1600]{0,1:T(8,128)(2,1)S(1)} %copy-done.37), kind=kOutput, calls=%fused_computation.8 | convolution fusion | flops 5245440000 | bytes 11673600 | tf_op jit(solution)/shard_map/dot_general | solution.py:445
  217.2 7.0 %all-gather.8.cloned.1.call-done = bf16[1600,1600]{1,0:T(8,128)(2,1)} async-done(((bf16[200,1600]{1,0:T(8,128)(2,1)}), bf16[1600,1600]{1,0:T(8,128)(2,1)}) %all-gather.8.cloned.1.call-update) | async-done | bytes 5120016 | tf_op jit(solution)/shard_map/all_gather | solution.py:183
  224.2 13.2 %multiply_convert_fusion = bf16[1024,1600]{0,1:T(8,128)(2,1)S(1)} fusion(bf16[1600,1600]{1,0:T(8,128)(2,1)} %all-gather.8.cloned.1.call-done, bf16[1024,1600]{0,1:T(8,128)(2,1)} %copy-done.36, f32[1024,1600]{0,1:T(8,128)} %get-tuple-element.201, f32[1600]{0:T(1024)S(1)} %reduce.6), kind=kOutput, calls=%fused_computation.22 | convolution fusion | flops 5278924800 | bytes 18233600 | tf_op jit(solution)/shard_map/dot_general | solution.py:445
  237.4 11.1 %fusion.67 = (bf16[1024,1600]{0,1:T(8,128)(2,1)S(1)}, f32[1024,1600]{0,1:T(8,128)}) fusion(bf16[1600,1600]{1,0:T(8,128)(2,1)} %all-gather.6.cloned.1.call-done, bf16[1024,1600]{0,1:T(8,128)(2,1)S(1)} %multiply_convert_fusion), kind=kOutput, calls=%fused_computation.223 | convolution fusion | flops 5244518400 | bytes 18227200 | tf_op jit(solution)/shard_map/dot_general | solution.py:445
  249.9 10.1 %convolution_convert_fusion.1 = bf16[1600,1600]{1,0:T(8,128)(2,1)} fusion(bf16[1024,1600]{0,1:T(8,128)(2,1)S(1)} %multiply_convert_fusion, bf16[256,1600]{0,1:T(8,128)(2,1)} %collective-permute-done.23, bf16[256,1600]{0,1:T(8,128)(2,1)} %collective-permute-done.22, bf16[256,1600]{0,1:T(8,128)(2,1)S(1)} %copy-done.55, bf16[256,1600]{0,1:T(8,128)(2,1)S(1)} %copy-done.32), kind=kOutput, calls=%fused_computation.7 | convolution fusion | flops 5258547200 | bytes 11673600 | tf_op jit(solution)/shard_map/dot_general | solution.py:445
  263.6 11.6 %fusion.68 = (bf16[1024,1600]{0,1:T(8,128)(2,1)}, f32[1024,1600]{0,1:T(8,128)}) fusion(bf16[1024,1600]{0,1:T(8,128)(2,1)S(1)} %copy-done.59, bf16[1600,1600]{1,0:T(8,128)(2,1)} %all-gather.8.cloned.1.call-done), kind=kOutput, calls=%fused_computation.224 | convolution fusion | flops 5244518400 | bytes 18227200 | tf_op jit(solution)/shard_map/dot_general | solution.py:445
  275.1 7.1 %collective-permute-done.31 = bf16[256,1600]{0,1:T(8,128)(2,1)S(1)} collective-permute-done((bf16[256,1600]{0,1:T(8,128)(2,1)S(1)}, bf16[256,1600]{0,1:T(8,128)(2,1)S(1)}, u32[]{:S(2)}, u32[]{:S(2)}) %collective-permute-start.31) | collective-permute-done | bytes 819232 | tf_op jit(solution)/shard_map/ppermute | solution.py:48
  288.6 2.8 convert_reduce_fusion.5
  308.9 5.4 %collective-permute-done.33 = bf16[256,512]{1,0:T(8,128)(2,1)S(1)} collective-permute-done((bf16[256,512]{1,0:T(8,128)(2,1)S(1)}, bf16[256,512]{1,0:T(8,128)(2,1)S(1)}, u32[]{:S(2)}, u32[]{:S(2)}) %collective-permute-start.33) | collective-permute-done | bytes 262176 | tf_op jit(solution)/shard_map/ppermute | solution.py:46
  314.2 3.9 collective-permute-done.34
  321.6 27.1 %attention_backward.1 = bf16[1024,1408]{1,0:T(8,128)(2,1)S(1)} custom-call(s32[2]{0:T(128)S(1)} %pad_add_fusion.info, bf16[1024,1408]{1,0:T(8,128)(2,1)} %add_convert_fusion.q_ref.k_ref.v_ref, bf16[1024,1408]{1,0:T(8,128)(2,1)} %add_convert_fusion.q_ref.k_ref.v_ref, bf16[1024,1408]{1,0:T(8,128)(2,1)} %add_convert_fusion.q_ref.k_ref.v_ref, ...), custom_call_target="tpu_custom_call" | custom-call | flops 24956108800 | bytes 8650752 | tf_op jit(solution)/shard_map/attention_backward/pallas_call | solution.py:401
  348.8 10.6 %fusion.14 = f32[1024,1600]{0,1:T(8,128)} fusion(bf16[1024,1408]{1,0:T(8,128)(2,1)S(1)} %attention_backward.1, bf16[1600,1808]{1,0:T(8,128)(2,1)} %all-gather.4.cloned.1.call-done), kind=kOutput, calls=%fused_computation.28 | convolution fusion | flops 4613734400 | bytes 13942784 | tf_op jit(solution)/shard_map/dot_general | solution.py:445
  363.7 7.8 %convolution_convert_fusion = bf16[1600,1408]{1,0:T(8,128)(2,1)S(1)} fusion(bf16[1024,1600]{0,1:T(8,128)(2,1)} %fusion.5, bf16[1024,1408]{1,0:T(8,128)(2,1)} %copy-done), kind=kOutput, calls=%fused_computation.6 | convolution fusion | flops 4615987200 | bytes 10665984 | tf_op jit(solution)/shard_map/dot_general | solution.py:445
  371.4 3.0 pad_maximum_fusion
  375.2 2.9 fusion.59
  379.5 7.4 %fusion.53 = (f32[1600]{0:T(1024)S(1)}, f32[1600]{0:T(1024)S(1)}, bf16[1024,1600]{0,1:T(8,128)(2,1)}) fusion(f32[1024,1600]{0,1:T(8,128)} %fusion.14, f32[1024]{0:T(1024)S(1)} %copy-done.44, f32[1024]{0:T(1024)S(1)} %copy-done.42, bf16[1024,1600]{0,1:T(8,128)(2,1)S(1)} %copy-done.4), kind=kLoop, calls=%fused_computation.212 | loop fusion | flops 11465600 | bytes 13128192 | tf_op jit(solution)/shard_map/reduce_sum | solution.py:565
  410.0 5.8 %collective-permute-done.51 = f32[19200]{0:T(1024)S(1)} collective-permute-done((f32[19200]{0:T(1024)S(1)}, f32[19200]{0:T(1024)S(1)}, u32[]{:S(2)}, u32[]{:S(2)}) %collective-permute-start.51) | collective-permute-done | bytes 76832 | tf_op jit(solution)/shard_map/ppermute | solution.py:46
  419.2 2.8 add_convert_fusion.3
  428.6 15.9 %collective-permute-done.43 = bf16[256,1600]{0,1:T(8,128)(2,1)S(1)} collective-permute-done((bf16[256,1600]{0,1:T(8,128)(2,1)}, bf16[256,1600]{0,1:T(8,128)(2,1)S(1)}, u32[]{:S(2)}, u32[]{:S(2)}) %collective-permute-start.43) | collective-permute-done | bytes 819232 | tf_op jit(solution)/shard_map/ppermute | solution.py:46
  444.5 3.1 convert_add_fusion.2
  453.7 3.5 fusion.25
  (402 shorter events, 175.6 us)
Async XLA Ops:
  7.2 96.9 %all-gather.4.cloned.1.call-start = ((), (), s32[]{:S(2)}) async-start(), calls=%async_computation.3 | async-start | bytes 6912000 | tf_op jit(solution)/shard_map/all_gather | solution.py:183
  10.3 14.1 %collective-permute-start = (bf16[50,1808]{1,0:T(8,128)(2,1)S(1)}, bf16[50,1808]{1,0:T(8,128)(2,1)S(1)}, u32[]{:S(2)}, u32[]{:S(2)}) collective-permute-start(bf16[50,1808]{1,0:T(8,128)(2,1)S(1)} %get-tuple-element.59), channel_id=1, source_target_pairs={{0,3},{1,2},{2,1},{3,0},{4,7},{5,6},{6,5},{7,4},{8,11},{9,10},{10,... | collective-permute-start | bytes 542408 | tf_op jit(solution)/shard_map/ppermute | solution.py:46
  12.8 11.6 %collective-permute-start.1 = (bf16[50,1808]{1,0:T(8,128)(2,1)S(1)}, bf16[50,1808]{1,0:T(8,128)(2,1)}, u32[]{:S(2)}, u32[]{:S(2)}) collective-permute-start(bf16[50,1808]{1,0:T(8,128)(2,1)S(1)} %get-tuple-element.60), channel_id=1, source_target_pairs={{0,2},{1,3},{2,0},{3,1},{4,6},{5,7},{6,4},{7,5},{8,10},{9,11},{10,... | collective-permute-start | bytes 542408 | tf_op jit(solution)/shard_map/ppermute | solution.py:46
  13.4 11.0 %collective-permute-start.2 = (bf16[50,1808]{1,0:T(8,128)(2,1)S(1)}, bf16[50,1808]{1,0:T(8,128)(2,1)}, u32[]{:S(2)}, u32[]{:S(2)}) collective-permute-start(bf16[50,1808]{1,0:T(8,128)(2,1)S(1)} %get-tuple-element.61), channel_id=1, source_target_pairs={{0,1},{1,0},{2,3},{3,2},{4,5},{5,4},{6,7},{7,6},{8,9},{9,8},{10,11... | collective-permute-start | bytes 542408 | tf_op jit(solution)/shard_map/ppermute | solution.py:46
  34.0 20.8 %collective-permute-start.7 = (bf16[256,1600]{0,1:T(8,128)(2,1)}, bf16[256,1600]{0,1:T(8,128)(2,1)}, u32[]{:S(2)}, u32[]{:S(2)}) collective-permute-start(bf16[256,1600]{0,1:T(8,128)(2,1)} %slice_dynamic-update-slice_fusion.22), channel_id=1, source_target_pairs={{0,2},{1,3},{2,0},{3,1},{4,6},{5,7},{6,4},{7,5},{8,10},{9,11},{10,... | collective-permute-start | bytes 2457608 | tf_op jit(solution)/shard_map/ppermute | solution.py:48
  35.5 19.3 %collective-permute-start.6 = (bf16[256,1600]{0,1:T(8,128)(2,1)}, bf16[256,1600]{0,1:T(8,128)(2,1)}, u32[]{:S(2)}, u32[]{:S(2)}) collective-permute-start(bf16[256,1600]{0,1:T(8,128)(2,1)} %slice_dynamic-update-slice_fusion.22), channel_id=1, source_target_pairs={{0,1},{1,0},{2,3},{3,2},{4,5},{5,4},{6,7},{7,6},{8,9},{9,8},{10,11... | collective-permute-start | bytes 2457608 | tf_op jit(solution)/shard_map/ppermute | solution.py:48
  38.2 154.8 %all-gather.6.cloned.1.call-start = ((), (), s32[]{:S(2)}) async-start(), calls=%async_computation.4 | async-start | bytes 5990400 | tf_op jit(solution)/shard_map/all_gather | solution.py:183
  60.2 20.2 %collective-permute-start.13 = (bf16[256,1600]{0,1:T(8,128)(2,1)S(1)}, bf16[256,1600]{0,1:T(8,128)(2,1)S(1)}, u32[]{:S(2)}, u32[]{:S(2)}) collective-permute-start(bf16[256,1600]{0,1:T(8,128)(2,1)S(1)} %copy-done.12), channel_id=1, source_target_pairs={{0,2},{1,3},{2,0},{3,1},{4,6},{5,7},{6,4},{7,5},{8,10},{9,11},{10,... | collective-permute-start | bytes 2457608 | tf_op jit(solution)/shard_map/ppermute | solution.py:48
  99.2 125.0 %all-gather.8.cloned.1.call-start = ((), (), s32[]{:S(2)}) async-start(), calls=%async_computation.5 | async-start | bytes 5990400 | tf_op jit(solution)/shard_map/all_gather | solution.py:183
  108.0 48.6 %collective-permute-start.18 = (bf16[1600,400]{0,1:T(8,128)(2,1)}, bf16[1600,400]{0,1:T(8,128)(2,1)S(1)}, u32[]{:S(2)}, u32[]{:S(2)}) collective-permute-start(bf16[1600,400]{0,1:T(8,128)(2,1)} %copy.25), channel_id=1, source_target_pairs={{0,2},{1,3},{2,0},{3,1},{4,6},{5,7},{6,4},{7,5},{8,10},{9,11},{10,... | collective-permute-start | bytes 3840008 | tf_op jit(solution)/shard_map/ppermute | solution.py:46
  119.6 166.6 %reduce-scatter.13.cloned.1.call-start = ((), (), s32[]{:S(2)}) async-start(), calls=%async_computation.6 | async-start | bytes 5990400
  143.0 13.5 %collective-permute-start.15 = (bf16[256,512]{1,0:T(8,128)(2,1)S(1)}, bf16[256,512]{1,0:T(8,128)(2,1)S(1)}, u32[]{:S(2)}, u32[]{:S(2)}) collective-permute-start(bf16[256,512]{1,0:T(8,128)(2,1)S(1)} %get-tuple-element.161), channel_id=1, source_target_pairs={{0,3},{1,2},{2,1},{3,0},{4,7},{5,6},{6,5},{7,4},{8,11},{9,10},{10,... | collective-permute-start | bytes 786440 | tf_op jit(solution)/shard_map/ppermute | solution.py:46
  145.8 18.9 %collective-permute-start.20 = (bf16[1600,400]{0,1:T(8,128)(2,1)}, bf16[1600,400]{0,1:T(8,128)(2,1)}, u32[]{:S(2)}, u32[]{:S(2)}) collective-permute-start(bf16[1600,400]{0,1:T(8,128)(2,1)} %copy.25), channel_id=1, source_target_pairs={{0,1},{1,0},{2,3},{3,2},{4,5},{5,4},{6,7},{7,6},{8,9},{9,8},{10,11... | collective-permute-start | bytes 3840008 | tf_op jit(solution)/shard_map/ppermute | solution.py:46
  156.6 10.6 %collective-permute-start.19 = (bf16[1600,400]{0,1:T(8,128)(2,1)S(1)}, bf16[1600,400]{0,1:T(8,128)(2,1)S(1)}, u32[]{:S(2)}, u32[]{:S(2)}) collective-permute-start(bf16[1600,400]{0,1:T(8,128)(2,1)S(1)} %collective-permute-done.18), channel_id=1, source_target_pairs={{0,1},{1,0},{2,3},{3,2},{4,5},{5,4},{6,7},{7,6},{8,9},{9,8},{10,11... | collective-permute-start | bytes 3840008 | tf_op jit(solution)/shard_map/ppermute | solution.py:46
  171.5 20.5 %collective-permute-start.22 = (bf16[256,1600]{0,1:T(8,128)(2,1)S(1)}, bf16[256,1600]{0,1:T(8,128)(2,1)}, u32[]{:S(2)}, u32[]{:S(2)}) collective-permute-start(bf16[256,1600]{0,1:T(8,128)(2,1)S(1)} %add_convert_fusion.4), channel_id=1, source_target_pairs={{0,2},{1,3},{2,0},{3,1},{4,6},{5,7},{6,4},{7,5},{8,10},{9,11},{10,... | collective-permute-start | bytes 2457608 | tf_op jit(solution)/shard_map/ppermute | solution.py:48
  216.9 170.4 %reduce-scatter.15.cloned.1.call-start = ((), (), s32[]{:S(2)}) async-start(), calls=%async_computation.7 | async-start | bytes 5990400
  248.6 11.4 %collective-permute-start.29 = (bf16[256,1600]{0,1:T(8,128)(2,1)S(1)}, bf16[256,1600]{0,1:T(8,128)(2,1)}, u32[]{:S(2)}, u32[]{:S(2)}) collective-permute-start(bf16[256,1600]{0,1:T(8,128)(2,1)S(1)} %get-tuple-element.91), channel_id=1, source_target_pairs={{0,1},{1,0},{2,3},{3,2},{4,5},{5,4},{6,7},{7,6},{8,9},{9,8},{10,11... | collective-permute-start | bytes 2457608 | tf_op jit(solution)/shard_map/ppermute | solution.py:48
  262.0 20.2 %collective-permute-start.31 = (bf16[256,1600]{0,1:T(8,128)(2,1)S(1)}, bf16[256,1600]{0,1:T(8,128)(2,1)S(1)}, u32[]{:S(2)}, u32[]{:S(2)}) collective-permute-start(bf16[256,1600]{0,1:T(8,128)(2,1)S(1)} %fusion.28), channel_id=1, source_target_pairs={{0,2},{1,3},{2,0},{3,1},{4,6},{5,7},{6,4},{7,5},{8,10},{9,11},{10,... | collective-permute-start | bytes 2457608 | tf_op jit(solution)/shard_map/ppermute | solution.py:48
  263.5 18.7 %collective-permute-start.30 = (bf16[256,1600]{0,1:T(8,128)(2,1)S(1)}, bf16[256,1600]{0,1:T(8,128)(2,1)S(1)}, u32[]{:S(2)}, u32[]{:S(2)}) collective-permute-start(bf16[256,1600]{0,1:T(8,128)(2,1)S(1)} %get-tuple-element.92), channel_id=1, source_target_pairs={{0,1},{1,0},{2,3},{3,2},{4,5},{5,4},{6,7},{7,6},{8,9},{9,8},{10,11... | collective-permute-start | bytes 2457608 | tf_op jit(solution)/shard_map/ppermute | solution.py:48
  287.5 160.2 %reduce-scatter.17.cloned.1.call-start = ((), (), s32[]{:S(2)}) async-start(), calls=%async_computation.8 | async-start | bytes 6912000
  299.0 19.2 %collective-permute-start.36 = (bf16[1600,400]{0,1:T(8,128)(2,1)}, bf16[1600,400]{0,1:T(8,128)(2,1)}, u32[]{:S(2)}, u32[]{:S(2)}) collective-permute-start(bf16[1600,400]{0,1:T(8,128)(2,1)} %convolution_convert_fusion.3), channel_id=1, source_target_pairs={{0,1},{1,0},{2,3},{3,2},{4,5},{5,4},{6,7},{7,6},{8,9},{9,8},{10,11... | collective-permute-start | bytes 3840008 | tf_op jit(solution)/shard_map/ppermute | solution.py:46
  307.0 11.2 %collective-permute-start.34 = (bf16[256,512]{1,0:T(8,128)(2,1)S(1)}, bf16[256,512]{1,0:T(8,128)(2,1)S(1)}, u32[]{:S(2)}, u32[]{:S(2)}) collective-permute-start(bf16[256,512]{1,0:T(8,128)(2,1)S(1)} %select_select_fusion.4), channel_id=1, source_target_pairs={{0,3},{1,2},{2,1},{3,0},{4,7},{5,6},{6,5},{7,4},{8,11},{9,10},{10,... | collective-permute-start | bytes 786440 | tf_op jit(solution)/shard_map/ppermute | solution.py:46
  307.6 51.8 %collective-permute-start.35 = (bf16[1600,400]{0,1:T(8,128)(2,1)S(1)}, bf16[1600,400]{0,1:T(8,128)(2,1)S(1)}, u32[]{:S(2)}, u32[]{:S(2)}) collective-permute-start(bf16[1600,400]{0,1:T(8,128)(2,1)S(1)} %convolution_convert_fusion.5), channel_id=1, source_target_pairs={{0,1},{1,0},{2,3},{3,2},{4,5},{5,4},{6,7},{7,6},{8,9},{9,8},{10,11... | collective-permute-start | bytes 3840008 | tf_op jit(solution)/shard_map/ppermute | solution.py:46
  320.1 39.3 %collective-permute-start.37 = (bf16[1600,400]{0,1:T(8,128)(2,1)S(1)}, bf16[1600,400]{0,1:T(8,128)(2,1)S(1)}, u32[]{:S(2)}, u32[]{:S(2)}) collective-permute-start(bf16[1600,400]{0,1:T(8,128)(2,1)S(1)} %add_convert_fusion.2), channel_id=1, source_target_pairs={{0,2},{1,3},{2,0},{3,1},{4,6},{5,7},{6,4},{7,5},{8,10},{9,11},{10,... | collective-permute-start | bytes 3840008 | tf_op jit(solution)/shard_map/ppermute | solution.py:46
  378.1 20.6 %collective-permute-start.28 = (bf16[256,1600]{0,1:T(8,128)(2,1)}, bf16[256,1600]{0,1:T(8,128)(2,1)S(1)}, u32[]{:S(2)}, u32[]{:S(2)}) collective-permute-start(bf16[256,1600]{0,1:T(8,128)(2,1)} %get-tuple-element.144), channel_id=1, source_target_pairs={{0,1},{1,0},{2,3},{3,2},{4,5},{5,4},{6,7},{7,6},{8,9},{9,8},{10,11... | collective-permute-start | bytes 2457608 | tf_op jit(solution)/shard_map/ppermute | solution.py:46
  393.6 23.5 %collective-permute-start.40 = (bf16[256,1600]{0,1:T(8,128)(2,1)}, bf16[256,1600]{0,1:T(8,128)(2,1)}, u32[]{:S(2)}, u32[]{:S(2)}) collective-permute-start(bf16[256,1600]{0,1:T(8,128)(2,1)} %get-tuple-element.142), channel_id=1, source_target_pairs={{0,1},{1,0},{2,3},{3,2},{4,5},{5,4},{6,7},{7,6},{8,9},{9,8},{10,11... | collective-permute-start | bytes 2457608 | tf_op jit(solution)/shard_map/ppermute | solution.py:46
  396.6 10.4 %collective-permute-start.48 = (bf16[50,1600]{1,0:T(8,128)(2,1)}, bf16[50,1600]{1,0:T(8,128)(2,1)S(1)}, u32[]{:S(2)}, u32[]{:S(2)}) collective-permute-start(bf16[50,1600]{1,0:T(8,128)(2,1)} %get-tuple-element.188), channel_id=1, source_target_pairs={{0,2},{1,3},{2,0},{3,1},{4,6},{5,7},{6,4},{7,5},{8,10},{9,11},{10,... | collective-permute-start | bytes 480008 | tf_op jit(solution)/shard_map/ppermute | solution.py:46
  405.7 48.0 %collective-permute-start.27 = (bf16[256,1600]{0,1:T(8,128)(2,1)}, bf16[256,1600]{0,1:T(8,128)(2,1)}, u32[]{:S(2)}, u32[]{:S(2)}) collective-permute-start(bf16[256,1600]{0,1:T(8,128)(2,1)} %get-tuple-element.143), channel_id=1, source_target_pairs={{0,1},{1,0},{2,3},{3,2},{4,5},{5,4},{6,7},{7,6},{8,9},{9,8},{10,11... | collective-permute-start | bytes 2457608 | tf_op jit(solution)/shard_map/ppermute | solution.py:46
  405.7 48.0 %collective-permute-start.38 = (bf16[256,1600]{0,1:T(8,128)(2,1)}, bf16[256,1600]{0,1:T(8,128)(2,1)}, u32[]{:S(2)}, u32[]{:S(2)}) collective-permute-start(bf16[256,1600]{0,1:T(8,128)(2,1)} %fusion.30), channel_id=1, source_target_pairs={{0,2},{1,3},{2,0},{3,1},{4,6},{5,7},{6,4},{7,5},{8,10},{9,11},{10,... | collective-permute-start | bytes 2457608 | tf_op jit(solution)/shard_map/ppermute | solution.py:46
  407.0 21.6 %collective-permute-start.39 = (bf16[256,1600]{0,1:T(8,128)(2,1)}, bf16[256,1600]{0,1:T(8,128)(2,1)}, u32[]{:S(2)}, u32[]{:S(2)}) collective-permute-start(bf16[256,1600]{0,1:T(8,128)(2,1)} %get-tuple-element.141), channel_id=1, source_target_pairs={{0,1},{1,0},{2,3},{3,2},{4,5},{5,4},{6,7},{7,6},{8,9},{9,8},{10,11... | collective-permute-start | bytes 2457608 | tf_op jit(solution)/shard_map/ppermute | solution.py:46
  423.9 20.6 %collective-permute-start.43 = (bf16[256,1600]{0,1:T(8,128)(2,1)}, bf16[256,1600]{0,1:T(8,128)(2,1)S(1)}, u32[]{:S(2)}, u32[]{:S(2)}) collective-permute-start(bf16[256,1600]{0,1:T(8,128)(2,1)} %add_convert_fusion.3), channel_id=1, source_target_pairs={{0,2},{1,3},{2,0},{3,1},{4,6},{5,7},{6,4},{7,5},{8,10},{9,11},{10,... | collective-permute-start | bytes 2457608 | tf_op jit(solution)/shard_map/ppermute | solution.py:46
  450.1 10.8 %collective-permute-start.45 = (bf16[50,1808]{1,0:T(8,128)(2,1)S(1)}, bf16[50,1808]{1,0:T(8,128)(2,1)S(1)}, u32[]{:S(2)}, u32[]{:S(2)}) collective-permute-start(bf16[50,1808]{1,0:T(8,128)(2,1)S(1)} %get-tuple-element.180), channel_id=1, source_target_pairs={{0,2},{1,3},{2,0},{3,1},{4,6},{5,7},{6,4},{7,5},{8,10},{9,11},{10,... | collective-permute-start | bytes 542408 | tf_op jit(solution)/shard_map/ppermute | solution.py:46
  (88 other events, 707.8 us)
Sparse Core Ops, SparseCore 0:
  38.4 65.6 all-gather.3
  105.6 58.4 all-gather.5
  165.7 58.4 all-gather.7
  226.4 59.8 reduce-scatter.12
  288.4 59.8 reduce-scatter.14
  374.6 69.8 reduce-scatter.16
